TPU v7x, 256 devices: a whole 4x4x8 slice. The times are simulated.
256 devices in a mesh: dp: 16 (over y, x), expert: 16 (over z, core).
Axes of the slice: x: 4, y: 4, z: 8, core: 2. Of those that a mesh axis runs over, the one named last changes fastest.
Arguments:
- tokens: bfloat16 [16384, 2048], P(('dp', 'expert')), may hold values from -6 to 6
- expert_ids: int32 [16384, 8], P(('dp', 'expert')), may hold values from 0 to 31, all different within a row; in each aligned block of 64 rows (0 to 63, 64 to 127, ...) at most 24 rows name the same one
- gate_fixed: int32 [16384, 8], P(('dp', 'expert')), may hold values from 1 to 65535
- scorer_id: int32 [1024], P(('dp', 'expert')), may hold values from 0 to 1
- direction_tags: bfloat16 [2, 2048], replicated, may hold values from -6 to 6
- w_gate: bfloat16 [32, 2048, 512], P('expert'), may hold values from -0.125 to 0.125
- w_up: bfloat16 [32, 2048, 512], P('expert'), may hold values from -0.125 to 0.125
- w_down: bfloat16 [32, 512, 2048], P('expert'), may hold values from -0.25 to 0.25
- score_head: float32 [2048], replicated, may hold values from -0.125 to 0.125
Outputs:
- mixed: bfloat16 [16384, 2048], P(('dp', 'expert'))
- pair_score: float32 [1024], P(('dp', 'expert'))
Inputs may be any that keep to these rules, and one draw needn't show every extreme that they name: `expert_ids`: each row names 8 different experts. Among the rows of one device no expert is named by more than 24 rows, and in some devices' rows an expert is named by exactly 24.
All inputs are finite; a program needn't handle non-finite values.
Results may differ from a plain program's by a relative error of at most 0.04.
Values may be sent and summed in bfloat16 or wider, within the bound.
A program may use at most 64 MiB of HBM per device.

v0:
```python
import jax
import jax.numpy as jnp
from jax import lax
from jax.sharding import PartitionSpec as P

SEQ_LEN = 16
MOST = 24


def from_partner(block, axis, bit):
    count = lax.axis_size(axis)
    route = []
    for low in range(count):
        high = low | 1 << bit
        if high != low and high < count:
            route += [(low, high), (high, low)]
    return lax.ppermute(block, axis, route)


def route_ranks(expert_ids, expert_total):
    flat_ids = expert_ids.reshape(-1)
    entry_count = flat_ids.shape[0]
    onehot = flat_ids[:, None] == jnp.arange(expert_total, dtype=jnp.int32)[None, :]
    positions = jnp.arange(entry_count, dtype=jnp.int32)
    earlier = (positions[:, None] > positions[None, :]).astype(jnp.bfloat16)
    counts = jnp.dot(earlier, onehot.astype(jnp.bfloat16), preferred_element_type=jnp.float32)
    rank_in = jnp.sum(jnp.where(onehot, counts, 0.0), axis=1).astype(jnp.int32)
    return rank_in.reshape(expert_ids.shape)


def body(
    tokens, expert_ids, gate_fixed, scorer_id, direction_tags, w_gate, w_up, w_down, score_head
):
    expert_count = lax.axis_size("expert")
    per_device = w_gate.shape[0]
    tok_rows, model_width = tokens.shape
    top_count = expert_ids.shape[1]
    which_tag = jnp.repeat(scorer_id, SEQ_LEN)[:, None]
    tag_rows = jnp.where(
        which_tag == 1, direction_tags[1][None, :], direction_tags[0][None, :]
    ).astype(jnp.float32)
    inputs = (tokens.astype(jnp.float32) + tag_rows).astype(jnp.bfloat16)
    fixed_val = gate_fixed.astype(jnp.float32)
    weight = fixed_val / jnp.sum(fixed_val, axis=1, keepdims=True)
    rank_in = route_ranks(expert_ids, per_device * expert_count)
    inputs_all, ids_all, weight_all, rank_all = (
        lax.all_gather(inputs, "expert", axis=0, tiled=True),
        lax.all_gather(expert_ids, "expert", axis=0, tiled=True),
        lax.all_gather(weight.astype(jnp.bfloat16), "expert", axis=0, tiled=True).astype(
            weight.dtype
        ),
        lax.all_gather(rank_in, "expert", axis=0, tiled=True),
    )
    my_index = lax.axis_index("expert")
    local_count = per_device * MOST
    ids_cube = ids_all.reshape(expert_count, tok_rows, top_count)
    rank_cube = rank_all.reshape(expert_count, tok_rows, top_count)
    weight_cube = weight_all.reshape(expert_count, tok_rows, top_count)
    local_slot = ids_cube - my_index * per_device
    is_mine = (local_slot >= 0) & (local_slot < per_device)
    local_key = jnp.where(is_mine, local_slot * MOST + rank_cube, -1)
    match = (
        local_key[:, None, :, :] == jnp.arange(local_count, dtype=jnp.int32)[None, :, None, None]
    )
    picker = jnp.any(match, axis=3).astype(jnp.bfloat16)
    slot_weight = jnp.sum(jnp.where(match, weight_cube[:, None, :, :], 0.0), axis=(2, 3)).reshape(
        expert_count, per_device, MOST
    )
    inputs_cube = inputs_all.reshape(expert_count, tok_rows, model_width)
    row_block = jnp.einsum(
        "sqt,std->sqd", picker, inputs_cube, preferred_element_type=jnp.float32
    ).astype(jnp.bfloat16)
    row_block = row_block.reshape(expert_count, per_device, MOST, model_width)
    gate_proj = jnp.einsum("nemd,edf->nemf", row_block, w_gate, preferred_element_type=jnp.float32)
    up_proj = jnp.einsum("nemd,edf->nemf", row_block, w_up, preferred_element_type=jnp.float32)
    hidden = (jax.nn.silu(gate_proj) * up_proj).astype(jnp.bfloat16)
    down_out = jnp.einsum("nemf,efd->nemd", hidden, w_down, preferred_element_type=jnp.float32)
    result = (slot_weight[..., None] * down_out).astype(jnp.bfloat16)
    partial_value = jnp.einsum(
        "sqt,sqd->std",
        picker,
        result.reshape(expert_count, local_count, model_width),
        preferred_element_type=jnp.float32,
    )
    partial_value = partial_value.reshape(expert_count * tok_rows, model_width)
    received = lax.all_to_all(
        partial_value.astype(jnp.bfloat16), "expert", split_axis=0, concat_axis=0, tiled=True
    ).astype(partial_value.dtype)
    summed = received.reshape(expert_count, tok_rows, model_width).sum(axis=0)
    mixed = summed.astype(jnp.bfloat16)
    token_score = jnp.dot(mixed.astype(jnp.float32), score_head, precision=lax.Precision.HIGHEST)
    seq_score = token_score.reshape(-1, SEQ_LEN).sum(axis=1)
    partner = from_partner(seq_score, "dp", lax.axis_size("dp").bit_length() - 2)
    pair_score = jnp.abs(seq_score - partner) + 0.5 * (seq_score + partner)
    return (mixed, pair_score)


def solution(mesh):
    return jax.shard_map(
        body,
        mesh=mesh,
        in_specs=(
            P(("dp", "expert"), None),
            P(("dp", "expert"), None),
            P(("dp", "expert"), None),
            P(("dp", "expert")),
            P(),
            P("expert", None, None),
            P("expert", None, None),
            P("expert", None, None),
            P(),
        ),
        out_specs=(P(("dp", "expert"), None), P(("dp", "expert"))),
        check_vma=False,
    )
```

profile of v0, /device:TPU:2, one launch (start us, length us, event | category | flops | bytes accessed | tf_op | source)
XLA Modules:
  0.0 201.4 jit_solution(7624634206513829561)
XLA Ops:
  7.2 0.7 broadcast_compare_fusion
  8.1 0.8 slice_reduce_fusion.1
  8.9 1.8 add_convert_fusion
  10.7 0.7 convert_reduce_fusion
  11.4 0.7 fusion.27
  12.1 20.0 %all-gather.2 = bf16[16,64,8]{1,2,0:T(8,128)(2,1)S(1)} all-gather(bf16[1,64,8]{1,2,0:T(8,128)(2,1)S(1)} %fusion.27), channel_id=1, replica_groups=mesh['dp'=16,'expert'=16] {'expert'}, dimensions={0}, use_global_device_ids=true | all-gather | bytes 17408 | tf_op jit(solution)/shard_map/all_gather | solution.py:49
  32.1 0.8 copy.28
  33.0 0.3 fusion.20
  33.4 14.7 %all-gather.1 = s32[16,64,8]{1,2,0:T(8,128)S(1)} all-gather(s32[1,64,8]{1,2,0:T(8,128)S(1)} %copy.29), channel_id=1, replica_groups=mesh['dp'=16,'expert'=16] {'expert'}, dimensions={0}, use_global_device_ids=true | all-gather | bytes 34816 | tf_op jit(solution)/shard_map/all_gather | solution.py:52
  48.1 16.2 %all-gather = s32[16,64,8]{1,2,0:T(8,128)S(1)} all-gather(s32[1,64,8]{1,2,0:T(8,128)} %bitcast.68), channel_id=1, replica_groups=mesh['dp'=16,'expert'=16] {'expert'}, dimensions={0}, use_global_device_ids=true | all-gather | bytes 34816 | tf_op jit(solution)/shard_map/all_gather | solution.py:48
  64.3 1.7 select_reduce_fusion
  66.0 1.2 fusion.9
  67.3 3.3 %convolution_convert_fusion.1 = bf16[16,48,2048]{2,1,0:T(8,128)(2,1)S(1)} fusion(pred[16,48,64]{2,1,0:T(8,128)(4,1)S(1)} %fusion.9, bf16[16,64,2048]{2,1,0:T(8,128)(2,1)} %bitcast.64), kind=kOutput, calls=%fused_computation.9 | convolution fusion | flops 202899456 | bytes 7389184 | tf_op jit(solution)/shard_map/sqt,std->sqd/dot_general | solution.py:70
  70.6 0.1 copy-done.2
  70.7 3.0 %fusion.5 = f32[2,16,24,512]{3,2,1,0:T(8,128)} fusion(bf16[2,2048,512]{2,1,0:T(8,128)(2,1)S(1)} %copy-done.2, bf16[16,2,24,2048]{3,2,1,0:T(8,128)(2,1)S(1)} %bitcast.65), kind=kOutput, calls=%fused_computation.6 | convolution fusion | flops 1610612736 | bytes 8912896 | tf_op jit(solution)/shard_map/nemd,edf->nemf/dot_general | solution.py:74
  73.7 9.2 %fusion = bf16[16,2,24,2048]{3,2,0,1:T(8,128)(2,1)} fusion(bf16[2,512,2048]{2,1,0:T(8,128)(2,1)} %param.16, f32[16,2,24]{2,0,1:T(8,128)S(1)} %copy.30, f32[2,16,24,512]{3,2,1,0:T(8,128)} %fusion.5, bf16[2,2048,512]{2,1,0:T(8,128)(2,1)} %param.15, bf16[16,2,24,2048]{3,2,1,0:T(8,128)(2,1)S(1)} %bitcast.66), kind=kOutput, calls=%fused_computation.1 | convolution fusion | flops 3226730496 | bytes 16256000 | tf_op jit(solution)/shard_map/nemf,efd->nemd/dot_general | solution.py:77
  82.8 2.3 %copy.33 = bf16[16,2,24,2048]{3,2,1,0:T(8,128)(2,1)S(1)} copy(bf16[16,2,24,2048]{3,2,0,1:T(8,128)(2,1)} %fusion) | data formatting | bytes 6291456 | tf_op jit(solution)/shard_map/convert_element_type | solution.py:78
  85.1 1.3 convolution_convert_fusion
  86.4 98.3 %all_to_all.6 = bf16[16,64,2048]{2,1,0:T(8,128)(2,1)} all-to-all(bf16[16,64,2048]{2,1,0:T(8,128)(2,1)S(1)} %convolution_convert_fusion), channel_id=1, replica_groups=mesh['dp'=16,'expert'=16] {'expert'}, dimensions={0} | all-to-all | bytes 8388608 | tf_op jit(solution)/shard_map/all_to_all | solution.py:86
  184.8 3.0 %reduce_sum.51 = bf16[64,2048]{1,0:T(8,128)(2,1)S(1)} reduce(bf16[16,64,2048]{2,1,0:T(8,128)(2,1)} %all_to_all.6, bf16[]{:T(256)} %constant.24.clone.1), dimensions={0}, to_apply=%region_4.5 | reduce | flops 1966080 | bytes 4456450 | tf_op jit(solution)/shard_map/reduce_sum | solution.py:89
  187.8 1.0 fusion.29
  188.9 3.3 %collective-permute-start = (f32[4]{0:T(128)S(1)}, f32[4]{0:T(128)S(1)}, u32[]{:S(2)}, u32[]{:S(2)}) collective-permute-start(f32[4]{0:T(128)S(1)} %reduce_sum.52), channel_id=1, source_target_pairs={{0,128},{128,0},{16,144},{144,16},{32,160},{160,32},{48,176},{176,... | collective-permute-start | bytes 56 | tf_op jit(solution)/shard_map/ppermute | solution.py:17
  192.2 1.8 collective-permute-done
  194.1 0.5 multiply_add_fusion
  (19 shorter events, 0.7 us)
Async XLA Ops:
  7.2 180.6 %copy-start = (f32[2048]{0:T(1024)S(1)}, f32[2048]{0:T(1024)}, u32[]{:S(2)}) copy-start(f32[2048]{0:T(1024)} %param.17) | copy-start | bytes 24580
  7.2 60.1 %all-gather.5.cloned.1.call-start = ((), (), s32[]{:S(2)}) async-start(), calls=%async_computation.1 | async-start | bytes 4456448 | tf_op jit(solution)/shard_map/all_gather | solution.py:47
  67.3 3.5 %copy-start.2 = (bf16[2,2048,512]{2,1,0:T(8,128)(2,1)S(1)}, bf16[2,2048,512]{2,1,0:T(8,128)(2,1)}, u32[]{:S(2)}) copy-start(bf16[2,2048,512]{2,1,0:T(8,128)(2,1)} %param.14) | copy-start | bytes 12582916
  187.8 6.8 %copy-start.1 = (bf16[64,2048]{1,0:T(8,128)(2,1)}, bf16[64,2048]{1,0:T(8,128)(2,1)S(1)}, u32[]{:S(2)}) copy-start(bf16[64,2048]{1,0:T(8,128)(2,1)S(1)} %reduce_sum.51) | copy-start | bytes 786436
  188.9 5.1 %collective-permute-start = (f32[4]{0:T(128)S(1)}, f32[4]{0:T(128)S(1)}, u32[]{:S(2)}, u32[]{:S(2)}) collective-permute-start(f32[4]{0:T(128)S(1)} %reduce_sum.52), channel_id=1, source_target_pairs={{0,128},{128,0},{16,144},{144,16},{32,160},{160,32},{48,176},{176,... | collective-permute-start | bytes 56 | tf_op jit(solution)/shard_map/ppermute | solution.py:17
Sparse Core Ops, SparseCore 0:
  10.8 45.1 all-gather.4
where the time goes:
time: 203 us; the launch traced here: 201 us
  blocking collectives  149 us (73%)
  matrix products  18 us (9%)
  between operations  14.1 us (7%)
  other arithmetic  10.3 us (5%)
  local copies, waits for them, and re-layouts  4.53 us (2%)
  starting transfers between devices  3.34 us (2%)
    all_to_all x1, blocking collectives, body(): lax.all_to_all(partial_value.astype(jnp.bfloat16), 'expert', split_axis=0...  98.3 us
    all_gather x1, blocking collectives, body(): lax.all_gather(weight.astype(jnp.bfloat16), 'expert', axis=0, tiled=True)  20 us
    all_gather x1, blocking collectives, body(): lax.all_gather(expert_ids, 'expert', axis=0, tiled=True)  16.2 us
    all_gather x1, blocking collectives, body(): lax.all_gather(rank_in, 'expert', axis=0, tiled=True)  14.7 us
    dot_general x1, matrix products, body(): jnp.einsum('nemf,efd->nemd', hidden, w_down, preferred_element_type=jnp.f...  9.16 us
  transfers between devices with their start and end apart: 2, of which 1 were waited for; matrix products, arithmetic and copies ran while one was open for 3% of the time, Pallas kernels for 0%

commit v1 on v0

v1 whole, which is shorter than its diff:
```python
import jax
import jax.numpy as jnp
from jax import lax
from jax.sharding import Mesh
from jax.sharding import PartitionSpec as P

SEQ_LEN = 16
MOST = 24


def from_partner(block, axis, bit):
    count = lax.axis_size(axis)
    route = []
    for low in range(count):
        high = low | 1 << bit
        if high != low and high < count:
            route += [(low, high), (high, low)]
    return lax.ppermute(block, axis, route)


def route_ranks(expert_ids, expert_total):
    flat_ids = expert_ids.reshape(-1)
    entry_count = flat_ids.shape[0]
    onehot = flat_ids[:, None] == jnp.arange(expert_total, dtype=jnp.int32)[None, :]
    positions = jnp.arange(entry_count, dtype=jnp.int32)
    earlier = (positions[:, None] > positions[None, :]).astype(jnp.bfloat16)
    counts = jnp.dot(earlier, onehot.astype(jnp.bfloat16), preferred_element_type=jnp.float32)
    rank_in = jnp.sum(jnp.where(onehot, counts, 0.0), axis=1).astype(jnp.int32)
    return rank_in.reshape(expert_ids.shape)


def gather_expert(block):
    along_z = lax.all_gather(block, "z", axis=0, tiled=False)
    return lax.all_gather(along_z, "c", axis=0, tiled=False)


def body(
    tokens, expert_ids, gate_fixed, scorer_id, direction_tags, w_gate, w_up, w_down, score_head
):
    z_count = lax.axis_size("z")
    c_count = lax.axis_size("c")
    expert_count = z_count * c_count
    per_device = w_gate.shape[0]
    tok_rows, model_width = tokens.shape
    top_count = expert_ids.shape[1]
    which_tag = jnp.repeat(scorer_id, SEQ_LEN)[:, None]
    tag_rows = jnp.where(
        which_tag == 1, direction_tags[1][None, :], direction_tags[0][None, :]
    ).astype(jnp.float32)
    inputs = (tokens.astype(jnp.float32) + tag_rows).astype(jnp.bfloat16)
    rank_in = route_ranks(expert_ids, per_device * expert_count)
    packed = jnp.concatenate([expert_ids, gate_fixed, rank_in], axis=1)
    inputs_all = gather_expert(inputs).reshape(expert_count, tok_rows, model_width)
    packed_all = gather_expert(packed).reshape(expert_count, tok_rows, 3 * top_count)
    ids_cube = packed_all[..., :top_count]
    fixed_val = packed_all[..., top_count : 2 * top_count].astype(jnp.float32)
    rank_cube = packed_all[..., 2 * top_count :]
    weight_cube = fixed_val / jnp.sum(fixed_val, axis=2, keepdims=True)
    my_index = lax.axis_index("z") * c_count + lax.axis_index("c")
    local_count = per_device * MOST
    local_slot = ids_cube - my_index * per_device
    is_mine = (local_slot >= 0) & (local_slot < per_device)
    local_key = jnp.where(is_mine, local_slot * MOST + rank_cube, -1)
    match = (
        local_key[:, None, :, :] == jnp.arange(local_count, dtype=jnp.int32)[None, :, None, None]
    )
    picker = jnp.any(match, axis=3).astype(jnp.bfloat16)
    slot_weight = jnp.sum(jnp.where(match, weight_cube[:, None, :, :], 0.0), axis=(2, 3)).reshape(
        expert_count, per_device, MOST
    )
    row_block = jnp.einsum(
        "sqt,std->sqd", picker, inputs_all, preferred_element_type=jnp.float32
    ).astype(jnp.bfloat16)
    row_block = row_block.reshape(expert_count, per_device, MOST, model_width)
    gate_proj = jnp.einsum("nemd,edf->nemf", row_block, w_gate, preferred_element_type=jnp.float32)
    up_proj = jnp.einsum("nemd,edf->nemf", row_block, w_up, preferred_element_type=jnp.float32)
    hidden = (jax.nn.silu(gate_proj) * up_proj).astype(jnp.bfloat16)
    down_out = jnp.einsum("nemf,efd->nemd", hidden, w_down, preferred_element_type=jnp.float32)
    result = (slot_weight[..., None] * down_out).astype(jnp.bfloat16)
    partial_value = jnp.einsum(
        "sqt,sqd->std",
        picker,
        result.reshape(expert_count, local_count, model_width),
        preferred_element_type=jnp.float32,
    )
    partial_value = partial_value.reshape(c_count, z_count * tok_rows, model_width)
    half = lax.psum_scatter(partial_value, "c", scatter_dimension=0, tiled=False)
    half = half.reshape(z_count, tok_rows, model_width).astype(jnp.bfloat16)
    summed = lax.psum_scatter(half, "z", scatter_dimension=0, tiled=False)
    mixed = summed.astype(jnp.bfloat16)
    token_score = jnp.dot(mixed.astype(jnp.float32), score_head, precision=lax.Precision.HIGHEST)
    seq_score = token_score.reshape(-1, SEQ_LEN).sum(axis=1)
    partner = from_partner(seq_score, "dp", lax.axis_size("dp").bit_length() - 2)
    pair_score = jnp.abs(seq_score - partner) + 0.5 * (seq_score + partner)
    return (mixed, pair_score)


def solution(mesh):
    dp_count, expert_count = mesh.devices.shape
    split = Mesh(mesh.devices.reshape(dp_count, expert_count // 2, 2), ("dp", "z", "c"))
    rows = P(("dp", "z", "c"), None)
    return jax.shard_map(
        body,
        mesh=split,
        in_specs=(
            rows,
            rows,
            rows,
            P(("dp", "z", "c")),
            P(),
            P(("z", "c"), None, None),
            P(("z", "c"), None, None),
            P(("z", "c"), None, None),
            P(),
        ),
        out_specs=(rows, P(("dp", "z", "c"))),
        check_vma=False,
    )
```

time: 203 us -> 192 us (0.946)
  blocking collectives: 149 us -> 26.5 us
  waiting for transfers between devices: 1.87 us -> 111 us
  matrix products: 18 us -> 22.2 us
    all_to_all x1 -> x0, blocking collectives: 98.3 us -> none  [body(): lax.all_to_all(partial_value.astype(jnp.bfloat16), 'expert', split_axis=0...]
    reduce_scatter x0 -> x2, waiting for transfers between devices: none -> 64.3 us  [the longest x1 43.5 us: body(): summed = lax.psum_scatter(half, 'z', scatter_dimension=0, tiled=False)]
    all_gather x1 -> x2, waiting for transfers between devices: 0.02 us -> 44.2 us  [the longest x1 44.2 us: gather_expert(): along_z = lax.all_gather(block, 'z', axis=0, tiled=False)]
    all_gather x3 -> x2, blocking collectives: 50.9 us -> 26.5 us  [the longest x1 24.6 us: gather_expert(): along_z = lax.all_gather(block, 'z', axis=0, tiled=False)]
    convert_element_type x0 -> x1, other arithmetic: none -> 3.86 us  [body(): half = half.reshape(z_count, tok_rows, model_width).astype(jnp.bfloat16)]
    reduce_sum x2 -> x0, other arithmetic: 3.68 us -> none  [the longest x1 2.98 us: body(): summed = received.reshape(expert_count, tok_rows, model_width).sum(axis=0)]
    dot_general x1, matrix products: 1.3 us -> 4.53 us  [body(): jnp.einsum('sqt,sqd->std', picker, result.reshape(expert_count, local_cou...]
  transfers between devices with their start and end apart: 2 -> 5, of which waited for: 1 -> 4; matrix products, arithmetic and copies ran while one was open for 3% -> 2% of each run, Pallas kernels for 0% -> 0%
where the time goes in v1:
time: 192 us; the launch traced here: 191 us
  waiting for transfers between devices  111 us (58%)
  blocking collectives  26.5 us (14%)
  matrix products  22.2 us (12%)
  between operations  13.9 us (7%)
  other arithmetic  10.2 us (5%)
  local copies, waits for them, and re-layouts  4.53 us (2%)
  starting transfers between devices  3.29 us (2%)
    all_gather x1, waiting for transfers between devices, gather_expert(): along_z = lax.all_gather(block, 'z', axis=0, tiled=False)  44.2 us
    reduce_scatter x1, waiting for transfers between devices, body(): summed = lax.psum_scatter(half, 'z', scatter_dimension=0, tiled=False)  43.5 us
    all_gather x1, blocking collectives, gather_expert(): along_z = lax.all_gather(block, 'z', axis=0, tiled=False)  24.6 us
    reduce_scatter x1, waiting for transfers between devices, body(): lax.psum_scatter(partial_value, 'c', scatter_dimension=0, tiled=False)  20.9 us
    dot_general x1, matrix products, body(): jnp.einsum('nemf,efd->nemd', hidden, w_down, preferred_element_type=jnp.f...  9.16 us
    dot_general x1, matrix products, body(): jnp.einsum('sqt,sqd->std', picker, result.reshape(expert_count, local_cou...  4.53 us
    convert_element_type x1, other arithmetic, body(): half = half.reshape(z_count, tok_rows, model_width).astype(jnp.bfloat16)  3.86 us
  transfers between devices with their start and end apart: 5, of which 4 were waited for; matrix products, arithmetic and copies ran while one was open for 2% of the time, Pallas kernels for 0%

profile of v1, /device:TPU:2, one launch (start us, length us, event | category | flops | bytes accessed | tf_op | source)
XLA Modules:
  0.0 191.3 jit_solution(8647020230223499830)
XLA Ops:
  7.2 0.7 broadcast_compare_fusion
  8.1 0.8 slice_reduce_fusion.1
  8.9 1.8 add_convert_fusion
  10.8 44.2 %all-gather.8.cloned.1.call-done = bf16[512,2048]{1,0:T(8,128)(2,1)} async-done(((bf16[64,2048]{1,0:T(8,128)(2,1)}), bf16[512,2048]{1,0:T(8,128)(2,1)}) %all-gather.8.cloned.1.call-update) | async-done | bytes 2097168 | tf_op jit(solution)/shard_map/all_gather | solution.py:33
  55.0 0.8 copy.28
  55.9 0.3 fusion.20
  56.3 24.6 %all-gather.4 = s32[8,64,24]{1,2,0:T(8,128)S(1)} all-gather(s32[1,64,24]{1,2,0:T(8,128)S(1)} %add_bitcast_fusion), channel_id=2, replica_groups=mesh['dp'=16,'z'=8,'c'=2] {'z'}, dimensions={0}, use_global_device_ids=true | all-gather | bytes 55296 | tf_op jit(solution)/shard_map/all_gather | solution.py:33
  81.0 1.9 %all-gather.1 = s32[16,64,24]{1,2,0:T(8,128)S(1)} all-gather(s32[8,64,24]{1,2,0:T(8,128)S(1)} %all-gather.4), channel_id=3, replica_groups=mesh['dp'=16,'z'=8,'c'=2] {'c'}, dimensions={0}, use_global_device_ids=true | all-gather | bytes 147456 | tf_op jit(solution)/shard_map/all_gather | solution.py:34
  82.9 0.4 fusion.27
  83.3 1.6 select_reduce_fusion
  85.1 1.2 fusion.9
  86.3 3.3 %convolution_convert_fusion = bf16[16,48,2048]{2,1,0:T(8,128)(2,1)S(1)} fusion(pred[16,48,64]{2,1,0:T(8,128)(4,1)S(1)} %fusion.9, bf16[16,64,2048]{2,1,0:T(8,128)(2,1)} %all-gather.10.cloned.1.call-done), kind=kOutput, calls=%fused_computation.8 | convolution fusion | flops 202899456 | bytes 7389184 | tf_op jit(solution)/shard_map/sqt,std->sqd/dot_general | solution.py:71
  89.6 0.1 copy-done.3
  89.7 3.0 %fusion.5 = f32[2,16,24,512]{3,2,1,0:T(8,128)} fusion(bf16[2,2048,512]{2,1,0:T(8,128)(2,1)S(1)} %copy-done.3, bf16[16,2,24,2048]{3,2,1,0:T(8,128)(2,1)S(1)} %bitcast.68), kind=kOutput, calls=%fused_computation.6 | convolution fusion | flops 1610612736 | bytes 8912896 | tf_op jit(solution)/shard_map/nemd,edf->nemf/dot_general | solution.py:75
  92.7 9.2 %fusion = bf16[16,2,24,2048]{3,2,0,1:T(8,128)(2,1)} fusion(bf16[2,512,2048]{2,1,0:T(8,128)(2,1)} %param.16, f32[16,2,24]{2,0,1:T(8,128)S(1)} %copy.30, f32[2,16,24,512]{3,2,1,0:T(8,128)} %fusion.5, bf16[2,2048,512]{2,1,0:T(8,128)(2,1)} %param.15, bf16[16,2,24,2048]{3,2,1,0:T(8,128)(2,1)S(1)} %bitcast.69), kind=kOutput, calls=%fused_computation.1 | convolution fusion | flops 3226730496 | bytes 16256000 | tf_op jit(solution)/shard_map/nemf,efd->nemd/dot_general | solution.py:78
  101.8 2.3 %copy.33 = bf16[16,2,24,2048]{3,2,1,0:T(8,128)(2,1)S(1)} copy(bf16[16,2,24,2048]{3,2,0,1:T(8,128)(2,1)} %fusion) | data formatting | bytes 6291456 | tf_op jit(solution)/shard_map/convert_element_type | solution.py:79
  104.1 4.5 %fusion.33 = f32[16,64,2048]{2,1,0:T(8,128)} fusion(pred[16,48,64]{2,1,0:T(8,128)(4,1)S(1)} %fusion.9, bf16[16,48,2048]{2,1,0:T(8,128)(2,1)S(1)} %bitcast.66), kind=kOutput, calls=%fused_computation.42 | convolution fusion | flops 201326592 | bytes 11583488 | tf_op jit(solution)/shard_map/sqt,sqd->std/dot_general | solution.py:80
  108.7 20.9 %reduce-scatter.3.cloned.1.call-done = f32[1,512,2048]{2,1,0:T(8,128)} async-done(((f32[2,512,2048]{2,1,0:T(8,128)}), f32[1,512,2048]{2,1,0:T(8,128)}) %reduce-scatter.3.cloned.1.call-update) | async-done | bytes 4194320 | tf_op jit(solution)/shard_map/reduce_scatter | solution.py:87
  129.6 3.9 %convert_element_type.47 = bf16[1,512,2048]{2,1,0:T(8,128)(2,1)} convert(f32[1,512,2048]{2,1,0:T(8,128)} %reduce-scatter.3.cloned.1.call-done) | non-fusion elementwise | flops 1048576 | bytes 6291456 | tf_op jit(solution)/shard_map/convert_element_type | solution.py:88
  133.5 43.5 %reduce-scatter.5.cloned.1.call-done = bf16[1,64,2048]{2,1,0:T(8,128)(2,1)} async-done(((bf16[8,64,2048]{2,1,0:T(8,128)(2,1)}), bf16[1,64,2048]{2,1,0:T(8,128)(2,1)}) %reduce-scatter.5.cloned.1.call-update) | async-done | bytes 262160 | tf_op jit(solution)/shard_map/reduce_scatter | solution.py:89
  177.0 2.0 %fusion.34 = f32[1,4,16]{2,0,1:T(1,128)S(1)} fusion(bf16[4,16,2048]{2,1,0:T(8,128)(2,1)} %bitcast.72, f32[2048,1,1]{0,1,2:T(1,128)S(1)} %bitcast.64), kind=kOutput, calls=%fused_computation.43 | convolution fusion | flops 1572864 | bytes 270592 | tf_op jit(solution)/shard_map/dot_general | solution.py:91
  179.1 3.1 %collective-permute-start = (f32[4]{0:T(128)S(1)}, f32[4]{0:T(128)S(1)}, u32[]{:S(2)}, u32[]{:S(2)}) collective-permute-start(f32[4]{0:T(128)S(1)} %reduce_sum.39), channel_id=1, source_target_pairs={{0,128},{128,0},{16,144},{144,16},{32,160},{160,32},{48,176},{176,... | collective-permute-start | bytes 56 | tf_op jit(solution)/shard_map/ppermute | solution.py:18
  182.2 2.0 %collective-permute-done = f32[4]{0:T(128)S(1)} collective-permute-done((f32[4]{0:T(128)S(1)}, f32[4]{0:T(128)S(1)}, u32[]{:S(2)}, u32[]{:S(2)}) %collective-permute-start) | collective-permute-done | bytes 48 | tf_op jit(solution)/shard_map/ppermute | solution.py:18
  184.2 0.5 multiply_add_fusion
  (27 shorter events, 0.9 us)
Async XLA Ops:
  7.2 169.8 %copy-start = (f32[2048]{0:T(1024)S(1)}, f32[2048]{0:T(1024)}, u32[]{:S(2)}) copy-start(f32[2048]{0:T(1024)} %param.17) | copy-start | bytes 24580
  7.2 49.1 %copy-start.1 = (s32[64,8]{0,1:T(8,128)S(1)}, s32[64,8]{0,1:T(8,128)}, u32[]{:S(2)}) copy-start(s32[64,8]{0,1:T(8,128)} %param.10) | copy-start | bytes 6148
  7.2 49.1 %copy-start.2 = (s32[64,8]{0,1:T(8,128)S(1)}, s32[64,8]{0,1:T(8,128)}, u32[]{:S(2)}) copy-start(s32[64,8]{0,1:T(8,128)} %param.11) | copy-start | bytes 6148
  7.2 47.7 %all-gather.8.cloned.1.call-start = ((), (), s32[]{:S(2)}) async-start(), calls=%async_computation.4 | async-start | bytes 2359296 | tf_op jit(solution)/shard_map/all_gather | solution.py:33
  10.7 75.6 %all-gather.10.cloned.1.call-start = ((), (), s32[]{:S(2)}) async-start(), calls=%async_computation.5 | async-start | bytes 6291456 | tf_op jit(solution)/shard_map/all_gather | solution.py:34
  55.0 74.7 %reduce-scatter.3.cloned.1.call-start = ((), (), s32[]{:S(2)}) async-start(), calls=%async_computation.2 | async-start | bytes 12582912 | tf_op jit(solution)/shard_map/reduce_scatter | solution.py:87
  86.3 3.5 %copy-start.3 = (bf16[2,2048,512]{2,1,0:T(8,128)(2,1)S(1)}, bf16[2,2048,512]{2,1,0:T(8,128)(2,1)}, u32[]{:S(2)}) copy-start(bf16[2,2048,512]{2,1,0:T(8,128)(2,1)} %param.14) | copy-start | bytes 12582916
  108.7 68.3 %reduce-scatter.5.cloned.1.call-start = ((), (), s32[]{:S(2)}) async-start(), calls=%async_computation.3 | async-start | bytes 2359296 | tf_op jit(solution)/shard_map/reduce_scatter | solution.py:89
  179.1 5.1 %collective-permute-start = (f32[4]{0:T(128)S(1)}, f32[4]{0:T(128)S(1)}, u32[]{:S(2)}, u32[]{:S(2)}) collective-permute-start(f32[4]{0:T(128)S(1)} %reduce_sum.39), channel_id=1, source_target_pairs={{0,128},{128,0},{16,144},{144,16},{32,160},{160,32},{48,176},{176,... | collective-permute-start | bytes 56 | tf_op jit(solution)/shard_map/ppermute | solution.py:18
Sparse Core Ops, SparseCore 0:
  10.8 44.0 all-gather.7
  56.7 17.5 all-gather.9
  108.8 20.7 reduce-scatter.2
  133.6 43.3 reduce-scatter.4

commit v2 on v1

--- a/solution.py
+++ b/solution.py
@@ -1,6 +1,10 @@
+import functools
+
 import jax
 import jax.numpy as jnp
 from jax import lax
+from jax.experimental import pallas as pl
+from jax.experimental.pallas import tpu as pltpu
 from jax.sharding import Mesh
 from jax.sharding import PartitionSpec as P
 
@@ -27,6 +31,91 @@
     counts = jnp.dot(earlier, onehot.astype(jnp.bfloat16), preferred_element_type=jnp.float32)
     rank_in = jnp.sum(jnp.where(onehot, counts, 0.0), axis=1).astype(jnp.int32)
     return rank_in.reshape(expert_ids.shape)
+
+
+MESH = pl.DeviceIdType.MESH
+
+
+def dispatch_kernel(z_count, blk_ref, out_ref, send_sem, recv_sem, local_sem):
+    z = lax.axis_index("z")
+    c = lax.axis_index("c")
+    row = lax.axis_index("dp")
+    other = 1 - c
+    step = 1 - 2 * c
+    fwd = lax.rem(z + step + z_count, z_count)
+    bwd = lax.rem(z - step + z_count, z_count)
+    fwd_id, bwd_id, pair_id = (row, fwd, c), (row, bwd, c), (row, z, other)
+
+    barrier = pltpu.get_barrier_semaphore()
+    for target in (fwd_id, bwd_id, pair_id):
+        pl.semaphore_signal(barrier, 1, device_id=target, device_id_type=MESH)
+    pl.semaphore_wait(barrier, 3)
+
+    mine = c * z_count + z
+    local = pltpu.make_async_copy(blk_ref, out_ref.at[mine], local_sem.at[0])
+    local.start()
+    sends = []
+
+    def send(src, slot, target):
+        copy = pltpu.make_async_remote_copy(
+            src_ref=src,
+            dst_ref=out_ref.at[slot],
+            send_sem=send_sem.at[len(sends)],
+            recv_sem=recv_sem.at[slot],
+            device_id=target,
+            device_id_type=MESH,
+        )
+        copy.start()
+        sends.append(copy)
+
+    def arrive(slot):
+        pltpu.make_async_remote_copy(
+            src_ref=out_ref.at[slot],
+            dst_ref=out_ref.at[slot],
+            send_sem=send_sem.at[0],
+            recv_sem=recv_sem.at[slot],
+            device_id=pair_id,
+            device_id_type=MESH,
+        ).wait_recv()
+
+    send(blk_ref, mine, fwd_id)
+    send(blk_ref, mine, bwd_id)
+    send(blk_ref, mine, pair_id)
+    fwd_hops = z_count // 2
+    bwd_hops = z_count - 1 - fwd_hops
+    for hop in range(1, fwd_hops + 1):
+        slot = c * z_count + lax.rem(z - step * hop + 2 * z_count, z_count)
+        arrive(slot)
+        if hop < fwd_hops:
+            send(out_ref.at[slot], slot, fwd_id)
+        send(out_ref.at[slot], slot, pair_id)
+        if hop <= bwd_hops:
+            slot = c * z_count + lax.rem(z + step * hop + 2 * z_count, z_count)
+            arrive(slot)
+            if hop < bwd_hops:
+                send(out_ref.at[slot], slot, bwd_id)
+            send(out_ref.at[slot], slot, pair_id)
+    for zz in range(z_count):
+        arrive(other * z_count + zz)
+    local.wait()
+    for copy in sends:
+        copy.wait_send()
+
+
+def gather_blocks(block, z_count):
+    count = 2 * z_count
+    return pl.pallas_call(
+        functools.partial(dispatch_kernel, z_count),
+        out_shape=jax.ShapeDtypeStruct((count,) + block.shape, block.dtype),
+        in_specs=[pl.BlockSpec(memory_space=pl.ANY)],
+        out_specs=pl.BlockSpec(memory_space=pl.ANY),
+        scratch_shapes=[
+            pltpu.SemaphoreType.DMA((count,)),
+            pltpu.SemaphoreType.DMA((count,)),
+            pltpu.SemaphoreType.DMA((1,)),
+        ],
+        compiler_params=pltpu.CompilerParams(collective_id=0, has_side_effects=True),
+    )(block)
 
 
 def gather_expert(block):
@@ -49,12 +138,19 @@
     ).astype(jnp.float32)
     inputs = (tokens.astype(jnp.float32) + tag_rows).astype(jnp.bfloat16)
     rank_in = route_ranks(expert_ids, per_device * expert_count)
-    packed = jnp.concatenate([expert_ids, gate_fixed, rank_in], axis=1)
-    inputs_all = gather_expert(inputs).reshape(expert_count, tok_rows, model_width)
-    packed_all = gather_expert(packed).reshape(expert_count, tok_rows, 3 * top_count)
-    ids_cube = packed_all[..., :top_count]
-    fixed_val = packed_all[..., top_count : 2 * top_count].astype(jnp.float32)
-    rank_cube = packed_all[..., 2 * top_count :]
+    routes = jnp.concatenate(
+        [expert_ids, rank_in, gate_fixed // 256, gate_fixed % 256], axis=1
+    ).astype(jnp.bfloat16)
+    block = jnp.concatenate([inputs, routes.reshape(-1, model_width)], axis=0)
+    gathered = gather_blocks(block, z_count)
+    inputs_all = gathered[:, :tok_rows, :]
+    routes_all = gathered[:, tok_rows:, :].reshape(expert_count, tok_rows, 4 * top_count)
+    routes_all = routes_all.astype(jnp.int32)
+    ids_cube = routes_all[..., :top_count]
+    rank_cube = routes_all[..., top_count : 2 * top_count]
+    fixed_val = (
+        routes_all[..., 2 * top_count : 3 * top_count] * 256 + routes_all[..., 3 * top_count :]
+    ).astype(jnp.float32)
     weight_cube = fixed_val / jnp.sum(fixed_val, axis=2, keepdims=True)
     my_index = lax.axis_index("z") * c_count + lax.axis_index("c")
     local_count = per_device * MOST

time: 192 us -> 163 us (0.85)
  waiting for transfers between devices: 111 us -> 67.6 us
  Pallas kernels: 0 us -> 36.2 us
  blocking collectives: 26.5 us -> 0 us
  other arithmetic: 10.2 us -> 13 us
    all_gather x2 -> x0, waiting for transfers between devices: 44.2 us -> none  [the longest x1 44.2 us: gather_expert(): along_z = lax.all_gather(block, 'z', axis=0, tiled=False)]
    pallas_call x0 -> x1, Pallas kernels: none -> 36.2 us  [gather_blocks(): pl.pallas_call(functools.partial(dispatch_kernel, z_count), out_shape=jax...]
    all_gather x2 -> x0, blocking collectives: 26.5 us -> none  [the longest x1 24.6 us: gather_expert(): along_z = lax.all_gather(block, 'z', axis=0, tiled=False)]
  transfers between devices with their start and end apart: 5 -> 3, of which waited for: 4 -> 3; matrix products, arithmetic and copies ran while one was open for 2% -> 0% of each run, Pallas kernels for 0% -> 0%
where the time goes in v2:
time: 163 us; the launch traced here: 162 us
  waiting for transfers between devices  67.6 us (41%)
  Pallas kernels  36.2 us (22%)
  matrix products  22.2 us (14%)
  between operations  14.1 us (9%)
  other arithmetic  13 us (8%)
  local copies, waits for them, and re-layouts  6.15 us (4%)
  starting transfers between devices  3.05 us (2%)
    reduce_scatter x1, waiting for transfers between devices, body(): summed = lax.psum_scatter(half, 'z', scatter_dimension=0, tiled=False)  43.5 us
    pallas_call x1, Pallas kernels, gather_blocks(): pl.pallas_call(functools.partial(dispatch_kernel, z_count), out_shape=jax...  36.2 us
    reduce_scatter x1, waiting for transfers between devices, body(): lax.psum_scatter(partial_value, 'c', scatter_dimension=0, tiled=False)  21.9 us
    dot_general x1, matrix products, body(): jnp.einsum('nemf,efd->nemd', hidden, w_down, preferred_element_type=jnp.f...  9.16 us
    dot_general x1, matrix products, body(): jnp.einsum('sqt,sqd->std', picker, result.reshape(expert_count, local_cou...  4.53 us
    convert_element_type x1, other arithmetic, body(): half = half.reshape(z_count, tok_rows, model_width).astype(jnp.bfloat16)  3.86 us
    dot_general x1, matrix products, body(): jnp.einsum('sqt,std->sqd', picker, inputs_all, preferred_element_type=jnp...  3.3 us
  transfers between devices with their start and end apart: 3, of which 3 were waited for; matrix products, arithmetic and copies ran while one was open for 0% of the time, Pallas kernels for 0%

profile of v2, /device:TPU:2, one launch (start us, length us, event | category | flops | bytes accessed | tf_op | source)
XLA Modules:
  0.0 162.3 jit_solution(13726078628795834940)
XLA Ops:
  7.2 0.7 convert.14
  7.9 0.8 copy.34
  8.7 0.7 broadcast_compare_fusion
  9.5 0.8 slice_reduce_fusion.1
  10.4 0.8 copy.35
  11.9 1.1 add_convert_fusion
  13.0 0.7 pad_maximum_fusion.blk_ref
  13.8 36.2 %shard_map.104 = bf16[16,65,2048]{2,1,0:T(8,128)(2,1)} custom-call(bf16[65,2048]{1,0:T(8,128)(2,1)} %pad_maximum_fusion.blk_ref), custom_call_target="tpu_custom_call" | custom-call | tf_op jit(solution)/shard_map/pallas_call | solution.py:107
  49.9 1.4 convert_reduce_fusion
  51.5 0.5 fusion.49
  52.6 1.2 fusion.14
  54.2 1.7 %select_reduce_fusion = f32[16,48]{1,0:T(8,128)S(1)} fusion(f32[16,64,8]{1,2,0:T(8,128)S(1)} %convert_divide_fusion, s32[16,64,8]{1,2,0:T(8,128)S(1)} %copy.40), kind=kLoop, calls=%fused_computation.11 | loop fusion | flops 1178880 | bytes 68608 | tf_op jit(solution)/shard_map/reduce_sum | solution.py:164
  56.0 3.3 %fusion.11 = bf16[16,48,2048]{2,1,0:T(8,128)(2,1)S(1)} fusion(pred[16,48,64]{2,1,0:T(8,128)(4,1)S(1)} %fusion.14, bf16[16,65,2048]{2,1,0:T(8,128)(2,1)} %shard_map.104), kind=kOutput, calls=%fused_computation.10 | convolution fusion | flops 202899456 | bytes 7389184 | tf_op jit(solution)/shard_map/sqt,std->sqd/dot_general | solution.py:167
  59.4 3.0 %fusion.5 = f32[2,16,24,512]{3,2,1,0:T(8,128)} fusion(bf16[2,2048,512]{2,1,0:T(8,128)(2,1)S(1)} %copy-done.1, bf16[16,2,24,2048]{3,2,1,0:T(8,128)(2,1)S(1)} %bitcast.64), kind=kOutput, calls=%fused_computation.6 | convolution fusion | flops 1610612736 | bytes 8912896 | tf_op jit(solution)/shard_map/nemd,edf->nemf/dot_general | solution.py:171
  62.4 9.2 %fusion = bf16[16,2,24,2048]{3,2,0,1:T(8,128)(2,1)} fusion(bf16[2,512,2048]{2,1,0:T(8,128)(2,1)} %param.16, f32[16,2,24]{2,0,1:T(8,128)S(1)} %copy.43, f32[2,16,24,512]{3,2,1,0:T(8,128)} %fusion.5, bf16[2,2048,512]{2,1,0:T(8,128)(2,1)} %param.15, bf16[16,2,24,2048]{3,2,1,0:T(8,128)(2,1)S(1)} %bitcast.65), kind=kOutput, calls=%fused_computation.1 | convolution fusion | flops 3226730496 | bytes 16256000 | tf_op jit(solution)/shard_map/nemf,efd->nemd/dot_general | solution.py:174
  71.5 2.3 %copy.46 = bf16[16,2,24,2048]{3,2,1,0:T(8,128)(2,1)S(1)} copy(bf16[16,2,24,2048]{3,2,0,1:T(8,128)(2,1)} %fusion) | data formatting | bytes 6291456 | tf_op jit(solution)/shard_map/convert_element_type | solution.py:175
  73.8 4.5 %fusion.50 = f32[16,64,2048]{2,1,0:T(8,128)} fusion(pred[16,48,64]{2,1,0:T(8,128)(4,1)S(1)} %fusion.14, bf16[16,48,2048]{2,1,0:T(8,128)(2,1)S(1)} %bitcast.62), kind=kOutput, calls=%fused_computation.62 | convolution fusion | flops 201326592 | bytes 11583488 | tf_op jit(solution)/shard_map/sqt,sqd->std/dot_general | solution.py:176
  78.4 21.9 %reduce-scatter.3.cloned.1.call-done = f32[1,512,2048]{2,1,0:T(8,128)} async-done(((f32[2,512,2048]{2,1,0:T(8,128)}), f32[1,512,2048]{2,1,0:T(8,128)}) %reduce-scatter.3.cloned.1.call-update) | async-done | bytes 4194320 | tf_op jit(solution)/shard_map/reduce_scatter | solution.py:183
  100.4 3.9 %convert_element_type.67 = bf16[1,512,2048]{2,1,0:T(8,128)(2,1)} convert(f32[1,512,2048]{2,1,0:T(8,128)} %reduce-scatter.3.cloned.1.call-done) | non-fusion elementwise | flops 1048576 | bytes 6291456 | tf_op jit(solution)/shard_map/convert_element_type | solution.py:184
  104.3 43.5 %reduce-scatter.5.cloned.1.call-done = bf16[1,64,2048]{2,1,0:T(8,128)(2,1)} async-done(((bf16[8,64,2048]{2,1,0:T(8,128)(2,1)}), bf16[1,64,2048]{2,1,0:T(8,128)(2,1)}) %reduce-scatter.5.cloned.1.call-update) | async-done | bytes 262160 | tf_op jit(solution)/shard_map/reduce_scatter | solution.py:185
  147.7 2.0 %fusion.51 = f32[1,4,16]{2,0,1:T(1,128)S(1)} fusion(bf16[4,16,2048]{2,1,0:T(8,128)(2,1)} %bitcast.67, f32[2048,1,1]{0,1,2:T(1,128)S(1)} %bitcast.60), kind=kOutput, calls=%fused_computation.63 | convolution fusion | flops 1572864 | bytes 270592 | tf_op jit(solution)/shard_map/dot_general | solution.py:187
  149.8 3.0 %collective-permute-start = (f32[4]{0:T(128)S(1)}, f32[4]{0:T(128)S(1)}, u32[]{:S(2)}, u32[]{:S(2)}) collective-permute-start(f32[4]{0:T(128)S(1)} %reduce_sum.39), channel_id=1, source_target_pairs={{0,128},{128,0},{16,144},{144,16},{32,160},{160,32},{48,176},{176,... | collective-permute-start | bytes 56 | tf_op jit(solution)/shard_map/ppermute | solution.py:22
  152.8 2.2 %collective-permute-done = f32[4]{0:T(128)S(1)} collective-permute-done((f32[4]{0:T(128)S(1)}, f32[4]{0:T(128)S(1)}, u32[]{:S(2)}, u32[]{:S(2)}) %collective-permute-start) | collective-permute-done | bytes 48 | tf_op jit(solution)/shard_map/ppermute | solution.py:22
  155.0 0.5 multiply_add_fusion.1
  (26 shorter events, 2.6 us)
Async XLA Ops:
  7.2 140.6 %copy-start = (f32[2048]{0:T(1024)S(1)}, f32[2048]{0:T(1024)}, u32[]{:S(2)}) copy-start(f32[2048]{0:T(1024)} %param.17) | copy-start | bytes 24580
  7.2 93.2 %reduce-scatter.3.cloned.1.call-start = ((), (), s32[]{:S(2)}) async-start(), calls=%async_computation.2 | async-start | bytes 12582912 | tf_op jit(solution)/shard_map/reduce_scatter | solution.py:183
  56.0 3.5 %copy-start.1 = (bf16[2,2048,512]{2,1,0:T(8,128)(2,1)S(1)}, bf16[2,2048,512]{2,1,0:T(8,128)(2,1)}, u32[]{:S(2)}) copy-start(bf16[2,2048,512]{2,1,0:T(8,128)(2,1)} %param.14) | copy-start | bytes 12582916
  78.4 69.3 %reduce-scatter.5.cloned.1.call-start = ((), (), s32[]{:S(2)}) async-start(), calls=%async_computation.3 | async-start | bytes 2359296 | tf_op jit(solution)/shard_map/reduce_scatter | solution.py:185
  149.8 5.1 %collective-permute-start = (f32[4]{0:T(128)S(1)}, f32[4]{0:T(128)S(1)}, u32[]{:S(2)}, u32[]{:S(2)}) collective-permute-start(f32[4]{0:T(128)S(1)} %reduce_sum.39), channel_id=1, source_target_pairs={{0,128},{128,0},{16,144},{144,16},{32,160},{160,32},{48,176},{176,... | collective-permute-start | bytes 56 | tf_op jit(solution)/shard_map/ppermute | solution.py:22
Sparse Core Ops, SparseCore 0:
  78.5 21.8 reduce-scatter.2
  104.4 43.3 reduce-scatter.4

commit v3 on v2

--- a/solution.py
+++ b/solution.py
@@ -118,9 +118,109 @@
     )(block)
 
 
-def gather_expert(block):
-    along_z = lax.all_gather(block, "z", axis=0, tiled=False)
-    return lax.all_gather(along_z, "c", axis=0, tiled=False)
+def combine_kernel(
+    z_count, part_ref, out_ref, pair_buf, fwd_buf, bwd_buf, fwd_out, bwd_out, send_sem, recv_sem
+):
+    z = lax.axis_index("z")
+    c = lax.axis_index("c")
+    row = lax.axis_index("dp")
+    other = 1 - c
+    step = 1 - 2 * c
+    fwd = lax.rem(z + step + z_count, z_count)
+    bwd = lax.rem(z - step + z_count, z_count)
+    fwd_id, bwd_id, pair_id = (row, fwd, c), (row, bwd, c), (row, z, other)
+    fwd_hops = z_count // 2
+    bwd_hops = z_count - 1 - fwd_hops
+
+    barrier = pltpu.get_barrier_semaphore()
+    for target in (fwd_id, bwd_id, pair_id):
+        pl.semaphore_signal(barrier, 1, device_id=target, device_id_type=MESH)
+    pl.semaphore_wait(barrier, 3)
+
+    sends = []
+
+    def send(src, dst, sem, target):
+        copy = pltpu.make_async_remote_copy(
+            src_ref=src,
+            dst_ref=dst,
+            send_sem=send_sem.at[len(sends)],
+            recv_sem=recv_sem.at[sem],
+            device_id=target,
+            device_id_type=MESH,
+        )
+        copy.start()
+        sends.append(copy)
+
+    def arrive(dst, sem):
+        pltpu.make_async_remote_copy(
+            src_ref=dst,
+            dst_ref=dst,
+            send_sem=send_sem.at[0],
+            recv_sem=recv_sem.at[sem],
+            device_id=pair_id,
+            device_id_type=MESH,
+        ).wait_recv()
+
+    for zz in range(z_count):
+        send(part_ref.at[other, zz], pair_buf.at[zz], zz, pair_id)
+
+    def own(dest):
+        arrive(pair_buf.at[dest], dest)
+        return part_ref[c, dest].astype(jnp.float32) + pair_buf[dest].astype(jnp.float32)
+
+    fwd_sem = z_count
+    bwd_sem = z_count + fwd_hops
+    for hop in range(1, fwd_hops + 1):
+        dest = lax.rem(z + step * (fwd_hops + 1 - hop) + 2 * z_count, z_count)
+        total = own(dest)
+        if hop > 1:
+            arrive(fwd_buf.at[hop - 2], fwd_sem + hop - 2)
+            total = total + fwd_buf[hop - 2].astype(jnp.float32)
+        fwd_out[hop - 1] = total.astype(fwd_out.dtype)
+        send(fwd_out.at[hop - 1], fwd_buf.at[hop - 1], fwd_sem + hop - 1, fwd_id)
+        if hop <= bwd_hops:
+            dest = lax.rem(z - step * (bwd_hops + 1 - hop) + 2 * z_count, z_count)
+            total = own(dest)
+            if hop > 1:
+                arrive(bwd_buf.at[hop - 2], bwd_sem + hop - 2)
+                total = total + bwd_buf[hop - 2].astype(jnp.float32)
+            bwd_out[hop - 1] = total.astype(bwd_out.dtype)
+            send(bwd_out.at[hop - 1], bwd_buf.at[hop - 1], bwd_sem + hop - 1, bwd_id)
+    total = own(z)
+    arrive(fwd_buf.at[fwd_hops - 1], fwd_sem + fwd_hops - 1)
+    total = total + fwd_buf[fwd_hops - 1].astype(jnp.float32)
+    if bwd_hops > 0:
+        arrive(bwd_buf.at[bwd_hops - 1], bwd_sem + bwd_hops - 1)
+        total = total + bwd_buf[bwd_hops - 1].astype(jnp.float32)
+    out_ref[...] = total.astype(out_ref.dtype)
+    for copy in sends:
+        copy.wait_send()
+
+
+def scatter_sums(partial):
+    c_count, z_count, rows, width = partial.shape
+    fwd_hops = z_count // 2
+    bwd_hops = max(z_count - 1 - fwd_hops, 1)
+    block = (rows, width)
+    vmem = pl.BlockSpec(memory_space=pltpu.VMEM)
+    return pl.pallas_call(
+        functools.partial(combine_kernel, z_count),
+        out_shape=jax.ShapeDtypeStruct(block, partial.dtype),
+        in_specs=[vmem],
+        out_specs=vmem,
+        scratch_shapes=[
+            pltpu.VMEM((z_count,) + block, partial.dtype),
+            pltpu.VMEM((fwd_hops,) + block, partial.dtype),
+            pltpu.VMEM((bwd_hops,) + block, partial.dtype),
+            pltpu.VMEM((fwd_hops,) + block, partial.dtype),
+            pltpu.VMEM((bwd_hops,) + block, partial.dtype),
+            pltpu.SemaphoreType.DMA((2 * z_count,)),
+            pltpu.SemaphoreType.DMA((2 * z_count,)),
+        ],
+        compiler_params=pltpu.CompilerParams(
+            collective_id=1, has_side_effects=True, vmem_limit_bytes=48 * 1024 * 1024
+        ),
+    )(partial)
 
 
 def body(
@@ -179,11 +279,8 @@
         result.reshape(expert_count, local_count, model_width),
         preferred_element_type=jnp.float32,
     )
-    partial_value = partial_value.reshape(c_count, z_count * tok_rows, model_width)
-    half = lax.psum_scatter(partial_value, "c", scatter_dimension=0, tiled=False)
-    half = half.reshape(z_count, tok_rows, model_width).astype(jnp.bfloat16)
-    summed = lax.psum_scatter(half, "z", scatter_dimension=0, tiled=False)
-    mixed = summed.astype(jnp.bfloat16)
+    partial_value = partial_value.reshape(c_count, z_count, tok_rows, model_width)
+    mixed = scatter_sums(partial_value.astype(jnp.bfloat16))
     token_score = jnp.dot(mixed.astype(jnp.float32), score_head, precision=lax.Precision.HIGHEST)
     seq_score = token_score.reshape(-1, SEQ_LEN).sum(axis=1)
     partner = from_partner(seq_score, "dp", lax.axis_size("dp").bit_length() - 2)

time: 163 us -> 110 us (0.67)
  waiting for transfers between devices: 67.6 us -> 1.85 us
  Pallas kernels: 36.2 us -> 69 us
  between operations: 14.1 us -> 0.76 us
  matrix products: 22.2 us -> 17.3 us
  other arithmetic: 13 us -> 9.35 us
    reduce_scatter x2 -> x0, waiting for transfers between devices: 65.4 us -> none  [the longest x1 43.5 us: body(): summed = lax.psum_scatter(half, 'z', scatter_dimension=0, tiled=False)]
    pallas_call x0 -> x1, Pallas kernels: none -> 32.8 us  [scatter_sums(): pl.pallas_call(functools.partial(combine_kernel, z_count), out_shape=jax....]
    convert_element_type x1 -> x0, other arithmetic: 3.86 us -> none  [body(): half = half.reshape(z_count, tok_rows, model_width).astype(jnp.bfloat16)]
    dot_general x1, matrix products: 4.53 us -> 1.3 us  [body(): jnp.einsum('sqt,sqd->std', picker, result.reshape(expert_count, local_cou...]
    dot_general x1, matrix products: 1.96 us -> 0.3 us  [body(): jnp.dot(mixed.astype(jnp.float32), score_head, precision=lax.Precision.HI...]
  transfers between devices with their start and end apart: 3 -> 1, of which waited for: 3 -> 1; matrix products, arithmetic and copies ran while one was open for 0% -> 0% of each run, Pallas kernels for 0% -> 0%
where the time goes in v3:
time: 110 us; the launch traced here: 108 us
  Pallas kernels  69 us (63%)
  matrix products  17.3 us (16%)
  other arithmetic  9.35 us (8%)
  local copies, waits for them, and re-layouts  6.94 us (6%)
  starting transfers between devices  3.28 us (3%)
  waiting for transfers between devices  1.85 us (2%)
    pallas_call x1, Pallas kernels, gather_blocks(): pl.pallas_call(functools.partial(dispatch_kernel, z_count), out_shape=jax...  36.2 us
    pallas_call x1, Pallas kernels, scatter_sums(): pl.pallas_call(functools.partial(combine_kernel, z_count), out_shape=jax....  32.8 us
    dot_general x1, matrix products, body(): jnp.einsum('nemf,efd->nemd', hidden, w_down, preferred_element_type=jnp.f...  9.16 us
    dot_general x1, matrix products, body(): jnp.einsum('sqt,std->sqd', picker, inputs_all, preferred_element_type=jnp...  3.3 us
    ppermute x1, starting transfers between devices, from_partner(): return lax.ppermute(block, axis, route)  3.28 us
    dot_general x1, matrix products, body(): jnp.einsum('nemd,edf->nemf', row_block, w_gate, preferred_element_type=jn...  2.96 us
    unnamed x9, local copies, waits for them, and re-layouts  2.76 us
    convert_element_type x1, local copies, waits for them, and re-layouts, body(): result = (slot_weight[..., None] * down_out).astype(jnp.bfloat16)  2.29 us
  transfers between devices with their start and end apart: 1, of which 1 were waited for; matrix products, arithmetic and copies ran while one was open for 0% of the time, Pallas kernels for 0%

profile of v3, /device:TPU:2, one launch (start us, length us, event | category | flops | bytes accessed | tf_op | source)
XLA Modules:
  0.0 108.4 jit_solution(692470038798477791)
XLA Ops:
  0.6 0.7 convert.14
  1.3 0.8 copy.34
  2.1 0.7 broadcast_compare_fusion
  2.9 0.8 slice_reduce_fusion.1
  3.9 0.8 copy.35
  5.3 1.1 %add_convert_fusion = bf16[64,2048]{1,0:T(8,128)(2,1)S(1)} fusion(bf16[64,2048]{1,0:T(8,128)(2,1)} %param.9, pred[64]{0:T(512)(128)(4,1)S(1)} %eq.47, bf16[2048]{0:T(1024)(128)(2,1)S(1)} %get-tuple-element.3, bf16[2048]{0:T(1024)(128)(2,1)S(1)} %get-tuple-element.2), kind=kLoop, calls=%fused_computation.32 | loop fusion | flops 655360 | bytes 532544 | tf_op jit(solution)/shard_map/convert_element_type | solution.py:239
  6.4 0.7 pad_maximum_fusion.blk_ref
  7.2 36.2 %shard_map.104 = bf16[16,65,2048]{2,1,0:T(8,128)(2,1)} custom-call(bf16[65,2048]{1,0:T(8,128)(2,1)} %pad_maximum_fusion.blk_ref), custom_call_target="tpu_custom_call" | custom-call | tf_op jit(solution)/shard_map/pallas_call | solution.py:107
  43.3 1.4 %convert_reduce_fusion = s32[16,2048]{1,0:T(8,128)S(1)} fusion(bf16[16,65,2048]{2,1,0:T(8,128)(2,1)} %shard_map.104), kind=kLoop, calls=%fused_computation.34 | loop fusion | flops 32768 | bytes 196608 | tf_op jit(solution)/shard_map/convert_element_type | solution.py:248
  44.9 0.5 fusion.49
  46.0 1.2 %fusion.14 = pred[16,48,64]{2,1,0:T(8,128)(4,1)S(1)} fusion(s32[16,64,8]{1,2,0:T(8,128)S(1)} %copy.40), kind=kLoop, calls=%fused_computation.14 | loop fusion | flops 737280 | bytes 81920 | tf_op jit(solution)/shard_map/reduce_or | solution.py:263
  47.2 0.6 convert_divide_fusion
  47.8 1.7 %select_reduce_fusion = f32[16,48]{1,0:T(8,128)S(1)} fusion(f32[16,64,8]{1,2,0:T(8,128)S(1)} %convert_divide_fusion, s32[16,64,8]{1,2,0:T(8,128)S(1)} %copy.40), kind=kLoop, calls=%fused_computation.12 | loop fusion | flops 1178880 | bytes 68608 | tf_op jit(solution)/shard_map/reduce_sum | solution.py:264
  49.6 3.3 %fusion.11 = bf16[16,48,2048]{2,1,0:T(8,128)(2,1)S(1)} fusion(pred[16,48,64]{2,1,0:T(8,128)(4,1)S(1)} %fusion.14, bf16[16,65,2048]{2,1,0:T(8,128)(2,1)} %shard_map.104), kind=kOutput, calls=%fused_computation.11 | convolution fusion | flops 202899456 | bytes 7389184 | tf_op jit(solution)/shard_map/sqt,std->sqd/dot_general | solution.py:267
  53.0 3.0 %fusion.5 = f32[2,16,24,512]{3,2,1,0:T(8,128)} fusion(bf16[2,2048,512]{2,1,0:T(8,128)(2,1)S(1)} %copy-done.1, bf16[16,2,24,2048]{3,2,1,0:T(8,128)(2,1)S(1)} %bitcast.60), kind=kOutput, calls=%fused_computation.6 | convolution fusion | flops 1610612736 | bytes 8912896 | tf_op jit(solution)/shard_map/nemd,edf->nemf/dot_general | solution.py:271
  56.0 9.2 %fusion = bf16[16,2,24,2048]{3,2,0,1:T(8,128)(2,1)} fusion(bf16[2,512,2048]{2,1,0:T(8,128)(2,1)} %param.16, f32[16,2,24]{2,0,1:T(8,128)S(1)} %copy.43, f32[2,16,24,512]{3,2,1,0:T(8,128)} %fusion.5, bf16[2,2048,512]{2,1,0:T(8,128)(2,1)} %param.15, bf16[16,2,24,2048]{3,2,1,0:T(8,128)(2,1)S(1)} %bitcast.61), kind=kOutput, calls=%fused_computation.1 | convolution fusion | flops 3226730496 | bytes 16256000 | tf_op jit(solution)/shard_map/nemf,efd->nemd/dot_general | solution.py:274
  65.1 2.3 %copy.46 = bf16[16,2,24,2048]{3,2,1,0:T(8,128)(2,1)S(1)} copy(bf16[16,2,24,2048]{3,2,0,1:T(8,128)(2,1)} %fusion) | data formatting | bytes 6291456 | tf_op jit(solution)/shard_map/convert_element_type | solution.py:275
  67.4 1.3 %convolution_convert_fusion = bf16[16,64,2048]{2,1,0:T(8,128)(2,1)S(1)} fusion(pred[16,48,64]{2,1,0:T(8,128)(4,1)S(1)} %fusion.14, bf16[16,48,2048]{2,1,0:T(8,128)(2,1)S(1)} %bitcast.59), kind=kOutput, calls=%fused_computation.10 | convolution fusion | flops 203423744 | bytes 7389184 | tf_op jit(solution)/shard_map/sqt,sqd->std/dot_general | solution.py:276
  68.7 32.8 %shard_map.105 = bf16[64,2048]{1,0:T(8,128)(2,1)S(1)} custom-call(bf16[2,8,64,2048]{3,2,1,0:T(8,128)(2,1)S(1)} %bitcast.58), custom_call_target="tpu_custom_call" | custom-call | tf_op jit(solution)/shard_map/pallas_call | solution.py:206
  101.6 0.3 convolution_bitcast_fusion
  102.1 3.3 %collective-permute-start = (f32[4]{0:T(128)S(1)}, f32[4]{0:T(128)S(1)}, u32[]{:S(2)}, u32[]{:S(2)}) collective-permute-start(f32[4]{0:T(128)S(1)} %reduce_sum.39), channel_id=1, source_target_pairs={{0,128},{128,0},{16,144},{144,16},{32,160},{160,32},{48,176},{176,... | collective-permute-start | bytes 56 | tf_op jit(solution)/shard_map/ppermute | solution.py:22
  105.4 1.8 %collective-permute-done = f32[4]{0:T(128)S(1)} collective-permute-done((f32[4]{0:T(128)S(1)}, f32[4]{0:T(128)S(1)}, u32[]{:S(2)}, u32[]{:S(2)}) %collective-permute-start) | collective-permute-done | bytes 48 | tf_op jit(solution)/shard_map/ppermute | solution.py:22
  107.2 0.5 multiply_add_fusion.1
  107.7 0.7 copy.61
  (22 shorter events, 2.1 us)
Async XLA Ops:
  0.6 100.9 %copy-start = (f32[2048]{0:T(1024)S(1)}, f32[2048]{0:T(1024)}, u32[]{:S(2)}) copy-start(f32[2048]{0:T(1024)} %param.17) | copy-start | bytes 24580
  49.6 3.5 %copy-start.1 = (bf16[2,2048,512]{2,1,0:T(8,128)(2,1)S(1)}, bf16[2,2048,512]{2,1,0:T(8,128)(2,1)}, u32[]{:S(2)}) copy-start(bf16[2,2048,512]{2,1,0:T(8,128)(2,1)} %param.14) | copy-start | bytes 12582916
  102.1 5.1 %collective-permute-start = (f32[4]{0:T(128)S(1)}, f32[4]{0:T(128)S(1)}, u32[]{:S(2)}, u32[]{:S(2)}) collective-permute-start(f32[4]{0:T(128)S(1)} %reduce_sum.39), channel_id=1, source_target_pairs={{0,128},{128,0},{16,144},{144,16},{32,160},{160,32},{48,176},{176,... | collective-permute-start | bytes 56 | tf_op jit(solution)/shard_map/ppermute | solution.py:22

commit v4 on v3

--- a/solution.py
+++ b/solution.py
@@ -36,7 +36,7 @@
 MESH = pl.DeviceIdType.MESH
 
 
-def dispatch_kernel(z_count, blk_ref, out_ref, send_sem, recv_sem, local_sem):
+def dispatch_kernel(z_count, chunks, blk_ref, out_ref, send_sem, recv_sem, local_sem):
     z = lax.axis_index("z")
     c = lax.axis_index("c")
     row = lax.axis_index("dp")
@@ -45,6 +45,7 @@
     fwd = lax.rem(z + step + z_count, z_count)
     bwd = lax.rem(z - step + z_count, z_count)
     fwd_id, bwd_id, pair_id = (row, fwd, c), (row, bwd, c), (row, z, other)
+    piece = blk_ref.shape[0] // chunks
 
     barrier = pltpu.get_barrier_semaphore()
     for target in (fwd_id, bwd_id, pair_id):
@@ -56,62 +57,70 @@
     local.start()
     sends = []
 
-    def send(src, slot, target):
+    def part(ref, k):
+        return ref.at[pl.ds(k * piece, piece)]
+
+    def send(src, slot, k, target):
         copy = pltpu.make_async_remote_copy(
-            src_ref=src,
-            dst_ref=out_ref.at[slot],
+            src_ref=part(src, k),
+            dst_ref=part(out_ref.at[slot], k),
             send_sem=send_sem.at[len(sends)],
-            recv_sem=recv_sem.at[slot],
+            recv_sem=recv_sem.at[slot * chunks + k],
             device_id=target,
             device_id_type=MESH,
         )
         copy.start()
         sends.append(copy)
 
-    def arrive(slot):
+    def arrive(slot, k):
+        view = part(out_ref.at[slot], k)
         pltpu.make_async_remote_copy(
-            src_ref=out_ref.at[slot],
-            dst_ref=out_ref.at[slot],
+            src_ref=view,
+            dst_ref=view,
             send_sem=send_sem.at[0],
-            recv_sem=recv_sem.at[slot],
+            recv_sem=recv_sem.at[slot * chunks + k],
             device_id=pair_id,
             device_id_type=MESH,
         ).wait_recv()
 
-    send(blk_ref, mine, fwd_id)
-    send(blk_ref, mine, bwd_id)
-    send(blk_ref, mine, pair_id)
+    for k in range(chunks):
+        send(blk_ref, mine, k, fwd_id)
+        send(blk_ref, mine, k, bwd_id)
+    for k in range(chunks):
+        send(blk_ref, mine, k, pair_id)
     fwd_hops = z_count // 2
     bwd_hops = z_count - 1 - fwd_hops
     for hop in range(1, fwd_hops + 1):
-        slot = c * z_count + lax.rem(z - step * hop + 2 * z_count, z_count)
-        arrive(slot)
-        if hop < fwd_hops:
-            send(out_ref.at[slot], slot, fwd_id)
-        send(out_ref.at[slot], slot, pair_id)
-        if hop <= bwd_hops:
-            slot = c * z_count + lax.rem(z + step * hop + 2 * z_count, z_count)
-            arrive(slot)
-            if hop < bwd_hops:
-                send(out_ref.at[slot], slot, bwd_id)
-            send(out_ref.at[slot], slot, pair_id)
+        for k in range(chunks):
+            slot = c * z_count + lax.rem(z - step * hop + 2 * z_count, z_count)
+            arrive(slot, k)
+            if hop < fwd_hops:
+                send(out_ref.at[slot], slot, k, fwd_id)
+            send(out_ref.at[slot], slot, k, pair_id)
+            if hop <= bwd_hops:
+                slot = c * z_count + lax.rem(z + step * hop + 2 * z_count, z_count)
+                arrive(slot, k)
+                if hop < bwd_hops:
+                    send(out_ref.at[slot], slot, k, bwd_id)
+                send(out_ref.at[slot], slot, k, pair_id)
     for zz in range(z_count):
-        arrive(other * z_count + zz)
+        for k in range(chunks):
+            arrive(other * z_count + zz, k)
     local.wait()
     for copy in sends:
         copy.wait_send()
 
 
-def gather_blocks(block, z_count):
+def gather_blocks(block, z_count, chunks):
     count = 2 * z_count
     return pl.pallas_call(
-        functools.partial(dispatch_kernel, z_count),
+        functools.partial(dispatch_kernel, z_count, chunks),
         out_shape=jax.ShapeDtypeStruct((count,) + block.shape, block.dtype),
         in_specs=[pl.BlockSpec(memory_space=pl.ANY)],
         out_specs=pl.BlockSpec(memory_space=pl.ANY),
         scratch_shapes=[
-            pltpu.SemaphoreType.DMA((count,)),
-            pltpu.SemaphoreType.DMA((count,)),
+            pltpu.SemaphoreType.DMA((2 * count * chunks,)),
+            pltpu.SemaphoreType.DMA((count * chunks,)),
             pltpu.SemaphoreType.DMA((1,)),
         ],
         compiler_params=pltpu.CompilerParams(collective_id=0, has_side_effects=True),
@@ -119,7 +128,8 @@
 
 
 def combine_kernel(
-    z_count, part_ref, out_ref, pair_buf, fwd_buf, bwd_buf, fwd_out, bwd_out, send_sem, recv_sem
+    z_count, chunks, part_ref, out_ref, pair_buf, fwd_buf, bwd_buf, fwd_out, bwd_out,
+    send_sem, recv_sem,
 ):
     z = lax.axis_index("z")
     c = lax.axis_index("c")
@@ -131,6 +141,7 @@
     fwd_id, bwd_id, pair_id = (row, fwd, c), (row, bwd, c), (row, z, other)
     fwd_hops = z_count // 2
     bwd_hops = z_count - 1 - fwd_hops
+    piece = part_ref.shape[2] // chunks
 
     barrier = pltpu.get_barrier_semaphore()
     for target in (fwd_id, bwd_id, pair_id):
@@ -161,50 +172,71 @@
             device_id_type=MESH,
         ).wait_recv()
 
-    for zz in range(z_count):
-        send(part_ref.at[other, zz], pair_buf.at[zz], zz, pair_id)
-
-    def own(dest):
-        arrive(pair_buf.at[dest], dest)
-        return part_ref[c, dest].astype(jnp.float32) + pair_buf[dest].astype(jnp.float32)
+    def order(ring_step):
+        dests = []
+        for hop in range(1, fwd_hops + 1):
+            dests.append(lax.rem(z + ring_step * (fwd_hops + 1 - hop) + 2 * z_count, z_count))
+            if hop <= bwd_hops:
+                dests.append(lax.rem(z - ring_step * (bwd_hops + 1 - hop) + 2 * z_count, z_count))
+        return dests + [z]
+
+    for n, dest in enumerate(order(-step)):
+        send(part_ref.at[other, dest], pair_buf.at[n], n, pair_id)
+    def own(dest, n, k):
+        if k == 0:
+            arrive(pair_buf.at[n], n)
+        rows = pl.ds(k * piece, piece)
+        return part_ref[c, dest, rows].astype(jnp.float32) + pair_buf[n, rows].astype(
+            jnp.float32
+        )
 
     fwd_sem = z_count
-    bwd_sem = z_count + fwd_hops
+    bwd_sem = z_count + fwd_hops * chunks
     for hop in range(1, fwd_hops + 1):
-        dest = lax.rem(z + step * (fwd_hops + 1 - hop) + 2 * z_count, z_count)
-        total = own(dest)
-        if hop > 1:
-            arrive(fwd_buf.at[hop - 2], fwd_sem + hop - 2)
-            total = total + fwd_buf[hop - 2].astype(jnp.float32)
-        fwd_out[hop - 1] = total.astype(fwd_out.dtype)
-        send(fwd_out.at[hop - 1], fwd_buf.at[hop - 1], fwd_sem + hop - 1, fwd_id)
-        if hop <= bwd_hops:
-            dest = lax.rem(z - step * (bwd_hops + 1 - hop) + 2 * z_count, z_count)
-            total = own(dest)
+        for k in range(chunks):
+            rows = pl.ds(k * piece, piece)
+            dest = lax.rem(z + step * (fwd_hops + 1 - hop) + 2 * z_count, z_count)
+            n = hop - 1 + min(hop - 1, bwd_hops)
+            total = own(dest, n, k)
             if hop > 1:
-                arrive(bwd_buf.at[hop - 2], bwd_sem + hop - 2)
-                total = total + bwd_buf[hop - 2].astype(jnp.float32)
-            bwd_out[hop - 1] = total.astype(bwd_out.dtype)
-            send(bwd_out.at[hop - 1], bwd_buf.at[hop - 1], bwd_sem + hop - 1, bwd_id)
-    total = own(z)
-    arrive(fwd_buf.at[fwd_hops - 1], fwd_sem + fwd_hops - 1)
-    total = total + fwd_buf[fwd_hops - 1].astype(jnp.float32)
-    if bwd_hops > 0:
-        arrive(bwd_buf.at[bwd_hops - 1], bwd_sem + bwd_hops - 1)
-        total = total + bwd_buf[bwd_hops - 1].astype(jnp.float32)
-    out_ref[...] = total.astype(out_ref.dtype)
+                sem = fwd_sem + (hop - 2) * chunks + k
+                arrive(fwd_buf.at[hop - 2, rows], sem)
+                total = total + fwd_buf[hop - 2, rows].astype(jnp.float32)
+            fwd_out[hop - 1, rows] = total.astype(fwd_out.dtype)
+            sem = fwd_sem + (hop - 1) * chunks + k
+            send(fwd_out.at[hop - 1, rows], fwd_buf.at[hop - 1, rows], sem, fwd_id)
+            if hop <= bwd_hops:
+                dest = lax.rem(z - step * (bwd_hops + 1 - hop) + 2 * z_count, z_count)
+                total = own(dest, n + 1, k)
+                if hop > 1:
+                    sem = bwd_sem + (hop - 2) * chunks + k
+                    arrive(bwd_buf.at[hop - 2, rows], sem)
+                    total = total + bwd_buf[hop - 2, rows].astype(jnp.float32)
+                bwd_out[hop - 1, rows] = total.astype(bwd_out.dtype)
+                sem = bwd_sem + (hop - 1) * chunks + k
+                send(bwd_out.at[hop - 1, rows], bwd_buf.at[hop - 1, rows], sem, bwd_id)
+    for k in range(chunks):
+        rows = pl.ds(k * piece, piece)
+        total = own(z, fwd_hops + bwd_hops, k)
+        arrive(fwd_buf.at[fwd_hops - 1, rows], fwd_sem + (fwd_hops - 1) * chunks + k)
+        total = total + fwd_buf[fwd_hops - 1, rows].astype(jnp.float32)
+        if bwd_hops > 0:
+            arrive(bwd_buf.at[bwd_hops - 1, rows], bwd_sem + (bwd_hops - 1) * chunks + k)
+            total = total + bwd_buf[bwd_hops - 1, rows].astype(jnp.float32)
+        out_ref[rows] = total.astype(out_ref.dtype)
     for copy in sends:
         copy.wait_send()
 
 
-def scatter_sums(partial):
+def scatter_sums(partial, chunks):
     c_count, z_count, rows, width = partial.shape
     fwd_hops = z_count // 2
     bwd_hops = max(z_count - 1 - fwd_hops, 1)
     block = (rows, width)
     vmem = pl.BlockSpec(memory_space=pltpu.VMEM)
+    sems = z_count + (fwd_hops + bwd_hops) * chunks
     return pl.pallas_call(
-        functools.partial(combine_kernel, z_count),
+        functools.partial(combine_kernel, z_count, chunks),
         out_shape=jax.ShapeDtypeStruct(block, partial.dtype),
         in_specs=[vmem],
         out_specs=vmem,
@@ -214,8 +246,8 @@
             pltpu.VMEM((bwd_hops,) + block, partial.dtype),
             pltpu.VMEM((fwd_hops,) + block, partial.dtype),
             pltpu.VMEM((bwd_hops,) + block, partial.dtype),
-            pltpu.SemaphoreType.DMA((2 * z_count,)),
-            pltpu.SemaphoreType.DMA((2 * z_count,)),
+            pltpu.SemaphoreType.DMA((sems,)),
+            pltpu.SemaphoreType.DMA((sems,)),
         ],
         compiler_params=pltpu.CompilerParams(
             collective_id=1, has_side_effects=True, vmem_limit_bytes=48 * 1024 * 1024
@@ -241,11 +273,11 @@
     routes = jnp.concatenate(
         [expert_ids, rank_in, gate_fixed // 256, gate_fixed % 256], axis=1
     ).astype(jnp.bfloat16)
-    block = jnp.concatenate([inputs, routes.reshape(-1, model_width)], axis=0)
-    gathered = gather_blocks(block, z_count)
-    inputs_all = gathered[:, :tok_rows, :]
-    routes_all = gathered[:, tok_rows:, :].reshape(expert_count, tok_rows, 4 * top_count)
-    routes_all = routes_all.astype(jnp.int32)
+    routes = jnp.pad(routes, ((0, 0), (0, 128 - 4 * top_count)))
+    block = jnp.concatenate([inputs, routes], axis=1)
+    gathered = gather_blocks(block, z_count, 2)
+    inputs_all = gathered[:, :, :model_width]
+    routes_all = gathered[:, :, model_width : model_width + 4 * top_count].astype(jnp.int32)
     ids_cube = routes_all[..., :top_count]
     rank_cube = routes_all[..., top_count : 2 * top_count]
     fixed_val = (
@@ -280,7 +312,7 @@
         preferred_element_type=jnp.float32,
     )
     partial_value = partial_value.reshape(c_count, z_count, tok_rows, model_width)
-    mixed = scatter_sums(partial_value.astype(jnp.bfloat16))
+    mixed = scatter_sums(partial_value.astype(jnp.bfloat16), 2)
     token_score = jnp.dot(mixed.astype(jnp.float32), score_head, precision=lax.Precision.HIGHEST)
     seq_score = token_score.reshape(-1, SEQ_LEN).sum(axis=1)
     partner = from_partner(seq_score, "dp", lax.axis_size("dp").bit_length() - 2)

time: 110 us -> 98.5 us (0.90); the launches traced: 108 us -> 98.2 us
  Pallas kernels: 69 us -> 59.5 us
    pallas_call x2, Pallas kernels: 69 us -> 59.5 us  [the longest x1 32.1 us: gather_blocks(): pl.pallas_call(functools.partial(dispatch_kernel, z_count, chunks), out_s...]
    unnamed x9 -> x7, local copies, waits for them, and re-layouts: 2.76 us -> 2.39 us
where the time goes in v4:
time: 98.5 us; the launch traced here: 98.2 us
  Pallas kernels  59.5 us (60%)
  matrix products  17.3 us (18%)
  other arithmetic  8.99 us (9%)
  local copies, waits for them, and re-layouts  6.48 us (7%)
  starting transfers between devices  3.27 us (3%)
  waiting for transfers between devices  1.86 us (2%)
    pallas_call x1, Pallas kernels, gather_blocks(): pl.pallas_call(functools.partial(dispatch_kernel, z_count, chunks), out_s...  32.1 us
    pallas_call x1, Pallas kernels, scatter_sums(): pl.pallas_call(functools.partial(combine_kernel, z_count, chunks), out_sh...  27.4 us
    dot_general x1, matrix products, body(): jnp.einsum('nemf,efd->nemd', hidden, w_down, preferred_element_type=jnp.f...  9.16 us
    dot_general x1, matrix products, body(): jnp.einsum('sqt,std->sqd', picker, inputs_all, preferred_element_type=jnp...  3.3 us
    ppermute x1, starting transfers between devices, from_partner(): return lax.ppermute(block, axis, route)  3.27 us
    dot_general x1, matrix products, body(): jnp.einsum('nemd,edf->nemf', row_block, w_gate, preferred_element_type=jn...  2.96 us
    unnamed x7, local copies, waits for them, and re-layouts  2.39 us
    convert_element_type x1, local copies, waits for them, and re-layouts, body(): result = (slot_weight[..., None] * down_out).astype(jnp.bfloat16)  2.29 us
  transfers between devices with their start and end apart: 1, of which 1 were waited for; matrix products, arithmetic and copies ran while one was open for 0% of the time, Pallas kernels for 0%

profile of v4, /device:TPU:2, one launch (start us, length us, event | category | flops | bytes accessed | tf_op | source)
XLA Modules:
  0.0 98.2 jit_solution(7287936290026566830)
XLA Ops:
  0.6 0.7 convert.13
  1.3 0.8 copy.38
  2.1 0.7 broadcast_compare_fusion
  2.9 0.8 slice_reduce_fusion.1
  3.9 0.8 copy.39
  5.3 1.1 %add_convert_fusion = bf16[64,2048]{1,0:T(8,128)(2,1)S(1)} fusion(bf16[64,2048]{1,0:T(8,128)(2,1)} %param.9, pred[64]{0:T(512)(128)(4,1)S(1)} %eq.47, bf16[2048]{0:T(1024)(128)(2,1)S(1)} %get-tuple-element.3, bf16[2048]{0:T(1024)(128)(2,1)S(1)} %get-tuple-element.2), kind=kLoop, calls=%fused_computation.35 | loop fusion | flops 655360 | bytes 532544 | tf_op jit(solution)/shard_map/convert_element_type | solution.py:271
  6.3 0.7 pad_maximum_fusion.blk_ref
  7.1 32.1 %shard_map.104 = bf16[16,64,2176]{2,1,0:T(8,128)(2,1)} custom-call(bf16[64,2176]{1,0:T(8,128)(2,1)} %pad_maximum_fusion.blk_ref), custom_call_target="tpu_custom_call" | custom-call | tf_op jit(solution)/shard_map/pallas_call | solution.py:116
  39.2 1.0 %slice_convert_fusion = s32[16,64,32]{2,1,0:T(8,128)S(1)} fusion(bf16[16,64,2176]{2,1,0:T(8,128)(2,1)} %shard_map.104), kind=kLoop, calls=%fused_computation.38 | loop fusion | flops 32768 | bytes 196608 | tf_op jit(solution)/shard_map/convert_element_type | solution.py:280
  40.2 0.5 fusion.33
  40.7 0.5 broadcast_divide_fusion
  41.8 1.2 %fusion.14 = pred[16,48,64]{2,1,0:T(8,128)(4,1)S(1)} fusion(s32[16,64,8]{1,2,0:T(8,128)S(1)} %copy.44), kind=kLoop, calls=%fused_computation.14 | loop fusion | flops 737280 | bytes 81920 | tf_op jit(solution)/shard_map/reduce_or | solution.py:295
  43.0 1.7 %select_reduce_fusion = f32[16,48]{1,0:T(8,128)S(1)} fusion(f32[16,64,8]{1,2,0:T(8,128)S(1)} %copy.46, s32[16,64,8]{1,2,0:T(8,128)S(1)} %copy.44), kind=kLoop, calls=%fused_computation.12 | loop fusion | flops 1178880 | bytes 68608 | tf_op jit(solution)/shard_map/reduce_sum | solution.py:296
  44.7 3.3 %fusion.11 = bf16[16,48,2048]{2,1,0:T(8,128)(2,1)S(1)} fusion(pred[16,48,64]{2,1,0:T(8,128)(4,1)S(1)} %fusion.14, bf16[16,64,2176]{2,1,0:T(8,128)(2,1)} %shard_map.104), kind=kOutput, calls=%fused_computation.11 | convolution fusion | flops 202899456 | bytes 7389184 | tf_op jit(solution)/shard_map/sqt,std->sqd/dot_general | solution.py:299
  48.2 3.0 %fusion.5 = f32[2,16,24,512]{3,2,1,0:T(8,128)} fusion(bf16[2,2048,512]{2,1,0:T(8,128)(2,1)S(1)} %copy-done.1, bf16[16,2,24,2048]{3,2,1,0:T(8,128)(2,1)S(1)} %bitcast.60), kind=kOutput, calls=%fused_computation.6 | convolution fusion | flops 1610612736 | bytes 8912896 | tf_op jit(solution)/shard_map/nemd,edf->nemf/dot_general | solution.py:303
  51.1 9.2 %fusion = bf16[16,2,24,2048]{3,2,0,1:T(8,128)(2,1)} fusion(bf16[2,512,2048]{2,1,0:T(8,128)(2,1)} %param.16, f32[16,2,24]{2,0,1:T(8,128)S(1)} %copy.47, f32[2,16,24,512]{3,2,1,0:T(8,128)} %fusion.5, bf16[2,2048,512]{2,1,0:T(8,128)(2,1)} %param.15, bf16[16,2,24,2048]{3,2,1,0:T(8,128)(2,1)S(1)} %bitcast.61), kind=kOutput, calls=%fused_computation.1 | convolution fusion | flops 3226730496 | bytes 16256000 | tf_op jit(solution)/shard_map/nemf,efd->nemd/dot_general | solution.py:306
  60.3 2.3 %copy.50 = bf16[16,2,24,2048]{3,2,1,0:T(8,128)(2,1)S(1)} copy(bf16[16,2,24,2048]{3,2,0,1:T(8,128)(2,1)} %fusion) | data formatting | bytes 6291456 | tf_op jit(solution)/shard_map/convert_element_type | solution.py:307
  62.6 1.3 %convolution_convert_fusion = bf16[16,64,2048]{2,1,0:T(8,128)(2,1)S(1)} fusion(pred[16,48,64]{2,1,0:T(8,128)(4,1)S(1)} %fusion.14, bf16[16,48,2048]{2,1,0:T(8,128)(2,1)S(1)} %bitcast.59), kind=kOutput, calls=%fused_computation.10 | convolution fusion | flops 203423744 | bytes 7389184 | tf_op jit(solution)/shard_map/sqt,sqd->std/dot_general | solution.py:308
  63.9 27.4 %shard_map.105 = bf16[64,2048]{1,0:T(8,128)(2,1)S(1)} custom-call(bf16[2,8,64,2048]{3,2,1,0:T(8,128)(2,1)S(1)} %bitcast.58), custom_call_target="tpu_custom_call" | custom-call | tf_op jit(solution)/shard_map/pallas_call | solution.py:238
  91.3 0.3 convolution_bitcast_fusion
  91.8 3.3 %collective-permute-start = (f32[4]{0:T(128)S(1)}, f32[4]{0:T(128)S(1)}, u32[]{:S(2)}, u32[]{:S(2)}) collective-permute-start(f32[4]{0:T(128)S(1)} %reduce_sum.39), channel_id=1, source_target_pairs={{0,128},{128,0},{16,144},{144,16},{32,160},{160,32},{48,176},{176,... | collective-permute-start | bytes 56 | tf_op jit(solution)/shard_map/ppermute | solution.py:22
  95.1 1.9 %collective-permute-done = f32[4]{0:T(128)S(1)} collective-permute-done((f32[4]{0:T(128)S(1)}, f32[4]{0:T(128)S(1)}, u32[]{:S(2)}, u32[]{:S(2)}) %collective-permute-start) | collective-permute-done | bytes 48 | tf_op jit(solution)/shard_map/ppermute | solution.py:22
  97.0 0.5 multiply_add_fusion
  97.5 0.7 copy.63
  (20 shorter events, 1.9 us)
Async XLA Ops:
  0.6 90.7 %copy-start = (f32[2048]{0:T(1024)S(1)}, f32[2048]{0:T(1024)}, u32[]{:S(2)}) copy-start(f32[2048]{0:T(1024)} %param.17) | copy-start | bytes 24580
  44.7 3.5 %copy-start.1 = (bf16[2,2048,512]{2,1,0:T(8,128)(2,1)S(1)}, bf16[2,2048,512]{2,1,0:T(8,128)(2,1)}, u32[]{:S(2)}) copy-start(bf16[2,2048,512]{2,1,0:T(8,128)(2,1)} %param.14) | copy-start | bytes 12582916
  91.8 5.1 %collective-permute-start = (f32[4]{0:T(128)S(1)}, f32[4]{0:T(128)S(1)}, u32[]{:S(2)}, u32[]{:S(2)}) collective-permute-start(f32[4]{0:T(128)S(1)} %reduce_sum.39), channel_id=1, source_target_pairs={{0,128},{128,0},{16,144},{144,16},{32,160},{160,32},{48,176},{176,... | collective-permute-start | bytes 56 | tf_op jit(solution)/shard_map/ppermute | solution.py:22

commit v5 on v4

--- a/solution.py
+++ b/solution.py
@@ -275,7 +275,7 @@
     ).astype(jnp.bfloat16)
     routes = jnp.pad(routes, ((0, 0), (0, 128 - 4 * top_count)))
     block = jnp.concatenate([inputs, routes], axis=1)
-    gathered = gather_blocks(block, z_count, 2)
+    gathered = gather_blocks(block, z_count, 4)
     inputs_all = gathered[:, :, :model_width]
     routes_all = gathered[:, :, model_width : model_width + 4 * top_count].astype(jnp.int32)
     ids_cube = routes_all[..., :top_count]
@@ -312,7 +312,7 @@
         preferred_element_type=jnp.float32,
     )
     partial_value = partial_value.reshape(c_count, z_count, tok_rows, model_width)
-    mixed = scatter_sums(partial_value.astype(jnp.bfloat16), 2)
+    mixed = scatter_sums(partial_value.astype(jnp.bfloat16), 4)
     token_score = jnp.dot(mixed.astype(jnp.float32), score_head, precision=lax.Precision.HIGHEST)
     seq_score = token_score.reshape(-1, SEQ_LEN).sum(axis=1)
     partner = from_partner(seq_score, "dp", lax.axis_size("dp").bit_length() - 2)

time: 98.5 us -> 98.6 us (level)
  no operation moved by 1% of the time
where the time goes in v5:
time: 98.6 us; the launch traced here: 98.2 us
  Pallas kernels  59.5 us (60%)
  matrix products  17.3 us (18%)
  other arithmetic  8.99 us (9%)
  local copies, waits for them, and re-layouts  6.48 us (7%)
  starting transfers between devices  3.28 us (3%)
  waiting for transfers between devices  1.85 us (2%)
    pallas_call x1, Pallas kernels, gather_blocks(): pl.pallas_call(functools.partial(dispatch_kernel, z_count, chunks), out_s...  33 us
    pallas_call x1, Pallas kernels, scatter_sums(): pl.pallas_call(functools.partial(combine_kernel, z_count, chunks), out_sh...  26.5 us
    dot_general x1, matrix products, body(): jnp.einsum('nemf,efd->nemd', hidden, w_down, preferred_element_type=jnp.f...  9.16 us
    dot_general x1, matrix products, body(): jnp.einsum('sqt,std->sqd', picker, inputs_all, preferred_element_type=jnp...  3.3 us
    ppermute x1, starting transfers between devices, from_partner(): return lax.ppermute(block, axis, route)  3.28 us
    dot_general x1, matrix products, body(): jnp.einsum('nemd,edf->nemf', row_block, w_gate, preferred_element_type=jn...  2.96 us
    unnamed x7, local copies, waits for them, and re-layouts  2.4 us
    convert_element_type x1, local copies, waits for them, and re-layouts, body(): result = (slot_weight[..., None] * down_out).astype(jnp.bfloat16)  2.29 us
  transfers between devices with their start and end apart: 1, of which 1 were waited for; matrix products, arithmetic and copies ran while one was open for 0% of the time, Pallas kernels for 0%

profile of v5, /device:TPU:2, one launch (start us, length us, event | category | flops | bytes accessed | tf_op | source)
XLA Modules:
  0.0 98.2 jit_solution(10754153311407841327)
XLA Ops:
  0.6 0.7 convert.13
  1.3 0.8 copy.38
  2.1 0.7 broadcast_compare_fusion
  2.9 0.8 slice_reduce_fusion.1
  3.9 0.8 copy.39
  5.3 1.1 %add_convert_fusion = bf16[64,2048]{1,0:T(8,128)(2,1)S(1)} fusion(bf16[64,2048]{1,0:T(8,128)(2,1)} %param.9, pred[64]{0:T(512)(128)(4,1)S(1)} %eq.47, bf16[2048]{0:T(1024)(128)(2,1)S(1)} %get-tuple-element.3, bf16[2048]{0:T(1024)(128)(2,1)S(1)} %get-tuple-element.2), kind=kLoop, calls=%fused_computation.35 | loop fusion | flops 655360 | bytes 532544 | tf_op jit(solution)/shard_map/convert_element_type | solution.py:271
  6.3 0.7 pad_maximum_fusion.blk_ref
  7.1 33.0 %shard_map.104 = bf16[16,64,2176]{2,1,0:T(8,128)(2,1)} custom-call(bf16[64,2176]{1,0:T(8,128)(2,1)} %pad_maximum_fusion.blk_ref), custom_call_target="tpu_custom_call" | custom-call | tf_op jit(solution)/shard_map/pallas_call | solution.py:116
  40.1 1.0 %slice_convert_fusion = s32[16,64,32]{2,1,0:T(8,128)S(1)} fusion(bf16[16,64,2176]{2,1,0:T(8,128)(2,1)} %shard_map.104), kind=kLoop, calls=%fused_computation.38 | loop fusion | flops 32768 | bytes 196608 | tf_op jit(solution)/shard_map/convert_element_type | solution.py:280
  41.1 0.5 fusion.33
  41.6 0.5 broadcast_divide_fusion
  42.7 1.2 %fusion.14 = pred[16,48,64]{2,1,0:T(8,128)(4,1)S(1)} fusion(s32[16,64,8]{1,2,0:T(8,128)S(1)} %copy.44), kind=kLoop, calls=%fused_computation.14 | loop fusion | flops 737280 | bytes 81920 | tf_op jit(solution)/shard_map/reduce_or | solution.py:295
  43.9 1.7 %select_reduce_fusion = f32[16,48]{1,0:T(8,128)S(1)} fusion(f32[16,64,8]{1,2,0:T(8,128)S(1)} %copy.46, s32[16,64,8]{1,2,0:T(8,128)S(1)} %copy.44), kind=kLoop, calls=%fused_computation.12 | loop fusion | flops 1178880 | bytes 68608 | tf_op jit(solution)/shard_map/reduce_sum | solution.py:296
  45.6 3.3 %fusion.11 = bf16[16,48,2048]{2,1,0:T(8,128)(2,1)S(1)} fusion(pred[16,48,64]{2,1,0:T(8,128)(4,1)S(1)} %fusion.14, bf16[16,64,2176]{2,1,0:T(8,128)(2,1)} %shard_map.104), kind=kOutput, calls=%fused_computation.11 | convolution fusion | flops 202899456 | bytes 7389184 | tf_op jit(solution)/shard_map/sqt,std->sqd/dot_general | solution.py:299
  49.1 3.0 %fusion.5 = f32[2,16,24,512]{3,2,1,0:T(8,128)} fusion(bf16[2,2048,512]{2,1,0:T(8,128)(2,1)S(1)} %copy-done.1, bf16[16,2,24,2048]{3,2,1,0:T(8,128)(2,1)S(1)} %bitcast.60), kind=kOutput, calls=%fused_computation.6 | convolution fusion | flops 1610612736 | bytes 8912896 | tf_op jit(solution)/shard_map/nemd,edf->nemf/dot_general | solution.py:303
  52.0 9.2 %fusion = bf16[16,2,24,2048]{3,2,0,1:T(8,128)(2,1)} fusion(bf16[2,512,2048]{2,1,0:T(8,128)(2,1)} %param.16, f32[16,2,24]{2,0,1:T(8,128)S(1)} %copy.47, f32[2,16,24,512]{3,2,1,0:T(8,128)} %fusion.5, bf16[2,2048,512]{2,1,0:T(8,128)(2,1)} %param.15, bf16[16,2,24,2048]{3,2,1,0:T(8,128)(2,1)S(1)} %bitcast.61), kind=kOutput, calls=%fused_computation.1 | convolution fusion | flops 3226730496 | bytes 16256000 | tf_op jit(solution)/shard_map/nemf,efd->nemd/dot_general | solution.py:306
  61.2 2.3 %copy.50 = bf16[16,2,24,2048]{3,2,1,0:T(8,128)(2,1)S(1)} copy(bf16[16,2,24,2048]{3,2,0,1:T(8,128)(2,1)} %fusion) | data formatting | bytes 6291456 | tf_op jit(solution)/shard_map/convert_element_type | solution.py:307
  63.5 1.3 %convolution_convert_fusion = bf16[16,64,2048]{2,1,0:T(8,128)(2,1)S(1)} fusion(pred[16,48,64]{2,1,0:T(8,128)(4,1)S(1)} %fusion.14, bf16[16,48,2048]{2,1,0:T(8,128)(2,1)S(1)} %bitcast.59), kind=kOutput, calls=%fused_computation.10 | convolution fusion | flops 203423744 | bytes 7389184 | tf_op jit(solution)/shard_map/sqt,sqd->std/dot_general | solution.py:308
  64.8 26.5 %shard_map.105 = bf16[64,2048]{1,0:T(8,128)(2,1)S(1)} custom-call(bf16[2,8,64,2048]{3,2,1,0:T(8,128)(2,1)S(1)} %bitcast.58), custom_call_target="tpu_custom_call" | custom-call | tf_op jit(solution)/shard_map/pallas_call | solution.py:238
  91.3 0.3 convolution_bitcast_fusion
  91.9 3.3 %collective-permute-start = (f32[4]{0:T(128)S(1)}, f32[4]{0:T(128)S(1)}, u32[]{:S(2)}, u32[]{:S(2)}) collective-permute-start(f32[4]{0:T(128)S(1)} %reduce_sum.39), channel_id=1, source_target_pairs={{0,128},{128,0},{16,144},{144,16},{32,160},{160,32},{48,176},{176,... | collective-permute-start | bytes 56 | tf_op jit(solution)/shard_map/ppermute | solution.py:22
  95.2 1.8 %collective-permute-done = f32[4]{0:T(128)S(1)} collective-permute-done((f32[4]{0:T(128)S(1)}, f32[4]{0:T(128)S(1)}, u32[]{:S(2)}, u32[]{:S(2)}) %collective-permute-start) | collective-permute-done | bytes 48 | tf_op jit(solution)/shard_map/ppermute | solution.py:22
  97.0 0.5 multiply_add_fusion
  97.5 0.7 copy.63
  (20 shorter events, 1.9 us)
Async XLA Ops:
  0.6 90.7 %copy-start = (f32[2048]{0:T(1024)S(1)}, f32[2048]{0:T(1024)}, u32[]{:S(2)}) copy-start(f32[2048]{0:T(1024)} %param.17) | copy-start | bytes 24580
  45.6 3.5 %copy-start.1 = (bf16[2,2048,512]{2,1,0:T(8,128)(2,1)S(1)}, bf16[2,2048,512]{2,1,0:T(8,128)(2,1)}, u32[]{:S(2)}) copy-start(bf16[2,2048,512]{2,1,0:T(8,128)(2,1)} %param.14) | copy-start | bytes 12582916
  91.9 5.1 %collective-permute-start = (f32[4]{0:T(128)S(1)}, f32[4]{0:T(128)S(1)}, u32[]{:S(2)}, u32[]{:S(2)}) collective-permute-start(f32[4]{0:T(128)S(1)} %reduce_sum.39), channel_id=1, source_target_pairs={{0,128},{128,0},{16,144},{144,16},{32,160},{160,32},{48,176},{176,... | collective-permute-start | bytes 56 | tf_op jit(solution)/shard_map/ppermute | solution.py:22

commit v6 on v5

--- a/solution.py
+++ b/solution.py
@@ -128,25 +128,23 @@
 
 
 def combine_kernel(
-    z_count, chunks, part_ref, out_ref, pair_buf, fwd_buf, bwd_buf, fwd_out, bwd_out,
-    send_sem, recv_sem,
+    z_count, chunks, part_ref, out_ref, fwd_buf, bwd_buf, fwd_out, bwd_out, send_sem, recv_sem
 ):
     z = lax.axis_index("z")
     c = lax.axis_index("c")
     row = lax.axis_index("dp")
-    other = 1 - c
     step = 1 - 2 * c
     fwd = lax.rem(z + step + z_count, z_count)
     bwd = lax.rem(z - step + z_count, z_count)
-    fwd_id, bwd_id, pair_id = (row, fwd, c), (row, bwd, c), (row, z, other)
+    fwd_id, bwd_id = (row, fwd, c), (row, bwd, c)
     fwd_hops = z_count // 2
     bwd_hops = z_count - 1 - fwd_hops
-    piece = part_ref.shape[2] // chunks
+    piece = part_ref.shape[1] // chunks
 
     barrier = pltpu.get_barrier_semaphore()
-    for target in (fwd_id, bwd_id, pair_id):
+    for target in (fwd_id, bwd_id):
         pl.semaphore_signal(barrier, 1, device_id=target, device_id_type=MESH)
-    pl.semaphore_wait(barrier, 3)
+    pl.semaphore_wait(barrier, 2)
 
     sends = []
 
@@ -168,46 +166,29 @@
             dst_ref=dst,
             send_sem=send_sem.at[0],
             recv_sem=recv_sem.at[sem],
-            device_id=pair_id,
+            device_id=fwd_id,
             device_id_type=MESH,
         ).wait_recv()
 
-    def order(ring_step):
-        dests = []
-        for hop in range(1, fwd_hops + 1):
-            dests.append(lax.rem(z + ring_step * (fwd_hops + 1 - hop) + 2 * z_count, z_count))
-            if hop <= bwd_hops:
-                dests.append(lax.rem(z - ring_step * (bwd_hops + 1 - hop) + 2 * z_count, z_count))
-        return dests + [z]
-
-    for n, dest in enumerate(order(-step)):
-        send(part_ref.at[other, dest], pair_buf.at[n], n, pair_id)
-    def own(dest, n, k):
-        if k == 0:
-            arrive(pair_buf.at[n], n)
-        rows = pl.ds(k * piece, piece)
-        return part_ref[c, dest, rows].astype(jnp.float32) + pair_buf[n, rows].astype(
-            jnp.float32
-        )
-
-    fwd_sem = z_count
-    bwd_sem = z_count + fwd_hops * chunks
+    def own(dest, rows):
+        return part_ref[dest, rows].astype(jnp.float32)
+
+    bwd_sem = fwd_hops * chunks
     for hop in range(1, fwd_hops + 1):
         for k in range(chunks):
             rows = pl.ds(k * piece, piece)
             dest = lax.rem(z + step * (fwd_hops + 1 - hop) + 2 * z_count, z_count)
-            n = hop - 1 + min(hop - 1, bwd_hops)
-            total = own(dest, n, k)
+            total = own(dest, rows)
             if hop > 1:
-                sem = fwd_sem + (hop - 2) * chunks + k
+                sem = (hop - 2) * chunks + k
                 arrive(fwd_buf.at[hop - 2, rows], sem)
                 total = total + fwd_buf[hop - 2, rows].astype(jnp.float32)
             fwd_out[hop - 1, rows] = total.astype(fwd_out.dtype)
-            sem = fwd_sem + (hop - 1) * chunks + k
+            sem = (hop - 1) * chunks + k
             send(fwd_out.at[hop - 1, rows], fwd_buf.at[hop - 1, rows], sem, fwd_id)
             if hop <= bwd_hops:
                 dest = lax.rem(z - step * (bwd_hops + 1 - hop) + 2 * z_count, z_count)
-                total = own(dest, n + 1, k)
+                total = own(dest, rows)
                 if hop > 1:
                     sem = bwd_sem + (hop - 2) * chunks + k
                     arrive(bwd_buf.at[hop - 2, rows], sem)
@@ -217,8 +198,8 @@
                 send(bwd_out.at[hop - 1, rows], bwd_buf.at[hop - 1, rows], sem, bwd_id)
     for k in range(chunks):
         rows = pl.ds(k * piece, piece)
-        total = own(z, fwd_hops + bwd_hops, k)
-        arrive(fwd_buf.at[fwd_hops - 1, rows], fwd_sem + (fwd_hops - 1) * chunks + k)
+        total = own(z, rows)
+        arrive(fwd_buf.at[fwd_hops - 1, rows], (fwd_hops - 1) * chunks + k)
         total = total + fwd_buf[fwd_hops - 1, rows].astype(jnp.float32)
         if bwd_hops > 0:
             arrive(bwd_buf.at[bwd_hops - 1, rows], bwd_sem + (bwd_hops - 1) * chunks + k)
@@ -229,19 +210,18 @@
 
 
 def scatter_sums(partial, chunks):
-    c_count, z_count, rows, width = partial.shape
+    z_count, rows, width = partial.shape
     fwd_hops = z_count // 2
     bwd_hops = max(z_count - 1 - fwd_hops, 1)
     block = (rows, width)
     vmem = pl.BlockSpec(memory_space=pltpu.VMEM)
-    sems = z_count + (fwd_hops + bwd_hops) * chunks
+    sems = (fwd_hops + bwd_hops) * chunks
     return pl.pallas_call(
         functools.partial(combine_kernel, z_count, chunks),
         out_shape=jax.ShapeDtypeStruct(block, partial.dtype),
         in_specs=[vmem],
         out_specs=vmem,
         scratch_shapes=[
-            pltpu.VMEM((z_count,) + block, partial.dtype),
             pltpu.VMEM((fwd_hops,) + block, partial.dtype),
             pltpu.VMEM((bwd_hops,) + block, partial.dtype),
             pltpu.VMEM((fwd_hops,) + block, partial.dtype),
@@ -253,6 +233,37 @@
             collective_id=1, has_side_effects=True, vmem_limit_bytes=48 * 1024 * 1024
         ),
     )(partial)
+
+
+def expert_partials(inputs_all, ids_cube, rank_cube, weight_cube, my_index, w_gate, w_up, w_down):
+    source_count, tok_rows, model_width = inputs_all.shape
+    per_device = w_gate.shape[0]
+    local_count = per_device * MOST
+    local_slot = ids_cube - my_index * per_device
+    is_mine = (local_slot >= 0) & (local_slot < per_device)
+    local_key = jnp.where(is_mine, local_slot * MOST + rank_cube, -1)
+    match = (
+        local_key[:, None, :, :] == jnp.arange(local_count, dtype=jnp.int32)[None, :, None, None]
+    )
+    picker = jnp.any(match, axis=3).astype(jnp.bfloat16)
+    slot_weight = jnp.sum(jnp.where(match, weight_cube[:, None, :, :], 0.0), axis=(2, 3)).reshape(
+        source_count, per_device, MOST
+    )
+    row_block = jnp.einsum(
+        "sqt,std->sqd", picker, inputs_all, preferred_element_type=jnp.float32
+    ).astype(jnp.bfloat16)
+    row_block = row_block.reshape(source_count, per_device, MOST, model_width)
+    gate_proj = jnp.einsum("nemd,edf->nemf", row_block, w_gate, preferred_element_type=jnp.float32)
+    up_proj = jnp.einsum("nemd,edf->nemf", row_block, w_up, preferred_element_type=jnp.float32)
+    hidden = (jax.nn.silu(gate_proj) * up_proj).astype(jnp.bfloat16)
+    down_out = jnp.einsum("nemf,efd->nemd", hidden, w_down, preferred_element_type=jnp.float32)
+    result = (slot_weight[..., None] * down_out).astype(jnp.bfloat16)
+    return jnp.einsum(
+        "sqt,sqd->std",
+        picker,
+        result.reshape(source_count, local_count, model_width),
+        preferred_element_type=jnp.float32,
+    )
 
 
 def body(
@@ -285,34 +296,29 @@
     ).astype(jnp.float32)
     weight_cube = fixed_val / jnp.sum(fixed_val, axis=2, keepdims=True)
     my_index = lax.axis_index("z") * c_count + lax.axis_index("c")
-    local_count = per_device * MOST
-    local_slot = ids_cube - my_index * per_device
-    is_mine = (local_slot >= 0) & (local_slot < per_device)
-    local_key = jnp.where(is_mine, local_slot * MOST + rank_cube, -1)
-    match = (
-        local_key[:, None, :, :] == jnp.arange(local_count, dtype=jnp.int32)[None, :, None, None]
-    )
-    picker = jnp.any(match, axis=3).astype(jnp.bfloat16)
-    slot_weight = jnp.sum(jnp.where(match, weight_cube[:, None, :, :], 0.0), axis=(2, 3)).reshape(
-        expert_count, per_device, MOST
-    )
-    row_block = jnp.einsum(
-        "sqt,std->sqd", picker, inputs_all, preferred_element_type=jnp.float32
-    ).astype(jnp.bfloat16)
-    row_block = row_block.reshape(expert_count, per_device, MOST, model_width)
-    gate_proj = jnp.einsum("nemd,edf->nemf", row_block, w_gate, preferred_element_type=jnp.float32)
-    up_proj = jnp.einsum("nemd,edf->nemf", row_block, w_up, preferred_element_type=jnp.float32)
-    hidden = (jax.nn.silu(gate_proj) * up_proj).astype(jnp.bfloat16)
-    down_out = jnp.einsum("nemf,efd->nemd", hidden, w_down, preferred_element_type=jnp.float32)
-    result = (slot_weight[..., None] * down_out).astype(jnp.bfloat16)
-    partial_value = jnp.einsum(
-        "sqt,sqd->std",
-        picker,
-        result.reshape(expert_count, local_count, model_width),
-        preferred_element_type=jnp.float32,
-    )
-    partial_value = partial_value.reshape(c_count, z_count, tok_rows, model_width)
-    mixed = scatter_sums(partial_value.astype(jnp.bfloat16), 4)
+    c = lax.axis_index("c")
+
+    def ring(cube, which):
+        shaped = cube.reshape((c_count, z_count) + cube.shape[1:])
+        return lax.dynamic_index_in_dim(shaped, which, axis=0, keepdims=False)
+
+    def partials(which):
+        return expert_partials(
+            ring(inputs_all, which),
+            ring(ids_cube, which),
+            ring(rank_cube, which),
+            ring(weight_cube, which),
+            my_index,
+            w_gate,
+            w_up,
+            w_down,
+        )
+
+    for_partner = partials(1 - c).astype(jnp.bfloat16)
+    from_partner_core = lax.ppermute(for_partner, "c", [(0, 1), (1, 0)])
+    own_ring = partials(c)
+    chip_sum = (own_ring + from_partner_core.astype(jnp.float32)).astype(jnp.bfloat16)
+    mixed = scatter_sums(chip_sum, 4)
     token_score = jnp.dot(mixed.astype(jnp.float32), score_head, precision=lax.Precision.HIGHEST)
     seq_score = token_score.reshape(-1, SEQ_LEN).sum(axis=1)
     partner = from_partner(seq_score, "dp", lax.axis_size("dp").bit_length() - 2)

time: 98.6 us -> 116 us (1.18)
  matrix products: 17.3 us -> 27.9 us
  local copies, waits for them, and re-layouts: 6.48 us -> 12 us
  other arithmetic: 8.99 us -> 11.5 us
  Pallas kernels: 59.5 us -> 57.2 us
    dot_general x4 -> x8, matrix products: 16.7 us -> 27.3 us  [the longest x2 12.6 us: expert_partials(): jnp.einsum('nemf,efd->nemd', hidden, w_down, preferred_element_type=jnp.f...]
    slice x0 -> x2, local copies, waits for them, and re-layouts: none -> 4.95 us  [the longest x1 4.74 us: body(): inputs_all = gathered[:, :, :model_width]]
    div x1, other arithmetic: 0.47 us -> 2.95 us  [body(): weight_cube = fixed_val / jnp.sum(fixed_val, axis=2, keepdims=True)]
    pallas_call x1, Pallas kernels: 26.5 us -> 24.2 us  [scatter_sums(): pl.pallas_call(functools.partial(combine_kernel, z_count, chunks), out_sh...]
    unnamed x7 -> x11, local copies, waits for them, and re-layouts: 2.4 us -> 3.62 us
  transfers between devices with their start and end apart: 1 -> 2, of which waited for: 1 -> 1; matrix products, arithmetic and copies ran while one was open for 0% -> 13% of each run, Pallas kernels for 0% -> 0%
where the time goes in v6:
time: 116 us; the launch traced here: 115 us
  Pallas kernels  57.2 us (49%)
  matrix products  27.9 us (24%)
  local copies, waits for them, and re-layouts  12 us (10%)
  other arithmetic  11.5 us (10%)
  starting transfers between devices  4.02 us (3%)
  waiting for transfers between devices  1.85 us (2%)
    pallas_call x1, Pallas kernels, gather_blocks(): pl.pallas_call(functools.partial(dispatch_kernel, z_count, chunks), out_s...  33 us
    pallas_call x1, Pallas kernels, scatter_sums(): pl.pallas_call(functools.partial(combine_kernel, z_count, chunks), out_sh...  24.2 us
    dot_general x2, matrix products, expert_partials(): jnp.einsum('nemf,efd->nemd', hidden, w_down, preferred_element_type=jnp.f...  12.6 us
    dot_general x2, matrix products, expert_partials(): jnp.einsum('nemd,edf->nemf', row_block, w_gate, preferred_element_type=jn...  7.26 us
    slice x1, local copies, waits for them, and re-layouts, body(): inputs_all = gathered[:, :, :model_width]  4.74 us
    dot_general x2, matrix products, expert_partials(): jnp.einsum('sqt,std->sqd', picker, inputs_all, preferred_element_type=jnp...  4.29 us
    unnamed x11, local copies, waits for them, and re-layouts  3.62 us
    ppermute x1, starting transfers between devices, from_partner(): return lax.ppermute(block, axis, route)  3.28 us
  transfers between devices with their start and end apart: 2, of which 1 were waited for; matrix products, arithmetic and copies ran while one was open for 13% of the time, Pallas kernels for 0%

profile of v6, /device:TPU:2, one launch (start us, length us, event | category | flops | bytes accessed | tf_op | source)
XLA Modules:
  0.0 115.3 jit_solution(5434298104345576283)
XLA Ops:
  1.3 0.8 copy.46
  2.9 0.8 slice_reduce_fusion.1
  3.9 0.8 copy.47
  5.3 1.1 add_convert_fusion.1
  7.1 33.0 %shard_map.104 = bf16[16,64,2176]{2,1,0:T(8,128)(2,1)} custom-call(bf16[64,2176]{1,0:T(8,128)(2,1)} %pad_maximum_fusion.blk_ref), custom_call_target="tpu_custom_call" | custom-call | tf_op jit(solution)/shard_map/pallas_call | solution.py:116
  40.1 1.0 slice_convert_fusion
  41.1 4.7 %slice.31 = bf16[16,64,2048]{2,1,0:T(8,128)(2,1)} slice(bf16[16,64,2176]{2,1,0:T(8,128)(2,1)} %shard_map.104), slice={[0:16], [0:64], [0:2048]} | slice | bytes 8388608 | tf_op jit(solution)/shard_map/slice | solution.py:290
  45.8 2.9 %fusion.49 = f32[16,64,8]{2,1,0:T(8,128)S(1)} fusion(s32[16,64,32]{2,1,0:T(8,128)S(1)} %slice_convert_fusion), kind=kOutput, calls=%fused_computation.39 | output fusion | flops 33799 | bytes 1081344 | tf_op jit(solution)/shard_map/div | solution.py:297
  49.2 0.8 select_bitcast_fusion
  50.7 0.8 select_reduce_fusion
  51.6 2.1 %convolution_convert_fusion.1 = bf16[8,48,2048]{2,1,0:T(8,128)(2,1)S(1)} fusion(pred[8,48,64]{2,1,0:T(8,128)(4,1)S(1)} %fusion.23, bf16[2,8,64,2048]{3,2,1,0:T(8,128)(2,1)} %bitcast.105, s32[]{:T(128)S(6)} %select_n.71), kind=kOutput, calls=%fused_computation.19 | convolution fusion | flops 101449728 | bytes 3694596 | tf_op jit(solution)/shard_map/sqt,std->sqd/dot_general | solution.py:252
  53.7 4.1 %fusion.34 = f32[8,2,24,512]{3,2,0,1:T(8,128)} fusion(bf16[2,2048,512]{2,1,0:T(8,128)(2,1)} %param.14, bf16[8,2,24,2048]{3,2,1,0:T(8,128)(2,1)S(1)} %bitcast.113), kind=kOutput, calls=%fused_computation.36 | convolution fusion | flops 805306368 | bytes 6553600 | tf_op jit(solution)/shard_map/nemd,edf->nemf/dot_general | solution.py:256
  57.8 5.6 %fusion.13 = bf16[8,2,24,2048]{3,2,0,1:T(8,128)(2,1)S(1)} fusion(bf16[2,512,2048]{2,1,0:T(8,128)(2,1)} %param.16, f32[8,2,24]{2,0,1:T(8,128)S(1)} %copy.60, bf16[2,2048,512]{2,1,0:T(8,128)(2,1)} %param.15, bf16[8,2,24,2048]{3,2,1,0:T(8,128)(2,1)S(1)} %bitcast.114, f32[8,2,24,512]{3,2,0,1:T(8,128)} %fusion.34), kind=kOutput, calls=%fused_computation.15 | convolution fusion | flops 1613365248 | bytes 12322304 | tf_op jit(solution)/shard_map/nemf,efd->nemd/dot_general | solution.py:259
  63.6 0.8 convolution_convert_fusion
  65.3 0.8 select_reduce_fusion.1
  66.8 2.1 %convolution_convert_fusion.2 = bf16[8,48,2048]{2,1,0:T(8,128)(2,1)S(1)} fusion(pred[8,48,64]{2,1,0:T(8,128)(4,1)S(1)} %fusion.24, bf16[2,8,64,2048]{3,2,1,0:T(8,128)(2,1)} %bitcast.106, s32[]{:T(128)S(6)} %select_n.67), kind=kOutput, calls=%fused_computation.20 | convolution fusion | flops 101449728 | bytes 3694596 | tf_op jit(solution)/shard_map/sqt,std->sqd/dot_general | solution.py:252
  69.0 1.1 copy-done.1
  70.1 3.2 %fusion.29 = f32[8,2,24,512]{3,2,0,1:T(8,128)S(1)} fusion(bf16[2,2048,512]{2,1,0:T(8,128)(2,1)} %param.14, bf16[8,2,24,2048]{3,2,1,0:T(8,128)(2,1)S(1)} %bitcast.111), kind=kOutput, calls=%fused_computation.35 | convolution fusion | flops 805306368 | bytes 6553600 | tf_op jit(solution)/shard_map/nemd,edf->nemf/dot_general | solution.py:256
  73.3 7.0 %fusion.14 = bf16[8,2,24,2048]{3,2,0,1:T(8,128)(2,1)} fusion(bf16[2,512,2048]{2,1,0:T(8,128)(2,1)} %param.16, f32[8,2,24]{2,0,1:T(8,128)S(1)} %copy.54, bf16[2,2048,512]{2,1,0:T(8,128)(2,1)} %param.15, bf16[8,2,24,2048]{3,2,1,0:T(8,128)(2,1)} %bitcast.112, f32[8,2,24,512]{3,2,0,1:T(8,128)S(1)} %fusion.29), kind=kOutput, calls=%fused_computation.17 | convolution fusion | flops 1613365248 | bytes 12322304 | tf_op jit(solution)/shard_map/nemf,efd->nemd/dot_general | solution.py:259
  80.3 1.5 %copy.57 = bf16[8,2,24,2048]{3,2,1,0:T(8,128)(2,1)S(1)} copy(bf16[8,2,24,2048]{3,2,0,1:T(8,128)(2,1)} %fusion.14) | data formatting | bytes 3145728 | tf_op jit(solution)/shard_map/convert_element_type | solution.py:260
  81.8 2.3 %add_convert_fusion.part_ref = bf16[8,64,2048]{2,1,0:T(8,128)(2,1)S(1)} fusion(bf16[8,64,2048]{2,1,0:T(8,128)(2,1)} %collective-permute-done, pred[8,48,64]{2,1,0:T(8,128)(4,1)S(1)} %fusion.24, bf16[8,48,2048]{2,1,0:T(8,128)(2,1)S(1)} %bitcast.108), kind=kOutput, calls=%fused_computation.13 | convolution fusion | flops 103809024 | bytes 5791744 | tf_op jit(solution)/shard_map/sqt,sqd->std/dot_general | solution.py:261
  84.2 24.2 %shard_map.105 = bf16[64,2048]{1,0:T(8,128)(2,1)S(1)} custom-call(bf16[8,64,2048]{2,1,0:T(8,128)(2,1)S(1)} %add_convert_fusion.part_ref), custom_call_target="tpu_custom_call" | custom-call | tf_op jit(solution)/shard_map/pallas_call | solution.py:219
  109.0 3.3 %collective-permute-start.1 = (f32[4]{0:T(128)S(1)}, f32[4]{0:T(128)S(1)}, u32[]{:S(2)}, u32[]{:S(2)}) collective-permute-start(f32[4]{0:T(128)S(1)} %reduce_sum.49), channel_id=1, source_target_pairs={{0,128},{128,0},{16,144},{144,16},{32,160},{160,32},{48,176},{176,... | collective-permute-start | bytes 56 | tf_op jit(solution)/shard_map/ppermute | solution.py:22
  112.3 1.8 %collective-permute-done.1 = f32[4]{0:T(128)S(1)} collective-permute-done((f32[4]{0:T(128)S(1)}, f32[4]{0:T(128)S(1)}, u32[]{:S(2)}, u32[]{:S(2)}) %collective-permute-start.1) | collective-permute-done | bytes 48 | tf_op jit(solution)/shard_map/ppermute | solution.py:22
  (37 shorter events, 7.6 us)
Async XLA Ops:
  0.6 107.8 %copy-start = (f32[2048]{0:T(1024)S(1)}, f32[2048]{0:T(1024)}, u32[]{:S(2)}) copy-start(f32[2048]{0:T(1024)} %param.17) | copy-start | bytes 24580
  63.6 1.6 %copy-start.2 = (s32[8,64,8]{2,1,0:T(8,128)S(1)}, s32[8,64,8]{2,1,0:T(8,128)}, u32[]{:S(2)}) copy-start(s32[8,64,8]{2,1,0:T(8,128)} %get-tuple-element.5) | copy-start | bytes 49156
  64.4 17.5 %collective-permute-start = (bf16[8,64,2048]{2,1,0:T(8,128)(2,1)S(1)}, bf16[8,64,2048]{2,1,0:T(8,128)(2,1)}, u32[]{:S(2)}, u32[]{:S(2)}) collective-permute-start(bf16[8,64,2048]{2,1,0:T(8,128)(2,1)S(1)} %convolution_convert_fusion), channel_id=1, source_target_pairs={{0,1},{1,0},{2,3},{3,2},{4,5},{5,4},{6,7},{7,6},{8,9},{9,8},{10,11... | collective-permute-start | bytes 6291464 | tf_op jit(solution)/shard_map/ppermute | solution.py:318
  69.0 1.2 copy-start.1
  109.0 5.1 %collective-permute-start.1 = (f32[4]{0:T(128)S(1)}, f32[4]{0:T(128)S(1)}, u32[]{:S(2)}, u32[]{:S(2)}) collective-permute-start(f32[4]{0:T(128)S(1)} %reduce_sum.49), channel_id=1, source_target_pairs={{0,128},{128,0},{16,144},{144,16},{32,160},{160,32},{48,176},{176,... | collective-permute-start | bytes 56 | tf_op jit(solution)/shard_map/ppermute | solution.py:22

commit v7 on v4

--- a/solution.py
+++ b/solution.py
@@ -253,6 +253,37 @@
             collective_id=1, has_side_effects=True, vmem_limit_bytes=48 * 1024 * 1024
         ),
     )(partial)
+
+
+def ffn_kernel(x_ref, sw_ref, wg_ref, wu_ref, wd_ref, o_ref):
+    sources, slots, width = x_ref.shape
+    rows = x_ref[...].reshape(sources * slots, width).astype(jnp.bfloat16)
+    gate_proj = jnp.dot(rows, wg_ref[0], preferred_element_type=jnp.float32)
+    up_proj = jnp.dot(rows, wu_ref[0], preferred_element_type=jnp.float32)
+    hidden = (gate_proj / (1.0 + jnp.exp(-gate_proj)) * up_proj).astype(jnp.bfloat16)
+    down_out = jnp.dot(hidden, wd_ref[0], preferred_element_type=jnp.float32)
+    result = (sw_ref[...].reshape(sources * slots, 1) * down_out).astype(jnp.bfloat16)
+    o_ref[...] = result.astype(jnp.float32).reshape(sources, slots, width)
+
+
+def expert_ffn(row_block, slot_weight, w_gate, w_up, w_down):
+    sources, slots, width = row_block.shape
+    per_device, _, hidden = w_gate.shape
+    rows = slots // per_device
+    return pl.pallas_call(
+        ffn_kernel,
+        out_shape=jax.ShapeDtypeStruct(row_block.shape, jnp.float32),
+        grid=(per_device,),
+        in_specs=[
+            pl.BlockSpec((sources, rows, width), lambda e: (0, e, 0)),
+            pl.BlockSpec((sources, rows, 1), lambda e: (0, e, 0)),
+            pl.BlockSpec((1, width, hidden), lambda e: (e, 0, 0)),
+            pl.BlockSpec((1, width, hidden), lambda e: (e, 0, 0)),
+            pl.BlockSpec((1, hidden, width), lambda e: (e, 0, 0)),
+        ],
+        out_specs=pl.BlockSpec((sources, rows, width), lambda e: (0, e, 0)),
+        compiler_params=pltpu.CompilerParams(vmem_limit_bytes=56 * 1024 * 1024),
+    )(row_block, slot_weight[..., None], w_gate, w_up, w_down)
 
 
 def body(
@@ -293,22 +324,13 @@
         local_key[:, None, :, :] == jnp.arange(local_count, dtype=jnp.int32)[None, :, None, None]
     )
     picker = jnp.any(match, axis=3).astype(jnp.bfloat16)
-    slot_weight = jnp.sum(jnp.where(match, weight_cube[:, None, :, :], 0.0), axis=(2, 3)).reshape(
-        expert_count, per_device, MOST
-    )
-    row_block = jnp.einsum(
-        "sqt,std->sqd", picker, inputs_all, preferred_element_type=jnp.float32
-    ).astype(jnp.bfloat16)
-    row_block = row_block.reshape(expert_count, per_device, MOST, model_width)
-    gate_proj = jnp.einsum("nemd,edf->nemf", row_block, w_gate, preferred_element_type=jnp.float32)
-    up_proj = jnp.einsum("nemd,edf->nemf", row_block, w_up, preferred_element_type=jnp.float32)
-    hidden = (jax.nn.silu(gate_proj) * up_proj).astype(jnp.bfloat16)
-    down_out = jnp.einsum("nemf,efd->nemd", hidden, w_down, preferred_element_type=jnp.float32)
-    result = (slot_weight[..., None] * down_out).astype(jnp.bfloat16)
+    slot_weight = jnp.sum(jnp.where(match, weight_cube[:, None, :, :], 0.0), axis=(2, 3))
+    row_block = jnp.einsum("sqt,std->sqd", picker, inputs_all, preferred_element_type=jnp.float32)
+    result = expert_ffn(row_block, slot_weight, w_gate, w_up, w_down).astype(jnp.bfloat16)
     partial_value = jnp.einsum(
         "sqt,sqd->std",
         picker,
-        result.reshape(expert_count, local_count, model_width),
+        result,
         preferred_element_type=jnp.float32,
     )
     partial_value = partial_value.reshape(c_count, z_count, tok_rows, model_width)

time: 98.5 us -> 101 us (1.025)
  Pallas kernels: 59.5 us -> 70.4 us
  matrix products: 17.3 us -> 10.5 us
  local copies, waits for them, and re-layouts: 6.48 us -> 4.96 us
    pallas_call x0 -> x1, Pallas kernels: none -> 10.9 us  [expert_ffn(): pl.pallas_call(ffn_kernel, out_shape=jax.ShapeDtypeStruct(row_block.shape...]
    dot_general x3 -> x1, matrix products: 13.4 us -> 4.08 us  [body(): jnp.einsum('sqt,sqd->std', picker, result, preferred_element_type=jnp.flo...]
    dot_general x1, matrix products: 3.3 us -> 5.81 us  [body(): jnp.einsum('sqt,std->sqd', picker, inputs_all, preferred_element_type=jnp...]
    convert_element_type x1 -> x0, local copies, waits for them, and re-layouts: 2.29 us -> none  [body(): result = (slot_weight[..., None] * down_out).astype(jnp.bfloat16)]
    unnamed x7 -> x5, local copies, waits for them, and re-layouts: 2.39 us -> 2.25 us
where the time goes in v7:
time: 101 us
  Pallas kernels  70.4 us (70%)
  matrix products  10.5 us (10%)
  other arithmetic  8.99 us (9%)
  local copies, waits for them, and re-layouts  4.96 us (5%)
  starting transfers between devices  3.31 us (3%)
  waiting for transfers between devices  1.82 us (2%)
    pallas_call x1, Pallas kernels, gather_blocks(): pl.pallas_call(functools.partial(dispatch_kernel, z_count, chunks), out_s...  32.1 us
    pallas_call x1, Pallas kernels, scatter_sums(): pl.pallas_call(functools.partial(combine_kernel, z_count, chunks), out_sh...  27.4 us
    pallas_call x1, Pallas kernels, expert_ffn(): pl.pallas_call(ffn_kernel, out_shape=jax.ShapeDtypeStruct(row_block.shape...  10.9 us
    dot_general x1, matrix products, body(): jnp.einsum('sqt,std->sqd', picker, inputs_all, preferred_element_type=jnp...  5.81 us
    dot_general x1, matrix products, body(): jnp.einsum('sqt,sqd->std', picker, result, preferred_element_type=jnp.flo...  4.08 us
    ppermute x1, starting transfers between devices, from_partner(): return lax.ppermute(block, axis, route)  3.31 us
    unnamed x5, local copies, waits for them, and re-layouts  2.25 us
  transfers between devices with their start and end apart: 1, of which 1 were waited for; matrix products, arithmetic and copies ran while one was open for 0% of the time, Pallas kernels for 0%

profile of v7, /device:TPU:2, one launch (start us, length us, event | category | flops | bytes accessed | tf_op | source)
XLA Modules:
  0.0 100.7 jit_solution(15825694122949146455)
XLA Ops:
  0.6 0.7 convert.13
  1.3 0.8 copy.32
  2.1 0.7 broadcast_compare_fusion
  2.9 0.8 slice_reduce_fusion.1
  3.9 0.8 copy.33
  4.8 0.3 fusion.4
  5.3 1.1 %add_convert_fusion = bf16[64,2048]{1,0:T(8,128)(2,1)S(1)} fusion(bf16[64,2048]{1,0:T(8,128)(2,1)} %param.9, pred[64]{0:T(512)(128)(4,1)S(1)} %eq.47, bf16[2048]{0:T(1024)(128)(2,1)S(1)} %get-tuple-element.3, bf16[2048]{0:T(1024)(128)(2,1)S(1)} %get-tuple-element.2), kind=kLoop, calls=%fused_computation.17 | loop fusion | flops 655360 | bytes 532544 | tf_op jit(solution)/shard_map/convert_element_type | solution.py:302
  6.3 0.7 pad_maximum_fusion.blk_ref
  7.1 32.1 %shard_map.104 = bf16[16,64,2176]{2,1,0:T(8,128)(2,1)} custom-call(bf16[64,2176]{1,0:T(8,128)(2,1)} %pad_maximum_fusion.blk_ref), custom_call_target="tpu_custom_call" | custom-call | tf_op jit(solution)/shard_map/pallas_call | solution.py:116
  39.2 1.0 slice_convert_fusion
  40.2 0.5 fusion.7
  40.7 0.5 broadcast_divide_fusion
  41.8 1.2 %fusion.3 = pred[16,48,64]{2,1,0:T(8,128)(4,1)S(1)} fusion(s32[16,64,8]{1,2,0:T(8,128)S(1)} %copy.38), kind=kLoop, calls=%fused_computation.6 | loop fusion | flops 737280 | bytes 81920 | tf_op jit(solution)/shard_map/reduce_or | solution.py:326
  43.0 1.7 %select_reduce_fusion = f32[16,48]{1,0:T(8,128)S(1)} fusion(f32[16,64,8]{1,2,0:T(8,128)S(1)} %copy.40, s32[16,64,8]{1,2,0:T(8,128)S(1)} %copy.38), kind=kLoop, calls=%fused_computation.4 | loop fusion | flops 1178880 | bytes 68608 | tf_op jit(solution)/shard_map/reduce_sum | solution.py:327
  44.6 1.0 copy.41.sw_ref
  45.6 5.8 %fusion.x_ref = f32[16,48,2048]{2,1,0:T(8,128)} fusion(pred[16,48,64]{2,1,0:T(8,128)(4,1)S(1)} %fusion.3, bf16[16,64,2176]{2,1,0:T(8,128)(2,1)} %shard_map.104), kind=kOutput, calls=%fused_computation | convolution fusion | flops 201326592 | bytes 10534912 | tf_op jit(solution)/shard_map/sqt,std->sqd/dot_general | solution.py:328
  51.4 10.9 %shard_map.105 = f32[16,48,2048]{2,1,0:T(8,128)} custom-call(f32[16,48,2048]{2,1,0:T(8,128)} %fusion.x_ref, f32[16,48,1]{2,1,0:T(8,128)} %copy.41.sw_ref, bf16[2,2048,512]{2,1,0:T(8,128)(2,1)} %wg_ref.1, bf16[2,2048,512]{2,1,0:T(8,128)(2,1)} %wu_ref.1, bf16[2,512,2048]{2,1,0:T(8,128)(2,1)} %wd_ref.1), custom_call_target="tpu_custom_call" | custom-call | tf_op jit(solution)/shard_map/pallas_call | solution.py:273
  62.3 4.1 %convolution_convert_fusion = bf16[16,64,2048]{2,1,0:T(8,128)(2,1)S(1)} fusion(pred[16,48,64]{2,1,0:T(8,128)(4,1)S(1)} %fusion.3, f32[16,48,2048]{2,1,0:T(8,128)} %shard_map.105), kind=kOutput, calls=%fused_computation.2 | convolution fusion | flops 204996608 | bytes 10534912 | tf_op jit(solution)/shard_map/sqt,sqd->std/dot_general | solution.py:330
  66.4 27.4 %shard_map.106 = bf16[64,2048]{1,0:T(8,128)(2,1)S(1)} custom-call(bf16[2,8,64,2048]{3,2,1,0:T(8,128)(2,1)S(1)} %bitcast.10), custom_call_target="tpu_custom_call" | custom-call | tf_op jit(solution)/shard_map/pallas_call | solution.py:238
  93.8 0.3 convolution_bitcast_fusion
  94.3 3.3 %collective-permute-start = (f32[4]{0:T(128)S(1)}, f32[4]{0:T(128)S(1)}, u32[]{:S(2)}, u32[]{:S(2)}) collective-permute-start(f32[4]{0:T(128)S(1)} %reduce_sum.39), channel_id=1, source_target_pairs={{0,128},{128,0},{16,144},{144,16},{32,160},{160,32},{48,176},{176,... | collective-permute-start | bytes 56 | tf_op jit(solution)/shard_map/ppermute | solution.py:22
  97.7 1.8 %collective-permute-done = f32[4]{0:T(128)S(1)} collective-permute-done((f32[4]{0:T(128)S(1)}, f32[4]{0:T(128)S(1)}, u32[]{:S(2)}, u32[]{:S(2)}) %collective-permute-start) | collective-permute-done | bytes 48 | tf_op jit(solution)/shard_map/ppermute | solution.py:22
  99.5 0.5 multiply_add_fusion
  100.0 0.7 copy.43
  (15 shorter events, 1.4 us)
Async XLA Ops:
  0.6 93.2 %copy-start = (f32[2048]{0:T(1024)S(1)}, f32[2048]{0:T(1024)}, u32[]{:S(2)}) copy-start(f32[2048]{0:T(1024)} %param.17) | copy-start | bytes 24580
  94.3 5.1 %collective-permute-start = (f32[4]{0:T(128)S(1)}, f32[4]{0:T(128)S(1)}, u32[]{:S(2)}, u32[]{:S(2)}) collective-permute-start(f32[4]{0:T(128)S(1)} %reduce_sum.39), channel_id=1, source_target_pairs={{0,128},{128,0},{16,144},{144,16},{32,160},{160,32},{48,176},{176,... | collective-permute-start | bytes 56 | tf_op jit(solution)/shard_map/ppermute | solution.py:22

commit v8 on v4

--- a/solution.py
+++ b/solution.py
@@ -253,6 +253,76 @@
             collective_id=1, has_side_effects=True, vmem_limit_bytes=48 * 1024 * 1024
         ),
     )(partial)
+
+
+def local_kernel(
+    inp_ref, pick_ref, pickt_ref, sw_ref, wg_hbm, wu_hbm, wd_hbm, o_ref, wg, wu, wd, x_scr, sem
+):
+    copies = [
+        pltpu.make_async_copy(src, dst, sem.at[n])
+        for n, (src, dst) in enumerate(((wg_hbm, wg), (wu_hbm, wu), (wd_hbm, wd)))
+    ]
+    for copy in copies:
+        copy.start()
+    sources, slots, _ = pick_ref.shape
+    per_device = wg.shape[0]
+    most = slots // per_device
+    width = o_ref.shape[2]
+
+    def gather(s, carry):
+        rows = jnp.dot(pick_ref[s], inp_ref[s, :, pl.ds(0, width)], preferred_element_type=jnp.float32)
+        start = pl.multiple_of(s * most, 8)
+        for e in range(per_device):
+            x_scr[e, pl.ds(start, most)] = rows[e * most : (e + 1) * most]
+        return carry
+
+    lax.fori_loop(0, sources, gather, 0)
+    for copy in copies:
+        copy.wait()
+    for e in range(per_device):
+        rows = x_scr[e].astype(jnp.bfloat16)
+        gate_proj = jnp.dot(rows, wg[e], preferred_element_type=jnp.float32)
+        up_proj = jnp.dot(rows, wu[e], preferred_element_type=jnp.float32)
+        hidden = (gate_proj / (1.0 + jnp.exp(-gate_proj)) * up_proj).astype(jnp.bfloat16)
+        down_out = jnp.dot(hidden, wd[e], preferred_element_type=jnp.float32)
+        x_scr[e] = (sw_ref[e] * down_out).astype(jnp.bfloat16).astype(jnp.float32)
+
+    def combine(s, carry):
+        start = pl.multiple_of(s * most, 8)
+        total = jnp.zeros(o_ref.shape[1:], jnp.float32)
+        for e in range(per_device):
+            result = x_scr[e, pl.ds(start, most)]
+            total = total + jnp.dot(pickt_ref[s, e], result, preferred_element_type=jnp.float32)
+        o_ref[s] = total.astype(o_ref.dtype)
+        return carry
+
+    lax.fori_loop(0, sources, combine, 0)
+
+
+def local_experts(gathered, picker, slot_weight, w_gate, w_up, w_down, model_width):
+    sources, slots, tok_rows = picker.shape
+    per_device = w_gate.shape[0]
+    most = slots // per_device
+    pick_t = picker.astype(jnp.float32).reshape(sources, per_device, most, tok_rows)
+    pick_t = jnp.swapaxes(pick_t, 2, 3)
+    weights = slot_weight.reshape(sources, per_device, most).transpose(1, 0, 2)
+    weights = weights.reshape(per_device, sources * most, 1)
+    vmem = pl.BlockSpec(memory_space=pltpu.VMEM)
+    hbm = pl.BlockSpec(memory_space=pl.ANY)
+    return pl.pallas_call(
+        local_kernel,
+        out_shape=jax.ShapeDtypeStruct((sources, tok_rows, model_width), jnp.bfloat16),
+        in_specs=[vmem, vmem, vmem, vmem, hbm, hbm, hbm],
+        out_specs=vmem,
+        scratch_shapes=[
+            pltpu.VMEM(w_gate.shape, w_gate.dtype),
+            pltpu.VMEM(w_up.shape, w_up.dtype),
+            pltpu.VMEM(w_down.shape, w_down.dtype),
+            pltpu.VMEM((per_device, sources * most, model_width), jnp.float32),
+            pltpu.SemaphoreType.DMA((3,)),
+        ],
+        compiler_params=pltpu.CompilerParams(vmem_limit_bytes=60 * 1024 * 1024),
+    )(gathered, picker, pick_t, weights, w_gate, w_up, w_down)
 
 
 def body(
@@ -293,26 +363,10 @@
         local_key[:, None, :, :] == jnp.arange(local_count, dtype=jnp.int32)[None, :, None, None]
     )
     picker = jnp.any(match, axis=3).astype(jnp.bfloat16)
-    slot_weight = jnp.sum(jnp.where(match, weight_cube[:, None, :, :], 0.0), axis=(2, 3)).reshape(
-        expert_count, per_device, MOST
-    )
-    row_block = jnp.einsum(
-        "sqt,std->sqd", picker, inputs_all, preferred_element_type=jnp.float32
-    ).astype(jnp.bfloat16)
-    row_block = row_block.reshape(expert_count, per_device, MOST, model_width)
-    gate_proj = jnp.einsum("nemd,edf->nemf", row_block, w_gate, preferred_element_type=jnp.float32)
-    up_proj = jnp.einsum("nemd,edf->nemf", row_block, w_up, preferred_element_type=jnp.float32)
-    hidden = (jax.nn.silu(gate_proj) * up_proj).astype(jnp.bfloat16)
-    down_out = jnp.einsum("nemf,efd->nemd", hidden, w_down, preferred_element_type=jnp.float32)
-    result = (slot_weight[..., None] * down_out).astype(jnp.bfloat16)
-    partial_value = jnp.einsum(
-        "sqt,sqd->std",
-        picker,
-        result.reshape(expert_count, local_count, model_width),
-        preferred_element_type=jnp.float32,
-    )
+    slot_weight = jnp.sum(jnp.where(match, weight_cube[:, None, :, :], 0.0), axis=(2, 3))
+    partial_value = local_experts(gathered, picker, slot_weight, w_gate, w_up, w_down, model_width)
     partial_value = partial_value.reshape(c_count, z_count, tok_rows, model_width)
-    mixed = scatter_sums(partial_value.astype(jnp.bfloat16), 2)
+    mixed = scatter_sums(partial_value, 2)
     token_score = jnp.dot(mixed.astype(jnp.float32), score_head, precision=lax.Precision.HIGHEST)
     seq_score = token_score.reshape(-1, SEQ_LEN).sum(axis=1)
     partner = from_partner(seq_score, "dp", lax.axis_size("dp").bit_length() - 2)

time: 98.5 us -> 103 us (1.046)
  Pallas kernels: 59.5 us -> 78.4 us
  matrix products: 17.3 us -> 0.58 us
  local copies, waits for them, and re-layouts: 6.48 us -> 8.44 us
    pallas_call x0 -> x1, Pallas kernels: none -> 19 us  [local_experts(): pl.pallas_call(local_kernel, out_shape=jax.ShapeDtypeStruct((sources, tok...]
    dot_general x4 -> x0, matrix products: 16.7 us -> none  [the longest x1 9.16 us: body(): jnp.einsum('nemf,efd->nemd', hidden, w_down, preferred_element_type=jnp.f...]
    convert_element_type x1 -> x0, local copies, waits for them, and re-layouts: 2.29 us -> none  [body(): result = (slot_weight[..., None] * down_out).astype(jnp.bfloat16)]
    unnamed x7 -> x9, local copies, waits for them, and re-layouts: 2.39 us -> 4.44 us
    transpose x0 -> x2, local copies, waits for them, and re-layouts: none -> 1.29 us  [the longest x1 1.28 us: local_experts(): pick_t = jnp.swapaxes(pick_t, 2, 3)]
where the time goes in v8:
time: 103 us; the launch traced here: 102 us
  Pallas kernels  78.4 us (76%)
  other arithmetic  9.03 us (9%)
  local copies, waits for them, and re-layouts  8.44 us (8%)
  starting transfers between devices  3.27 us (3%)
  waiting for transfers between devices  1.86 us (2%)
    pallas_call x1, Pallas kernels, gather_blocks(): pl.pallas_call(functools.partial(dispatch_kernel, z_count, chunks), out_s...  32.1 us
    pallas_call x1, Pallas kernels, scatter_sums(): pl.pallas_call(functools.partial(combine_kernel, z_count, chunks), out_sh...  27.3 us
    pallas_call x1, Pallas kernels, local_experts(): pl.pallas_call(local_kernel, out_shape=jax.ShapeDtypeStruct((sources, tok...  19 us
    unnamed x9, local copies, waits for them, and re-layouts  4.44 us
    ppermute x1, starting transfers between devices, from_partner(): return lax.ppermute(block, axis, route)  3.27 us
  transfers between devices with their start and end apart: 1, of which 1 were waited for; matrix products, arithmetic and copies ran while one was open for 0% of the time, Pallas kernels for 0%

profile of v8, /device:TPU:2, one launch (start us, length us, event | category | flops | bytes accessed | tf_op | source)
XLA Modules:
  0.0 102.3 jit_solution(11052316074469735967)
XLA Ops:
  0.6 0.7 convert.17
  1.3 0.8 copy.36
  2.1 0.7 broadcast_compare_fusion
  2.9 0.8 slice_reduce_fusion.1
  3.9 0.8 copy.37
  4.8 0.3 fusion.1
  5.3 1.1 %add_convert_fusion = bf16[64,2048]{1,0:T(8,128)(2,1)S(1)} fusion(bf16[64,2048]{1,0:T(8,128)(2,1)} %param.9, pred[64]{0:T(512)(128)(4,1)S(1)} %eq.47, bf16[2048]{0:T(1024)(128)(2,1)S(1)} %get-tuple-element.3, bf16[2048]{0:T(1024)(128)(2,1)S(1)} %get-tuple-element.2), kind=kLoop, calls=%fused_computation.13 | loop fusion | flops 655360 | bytes 532544 | tf_op jit(solution)/shard_map/convert_element_type | solution.py:341
  6.3 0.7 pad_maximum_fusion.blk_ref
  7.1 32.1 %shard_map.104.inp_ref = bf16[16,64,2176]{2,1,0:T(8,128)(2,1)} custom-call(bf16[64,2176]{1,0:T(8,128)(2,1)} %pad_maximum_fusion.blk_ref), custom_call_target="tpu_custom_call" | custom-call | tf_op jit(solution)/shard_map/pallas_call | solution.py:116
  39.2 1.0 slice_convert_fusion
  40.2 0.5 fusion.4
  40.7 0.5 broadcast_divide_fusion
  41.8 1.2 %fusion = pred[16,48,64]{2,1,0:T(8,128)(4,1)S(1)} fusion(s32[16,64,8]{1,2,0:T(8,128)S(1)} %copy.42), kind=kLoop, calls=%fused_computation.2 | loop fusion | flops 737280 | bytes 81920 | tf_op jit(solution)/shard_map/reduce_or | solution.py:365
  43.0 1.7 %select_reduce_fusion = f32[16,48]{1,0:T(8,128)S(1)} fusion(f32[16,64,8]{1,2,0:T(8,128)S(1)} %copy.45, s32[16,64,8]{1,2,0:T(8,128)S(1)} %copy.42), kind=kLoop, calls=%fused_computation | loop fusion | flops 1178880 | bytes 68608 | tf_op jit(solution)/shard_map/reduce_sum | solution.py:366
  44.8 0.9 reshape.47.sw_ref
  45.7 1.3 %copy.43 = f32[16,2,24,64]{2,3,1,0:T(8,128)} copy(bf16[16,2,24,64]{3,2,1,0:T(8,128)(2,1)S(1)} %bitcast.13) | data formatting | bytes 294912 | tf_op jit(solution)/shard_map/transpose | solution.py:307
  47.0 19.0 %shard_map.105 = bf16[16,64,2048]{2,1,0:T(8,128)(2,1)} custom-call(bf16[16,64,2176]{2,1,0:T(8,128)(2,1)} %shard_map.104.inp_ref, bf16[16,48,64]{2,1,0:T(8,128)(2,1)} %copy-done.2, f32[16,2,64,24]{3,2,1,0:T(8,128)} %bitcast.12, f32[2,384,1]{2,1,0:T(8,128)} %reshape.47.sw_ref, bf16[2,2048,512]{2,1,0:T(8,128)(2,1)} %wg_hbm.1, bf16[2,2048,512]{2,1,0:T(8,128)(2,1)} %wu_hbm.1, ...), custom_call_target="tpu_custom_call" | custom-call | tf_op jit(solution)/shard_map/pallas_call | solution.py:312
  66.0 2.2 %copy-done.1 = bf16[16,64,2048]{2,1,0:T(8,128)(2,1)S(1)} copy-done((bf16[16,64,2048]{2,1,0:T(8,128)(2,1)S(1)}, bf16[16,64,2048]{2,1,0:T(8,128)(2,1)}, u32[]{:S(2)}) %copy-start.1) | copy-done | bytes 4194328
  68.2 27.3 %shard_map.106 = bf16[64,2048]{1,0:T(8,128)(2,1)S(1)} custom-call(bf16[2,8,64,2048]{3,2,1,0:T(8,128)(2,1)S(1)} %bitcast.11), custom_call_target="tpu_custom_call" | custom-call | tf_op jit(solution)/shard_map/pallas_call | solution.py:238
  95.5 0.3 convolution_bitcast_fusion
  96.0 3.3 %collective-permute-start = (f32[4]{0:T(128)S(1)}, f32[4]{0:T(128)S(1)}, u32[]{:S(2)}, u32[]{:S(2)}) collective-permute-start(f32[4]{0:T(128)S(1)} %reduce_sum.39), channel_id=1, source_target_pairs={{0,128},{128,0},{16,144},{144,16},{32,160},{160,32},{48,176},{176,... | collective-permute-start | bytes 56 | tf_op jit(solution)/shard_map/ppermute | solution.py:22
  99.2 1.9 %collective-permute-done = f32[4]{0:T(128)S(1)} collective-permute-done((f32[4]{0:T(128)S(1)}, f32[4]{0:T(128)S(1)}, u32[]{:S(2)}, u32[]{:S(2)}) %collective-permute-start) | collective-permute-done | bytes 48 | tf_op jit(solution)/shard_map/ppermute | solution.py:22
  101.1 0.5 multiply_add_fusion
  101.6 0.7 copy.49
  (21 shorter events, 1.5 us)
Async XLA Ops:
  0.6 94.8 %copy-start = (f32[2048]{0:T(1024)S(1)}, f32[2048]{0:T(1024)}, u32[]{:S(2)}) copy-start(f32[2048]{0:T(1024)} %param.17) | copy-start | bytes 24580
  44.8 2.2 %copy-start.2 = (bf16[16,48,64]{2,1,0:T(8,128)(2,1)}, bf16[16,48,64]{2,1,0:T(8,128)(2,1)S(1)}, u32[]{:S(2)}) copy-start(bf16[16,48,64]{2,1,0:T(8,128)(2,1)S(1)} %convert_element_type.42.pick_ref) | copy-start | bytes 294916
  66.0 2.2 %copy-start.1 = (bf16[16,64,2048]{2,1,0:T(8,128)(2,1)S(1)}, bf16[16,64,2048]{2,1,0:T(8,128)(2,1)}, u32[]{:S(2)}) copy-start(bf16[16,64,2048]{2,1,0:T(8,128)(2,1)} %shard_map.105) | copy-start | bytes 12582916
  96.0 5.1 %collective-permute-start = (f32[4]{0:T(128)S(1)}, f32[4]{0:T(128)S(1)}, u32[]{:S(2)}, u32[]{:S(2)}) collective-permute-start(f32[4]{0:T(128)S(1)} %reduce_sum.39), channel_id=1, source_target_pairs={{0,128},{128,0},{16,144},{144,16},{32,160},{160,32},{48,176},{176,... | collective-permute-start | bytes 56 | tf_op jit(solution)/shard_map/ppermute | solution.py:22

commit v9 on v4

--- a/solution.py
+++ b/solution.py
@@ -116,14 +116,16 @@
     return pl.pallas_call(
         functools.partial(dispatch_kernel, z_count, chunks),
         out_shape=jax.ShapeDtypeStruct((count,) + block.shape, block.dtype),
-        in_specs=[pl.BlockSpec(memory_space=pl.ANY)],
-        out_specs=pl.BlockSpec(memory_space=pl.ANY),
+        in_specs=[pl.BlockSpec(memory_space=pltpu.VMEM)],
+        out_specs=pl.BlockSpec(memory_space=pltpu.VMEM),
         scratch_shapes=[
             pltpu.SemaphoreType.DMA((2 * count * chunks,)),
             pltpu.SemaphoreType.DMA((count * chunks,)),
             pltpu.SemaphoreType.DMA((1,)),
         ],
-        compiler_params=pltpu.CompilerParams(collective_id=0, has_side_effects=True),
+        compiler_params=pltpu.CompilerParams(
+            collective_id=0, has_side_effects=True, vmem_limit_bytes=32 * 1024 * 1024
+        ),
     )(block)
 
 

time: 98.5 us -> 98.1 us (level)
  local copies, waits for them, and re-layouts: 6.48 us -> 8.51 us
  other arithmetic: 8.99 us -> 7.34 us
    unnamed x7 -> x9, local copies, waits for them, and re-layouts: 2.39 us -> 4.42 us
where the time goes in v9:
time: 98.1 us; the launch traced here: 97.8 us
  Pallas kernels  58.7 us (60%)
  matrix products  17.3 us (18%)
  local copies, waits for them, and re-layouts  8.51 us (9%)
  other arithmetic  7.34 us (7%)
  starting transfers between devices  3.29 us (3%)
  waiting for transfers between devices  1.84 us (2%)
    pallas_call x1, Pallas kernels, gather_blocks(): pl.pallas_call(functools.partial(dispatch_kernel, z_count, chunks), out_s...  31.3 us
    pallas_call x1, Pallas kernels, scatter_sums(): pl.pallas_call(functools.partial(combine_kernel, z_count, chunks), out_sh...  27.4 us
    dot_general x1, matrix products, body(): jnp.einsum('nemf,efd->nemd', hidden, w_down, preferred_element_type=jnp.f...  9.16 us
    unnamed x9, local copies, waits for them, and re-layouts  4.42 us
    dot_general x1, matrix products, body(): jnp.einsum('sqt,std->sqd', picker, inputs_all, preferred_element_type=jnp...  3.3 us
    ppermute x1, starting transfers between devices, from_partner(): return lax.ppermute(block, axis, route)  3.29 us
    dot_general x1, matrix products, body(): jnp.einsum('nemd,edf->nemf', row_block, w_gate, preferred_element_type=jn...  2.96 us
    convert_element_type x1, local copies, waits for them, and re-layouts, body(): result = (slot_weight[..., None] * down_out).astype(jnp.bfloat16)  2.29 us
  transfers between devices with their start and end apart: 1, of which 1 were waited for; matrix products, arithmetic and copies ran while one was open for 0% of the time, Pallas kernels for 0%

profile of v9, /device:TPU:2, one launch (start us, length us, event | category | flops | bytes accessed | tf_op | source)
XLA Modules:
  0.0 97.8 jit_solution(1640421911519385824)
XLA Ops:
  0.6 0.7 convert.13
  1.3 0.8 copy.38
  2.1 0.7 broadcast_compare_fusion
  2.9 0.8 slice_reduce_fusion.1
  3.9 0.8 copy.39
  4.8 0.3 fusion.25
  5.3 1.1 %add_convert_fusion = bf16[64,2048]{1,0:T(8,128)(2,1)S(1)} fusion(bf16[64,2048]{1,0:T(8,128)(2,1)} %param.9, pred[64]{0:T(512)(128)(4,1)S(1)} %eq.47, bf16[2048]{0:T(1024)(128)(2,1)S(1)} %get-tuple-element.3, bf16[2048]{0:T(1024)(128)(2,1)S(1)} %get-tuple-element.2), kind=kLoop, calls=%fused_computation.35 | loop fusion | flops 655360 | bytes 532544 | tf_op jit(solution)/shard_map/convert_element_type | solution.py:273
  6.4 31.3 %shard_map.104 = bf16[16,64,2176]{2,1,0:T(8,128)(2,1)S(1)} custom-call(bf16[64,2176]{1,0:T(8,128)(2,1)S(1)} %pad_maximum_fusion.blk_ref), custom_call_target="tpu_custom_call" | custom-call | tf_op jit(solution)/shard_map/pallas_call | solution.py:116
  37.7 2.0 %copy-done.1 = bf16[16,64,2176]{2,1,0:T(8,128)(2,1)} copy-done((bf16[16,64,2176]{2,1,0:T(8,128)(2,1)}, bf16[16,64,2176]{2,1,0:T(8,128)(2,1)S(1)}, u32[]{:S(2)}) %copy-start.1) | copy-done | bytes 4456472
  39.8 0.5 fusion.33
  40.3 0.5 broadcast_divide_fusion
  41.3 1.2 %fusion.14 = pred[16,48,64]{2,1,0:T(8,128)(4,1)S(1)} fusion(s32[16,64,8]{1,2,0:T(8,128)S(1)} %copy.44), kind=kLoop, calls=%fused_computation.14 | loop fusion | flops 737280 | bytes 81920 | tf_op jit(solution)/shard_map/reduce_or | solution.py:297
  42.5 1.7 %select_reduce_fusion = f32[16,48]{1,0:T(8,128)S(1)} fusion(f32[16,64,8]{1,2,0:T(8,128)S(1)} %copy.46, s32[16,64,8]{1,2,0:T(8,128)S(1)} %copy.44), kind=kLoop, calls=%fused_computation.12 | loop fusion | flops 1178880 | bytes 68608 | tf_op jit(solution)/shard_map/reduce_sum | solution.py:298
  44.3 3.3 %fusion.11 = bf16[16,48,2048]{2,1,0:T(8,128)(2,1)S(1)} fusion(pred[16,48,64]{2,1,0:T(8,128)(4,1)S(1)} %fusion.14, bf16[16,64,2176]{2,1,0:T(8,128)(2,1)} %copy-done.1), kind=kOutput, calls=%fused_computation.11 | convolution fusion | flops 202899456 | bytes 7389184 | tf_op jit(solution)/shard_map/sqt,std->sqd/dot_general | solution.py:301
  47.7 3.0 %fusion.5 = f32[2,16,24,512]{3,2,1,0:T(8,128)} fusion(bf16[2,2048,512]{2,1,0:T(8,128)(2,1)S(1)} %copy-done.2, bf16[16,2,24,2048]{3,2,1,0:T(8,128)(2,1)S(1)} %bitcast.60), kind=kOutput, calls=%fused_computation.6 | convolution fusion | flops 1610612736 | bytes 8912896 | tf_op jit(solution)/shard_map/nemd,edf->nemf/dot_general | solution.py:305
  50.7 9.2 %fusion = bf16[16,2,24,2048]{3,2,0,1:T(8,128)(2,1)} fusion(bf16[2,512,2048]{2,1,0:T(8,128)(2,1)} %param.16, f32[16,2,24]{2,0,1:T(8,128)S(1)} %copy.47, f32[2,16,24,512]{3,2,1,0:T(8,128)} %fusion.5, bf16[2,2048,512]{2,1,0:T(8,128)(2,1)} %param.15, bf16[16,2,24,2048]{3,2,1,0:T(8,128)(2,1)S(1)} %bitcast.61), kind=kOutput, calls=%fused_computation.1 | convolution fusion | flops 3226730496 | bytes 16256000 | tf_op jit(solution)/shard_map/nemf,efd->nemd/dot_general | solution.py:308
  59.9 2.3 %copy.50 = bf16[16,2,24,2048]{3,2,1,0:T(8,128)(2,1)S(1)} copy(bf16[16,2,24,2048]{3,2,0,1:T(8,128)(2,1)} %fusion) | data formatting | bytes 6291456 | tf_op jit(solution)/shard_map/convert_element_type | solution.py:309
  62.1 1.3 %convolution_convert_fusion = bf16[16,64,2048]{2,1,0:T(8,128)(2,1)S(1)} fusion(pred[16,48,64]{2,1,0:T(8,128)(4,1)S(1)} %fusion.14, bf16[16,48,2048]{2,1,0:T(8,128)(2,1)S(1)} %bitcast.59), kind=kOutput, calls=%fused_computation.10 | convolution fusion | flops 203423744 | bytes 7389184 | tf_op jit(solution)/shard_map/sqt,sqd->std/dot_general | solution.py:310
  63.5 27.4 %shard_map.105 = bf16[64,2048]{1,0:T(8,128)(2,1)S(1)} custom-call(bf16[2,8,64,2048]{3,2,1,0:T(8,128)(2,1)S(1)} %bitcast.58), custom_call_target="tpu_custom_call" | custom-call | tf_op jit(solution)/shard_map/pallas_call | solution.py:240
  90.9 0.3 convolution_bitcast_fusion
  91.4 3.3 %collective-permute-start = (f32[4]{0:T(128)S(1)}, f32[4]{0:T(128)S(1)}, u32[]{:S(2)}, u32[]{:S(2)}) collective-permute-start(f32[4]{0:T(128)S(1)} %reduce_sum.39), channel_id=1, source_target_pairs={{0,128},{128,0},{16,144},{144,16},{32,160},{160,32},{48,176},{176,... | collective-permute-start | bytes 56 | tf_op jit(solution)/shard_map/ppermute | solution.py:22
  94.7 1.8 %collective-permute-done = f32[4]{0:T(128)S(1)} collective-permute-done((f32[4]{0:T(128)S(1)}, f32[4]{0:T(128)S(1)}, u32[]{:S(2)}, u32[]{:S(2)}) %collective-permute-start) | collective-permute-done | bytes 48 | tf_op jit(solution)/shard_map/ppermute | solution.py:22
  96.5 0.5 multiply_add_fusion
  97.1 0.7 copy.63
  (22 shorter events, 1.7 us)
Async XLA Ops:
  0.6 90.2 %copy-start = (f32[2048]{0:T(1024)S(1)}, f32[2048]{0:T(1024)}, u32[]{:S(2)}) copy-start(f32[2048]{0:T(1024)} %param.17) | copy-start | bytes 24580
  37.7 2.0 %copy-start.1 = (bf16[16,64,2176]{2,1,0:T(8,128)(2,1)}, bf16[16,64,2176]{2,1,0:T(8,128)(2,1)S(1)}, u32[]{:S(2)}) copy-start(bf16[16,64,2176]{2,1,0:T(8,128)(2,1)S(1)} %shard_map.104) | copy-start | bytes 13369348
  44.3 3.5 %copy-start.2 = (bf16[2,2048,512]{2,1,0:T(8,128)(2,1)S(1)}, bf16[2,2048,512]{2,1,0:T(8,128)(2,1)}, u32[]{:S(2)}) copy-start(bf16[2,2048,512]{2,1,0:T(8,128)(2,1)} %param.14) | copy-start | bytes 12582916
  91.4 5.1 %collective-permute-start = (f32[4]{0:T(128)S(1)}, f32[4]{0:T(128)S(1)}, u32[]{:S(2)}, u32[]{:S(2)}) collective-permute-start(f32[4]{0:T(128)S(1)} %reduce_sum.39), channel_id=1, source_target_pairs={{0,128},{128,0},{16,144},{144,16},{32,160},{160,32},{48,176},{176,... | collective-permute-start | bytes 56 | tf_op jit(solution)/shard_map/ppermute | solution.py:22

commit v10 on v9

--- a/solution.py
+++ b/solution.py
@@ -130,8 +130,8 @@
 
 
 def combine_kernel(
-    z_count, chunks, part_ref, out_ref, pair_buf, fwd_buf, bwd_buf, fwd_out, bwd_out,
-    send_sem, recv_sem,
+    z_count, dp_count, seq_len, chunks, part_ref, head_ref, out_ref, pair_out, pair_buf,
+    fwd_buf, bwd_buf, fwd_out, bwd_out, seq_out, seq_in, send_sem, recv_sem, seq_sem,
 ):
     z = lax.axis_index("z")
     c = lax.axis_index("c")
@@ -141,14 +141,15 @@
     fwd = lax.rem(z + step + z_count, z_count)
     bwd = lax.rem(z - step + z_count, z_count)
     fwd_id, bwd_id, pair_id = (row, fwd, c), (row, bwd, c), (row, z, other)
+    mate_id = (lax.rem(row + dp_count // 2, dp_count), z, c)
     fwd_hops = z_count // 2
     bwd_hops = z_count - 1 - fwd_hops
     piece = part_ref.shape[2] // chunks
 
     barrier = pltpu.get_barrier_semaphore()
-    for target in (fwd_id, bwd_id, pair_id):
+    for target in (fwd_id, bwd_id, pair_id, mate_id):
         pl.semaphore_signal(barrier, 1, device_id=target, device_id_type=MESH)
-    pl.semaphore_wait(barrier, 3)
+    pl.semaphore_wait(barrier, 4)
 
     sends = []
 
@@ -226,35 +227,62 @@
             arrive(bwd_buf.at[bwd_hops - 1, rows], bwd_sem + (bwd_hops - 1) * chunks + k)
             total = total + bwd_buf[bwd_hops - 1, rows].astype(jnp.float32)
         out_ref[rows] = total.astype(out_ref.dtype)
+    tok_rows, width = out_ref.shape
+    seqs = tok_rows // seq_len
+    scored = out_ref[...].astype(jnp.float32) * head_ref[...]
+    per_seq = jnp.sum(scored.reshape(seqs, seq_len, width), axis=1)
+    seq_score = jnp.sum(per_seq, axis=1, keepdims=True)
+    seq_out[...] = jnp.zeros(seq_out.shape, jnp.float32)
+    seq_out[pl.ds(0, seqs)] = jnp.broadcast_to(seq_score, (seqs, seq_out.shape[1]))
+    mate = pltpu.make_async_remote_copy(
+        src_ref=seq_out,
+        dst_ref=seq_in,
+        send_sem=seq_sem.at[0],
+        recv_sem=seq_sem.at[1],
+        device_id=mate_id,
+        device_id_type=MESH,
+    )
+    mate.start()
+    mate.wait()
+    mine = seq_out[...]
+    theirs = seq_in[...]
+    pair_out[...] = jnp.abs(mine - theirs) + 0.5 * (mine + theirs)
     for copy in sends:
         copy.wait_send()
 
 
-def scatter_sums(partial, chunks):
+def scatter_sums(partial, score_head, dp_count, seq_len, chunks):
     c_count, z_count, rows, width = partial.shape
     fwd_hops = z_count // 2
     bwd_hops = max(z_count - 1 - fwd_hops, 1)
     block = (rows, width)
     vmem = pl.BlockSpec(memory_space=pltpu.VMEM)
     sems = z_count + (fwd_hops + bwd_hops) * chunks
+    tile = (8, 128)
     return pl.pallas_call(
-        functools.partial(combine_kernel, z_count, chunks),
-        out_shape=jax.ShapeDtypeStruct(block, partial.dtype),
-        in_specs=[vmem],
-        out_specs=vmem,
+        functools.partial(combine_kernel, z_count, dp_count, seq_len, chunks),
+        out_shape=(
+            jax.ShapeDtypeStruct(block, partial.dtype),
+            jax.ShapeDtypeStruct(tile, jnp.float32),
+        ),
+        in_specs=[vmem, vmem],
+        out_specs=(vmem, vmem),
         scratch_shapes=[
             pltpu.VMEM((z_count,) + block, partial.dtype),
             pltpu.VMEM((fwd_hops,) + block, partial.dtype),
             pltpu.VMEM((bwd_hops,) + block, partial.dtype),
             pltpu.VMEM((fwd_hops,) + block, partial.dtype),
             pltpu.VMEM((bwd_hops,) + block, partial.dtype),
+            pltpu.VMEM(tile, jnp.float32),
+            pltpu.VMEM(tile, jnp.float32),
             pltpu.SemaphoreType.DMA((sems,)),
             pltpu.SemaphoreType.DMA((sems,)),
+            pltpu.SemaphoreType.DMA((2,)),
         ],
         compiler_params=pltpu.CompilerParams(
             collective_id=1, has_side_effects=True, vmem_limit_bytes=48 * 1024 * 1024
         ),
-    )(partial)
+    )(partial, score_head.reshape(1, -1))
 
 
 def body(
@@ -314,11 +342,10 @@
         preferred_element_type=jnp.float32,
     )
     partial_value = partial_value.reshape(c_count, z_count, tok_rows, model_width)
-    mixed = scatter_sums(partial_value.astype(jnp.bfloat16), 2)
-    token_score = jnp.dot(mixed.astype(jnp.float32), score_head, precision=lax.Precision.HIGHEST)
-    seq_score = token_score.reshape(-1, SEQ_LEN).sum(axis=1)
-    partner = from_partner(seq_score, "dp", lax.axis_size("dp").bit_length() - 2)
-    pair_score = jnp.abs(seq_score - partner) + 0.5 * (seq_score + partner)
+    mixed, pair_tile = scatter_sums(
+        partial_value.astype(jnp.bfloat16), score_head, lax.axis_size("dp"), SEQ_LEN, 2
+    )
+    pair_score = pair_tile[: tok_rows // SEQ_LEN, 0]
     return (mixed, pair_score)
 
 

time: 98.1 us -> 97.4 us (level)
  Pallas kernels: 58.7 us -> 63.7 us
  starting transfers between devices: 3.29 us -> 0 us
  waiting for transfers between devices: 1.84 us -> 0 us
    pallas_call x1, Pallas kernels: 27.4 us -> 32.4 us  [scatter_sums(): pl.pallas_call(functools.partial(combine_kernel, z_count, dp_count, seq_l...]
    ppermute x1 -> x0, starting transfers between devices: 3.29 us -> none  [from_partner(): return lax.ppermute(block, axis, route)]
    ppermute x1 -> x0, waiting for transfers between devices: 1.84 us -> none  [from_partner(): return lax.ppermute(block, axis, route)]
  transfers between devices with their start and end apart: 1 -> 0, of which waited for: 1 -> 0; matrix products, arithmetic and copies ran while one was open for 0% -> 0% of each run, Pallas kernels for 0% -> 0%
where the time goes in v10:
time: 97.4 us; the launch traced here: 97.1 us
  Pallas kernels  63.7 us (65%)
  matrix products  16.9 us (17%)
  local copies, waits for them, and re-layouts  9.03 us (9%)
  other arithmetic  6.68 us (7%)
    pallas_call x1, Pallas kernels, scatter_sums(): pl.pallas_call(functools.partial(combine_kernel, z_count, dp_count, seq_l...  32.4 us
    pallas_call x1, Pallas kernels, gather_blocks(): pl.pallas_call(functools.partial(dispatch_kernel, z_count, chunks), out_s...  31.3 us
    dot_general x1, matrix products, body(): jnp.einsum('nemf,efd->nemd', hidden, w_down, preferred_element_type=jnp.f...  9.1 us
    unnamed x9, local copies, waits for them, and re-layouts  4.42 us
    dot_general x1, matrix products, body(): jnp.einsum('sqt,std->sqd', picker, inputs_all, preferred_element_type=jnp...  3.3 us
    dot_general x1, matrix products, body(): jnp.einsum('nemd,edf->nemf', row_block, w_gate, preferred_element_type=jn...  2.93 us
    convert_element_type x1, local copies, waits for them, and re-layouts, body(): result = (slot_weight[..., None] * down_out).astype(jnp.bfloat16)  2.27 us

profile of v10, /device:TPU:2, one launch (start us, length us, event | category | flops | bytes accessed | tf_op | source)
XLA Modules:
  0.0 97.1 jit_solution(1675796827229229193)
XLA Ops:
  0.6 0.7 broadcast_compare_fusion
  1.5 0.7 convert.13
  2.2 0.8 slice_reduce_fusion.1
  3.1 0.8 copy.39
  3.9 0.8 copy.38
  4.8 0.3 fusion.25
  5.2 1.1 %add_convert_fusion = bf16[64,2048]{1,0:T(8,128)(2,1)S(1)} fusion(bf16[64,2048]{1,0:T(8,128)(2,1)} %param.9, pred[64]{0:T(512)(128)(4,1)S(1)} %eq.47, bf16[2048]{0:T(1024)(128)(2,1)S(1)} %get-tuple-element.7, bf16[2048]{0:T(1024)(128)(2,1)S(1)} %get-tuple-element.6), kind=kLoop, calls=%fused_computation.34 | loop fusion | flops 655360 | bytes 532544 | tf_op jit(solution)/shard_map/convert_element_type | solution.py:301
  6.4 31.3 %shard_map.104 = bf16[16,64,2176]{2,1,0:T(8,128)(2,1)S(1)} custom-call(bf16[64,2176]{1,0:T(8,128)(2,1)S(1)} %pad_maximum_fusion.blk_ref), custom_call_target="tpu_custom_call" | custom-call | tf_op jit(solution)/shard_map/pallas_call | solution.py:116
  37.7 2.0 %copy-done = bf16[16,64,2176]{2,1,0:T(8,128)(2,1)} copy-done((bf16[16,64,2176]{2,1,0:T(8,128)(2,1)}, bf16[16,64,2176]{2,1,0:T(8,128)(2,1)S(1)}, u32[]{:S(2)}) %copy-start) | copy-done | bytes 4456472
  39.8 0.5 fusion.33
  40.3 0.5 broadcast_divide_fusion
  40.8 0.2 copy.46
  40.9 0.2 fusion.32
  41.1 0.2 copy.44
  41.3 1.6 %select_reduce_fusion = f32[16,48]{1,0:T(8,128)S(1)} fusion(f32[16,64,8]{1,2,0:T(8,128)S(1)} %copy.46, s32[16,64,8]{1,2,0:T(8,128)S(1)} %copy.44), kind=kLoop, calls=%fused_computation.12 | loop fusion | flops 1178880 | bytes 68608 | tf_op jit(solution)/shard_map/reduce_sum | solution.py:326
  43.1 1.2 %fusion.14 = pred[16,48,64]{2,1,0:T(8,128)(4,1)S(1)} fusion(s32[16,64,8]{1,2,0:T(8,128)S(1)} %copy.44), kind=kLoop, calls=%fused_computation.14 | loop fusion | flops 737280 | bytes 81920 | tf_op jit(solution)/shard_map/reduce_or | solution.py:325
  44.3 3.3 %fusion.11 = bf16[16,48,2048]{2,1,0:T(8,128)(2,1)S(1)} fusion(pred[16,48,64]{2,1,0:T(8,128)(4,1)S(1)} %fusion.14, bf16[16,64,2176]{2,1,0:T(8,128)(2,1)} %copy-done), kind=kOutput, calls=%fused_computation.11 | convolution fusion | flops 202899456 | bytes 7389184 | tf_op jit(solution)/shard_map/sqt,std->sqd/dot_general | solution.py:329
  47.7 2.9 %fusion.5 = f32[2,16,24,512]{3,2,1,0:T(8,128)} fusion(bf16[2,2048,512]{2,1,0:T(8,128)(2,1)S(1)} %copy-done.2, bf16[16,2,24,2048]{3,2,1,0:T(8,128)(2,1)S(1)} %bitcast.56), kind=kOutput, calls=%fused_computation.6 | convolution fusion | flops 1610612736 | bytes 8912896 | tf_op jit(solution)/shard_map/nemd,edf->nemf/dot_general | solution.py:333
  50.6 9.1 %fusion = bf16[16,2,24,2048]{3,2,0,1:T(8,128)(2,1)} fusion(bf16[2,512,2048]{2,1,0:T(8,128)(2,1)} %param.16, f32[16,2,24]{2,0,1:T(8,128)S(1)} %copy.47, f32[2,16,24,512]{3,2,1,0:T(8,128)} %fusion.5, bf16[2,2048,512]{2,1,0:T(8,128)(2,1)} %param.15, bf16[16,2,24,2048]{3,2,1,0:T(8,128)(2,1)S(1)} %bitcast.57), kind=kOutput, calls=%fused_computation.1 | convolution fusion | flops 3226730496 | bytes 16256000 | tf_op jit(solution)/shard_map/nemf,efd->nemd/dot_general | solution.py:336
  59.7 2.3 %copy.50 = bf16[16,2,24,2048]{3,2,1,0:T(8,128)(2,1)S(1)} copy(bf16[16,2,24,2048]{3,2,0,1:T(8,128)(2,1)} %fusion) | data formatting | bytes 6291456 | tf_op jit(solution)/shard_map/convert_element_type | solution.py:337
  62.0 1.3 %convolution_convert_fusion = bf16[16,64,2048]{2,1,0:T(8,128)(2,1)S(1)} fusion(pred[16,48,64]{2,1,0:T(8,128)(4,1)S(1)} %fusion.14, bf16[16,48,2048]{2,1,0:T(8,128)(2,1)S(1)} %bitcast.55), kind=kOutput, calls=%fused_computation.10 | convolution fusion | flops 203423744 | bytes 7389184 | tf_op jit(solution)/shard_map/sqt,sqd->std/dot_general | solution.py:338
  63.3 32.4 %shard_map.105 = (bf16[64,2048]{1,0:T(8,128)(2,1)S(1)}, f32[8,128]{1,0:T(8,128)S(1)}) custom-call(bf16[2,8,64,2048]{3,2,1,0:T(8,128)(2,1)S(1)} %bitcast.53, f32[1,2048]{1,0:T(1,128)S(1)} %bitcast.54), custom_call_target="tpu_custom_call" | custom-call | tf_op jit(solution)/shard_map/pallas_call | solution.py:262
  95.8 0.6 slice_reduce_fusion.2
  96.4 0.7 copy.63
  (17 shorter events, 0.9 us)
Async XLA Ops:
  37.7 2.0 %copy-start = (bf16[16,64,2176]{2,1,0:T(8,128)(2,1)}, bf16[16,64,2176]{2,1,0:T(8,128)(2,1)S(1)}, u32[]{:S(2)}) copy-start(bf16[16,64,2176]{2,1,0:T(8,128)(2,1)S(1)} %shard_map.104) | copy-start | bytes 13369348
  44.3 3.5 %copy-start.2 = (bf16[2,2048,512]{2,1,0:T(8,128)(2,1)S(1)}, bf16[2,2048,512]{2,1,0:T(8,128)(2,1)}, u32[]{:S(2)}) copy-start(bf16[2,2048,512]{2,1,0:T(8,128)(2,1)} %param.14) | copy-start | bytes 12582916
  62.0 1.3 %copy-start.1 = (f32[2048]{0:T(1024)S(1)}, f32[2048]{0:T(1024)}, u32[]{:S(2)}) copy-start(f32[2048]{0:T(1024)} %param.17) | copy-start | bytes 24580

commit v11 on v10

--- a/solution.py
+++ b/solution.py
@@ -323,23 +323,19 @@
         local_key[:, None, :, :] == jnp.arange(local_count, dtype=jnp.int32)[None, :, None, None]
     )
     picker = jnp.any(match, axis=3).astype(jnp.bfloat16)
-    slot_weight = jnp.sum(jnp.where(match, weight_cube[:, None, :, :], 0.0), axis=(2, 3)).reshape(
-        expert_count, per_device, MOST
-    )
+    slot_weight = jnp.sum(jnp.where(match, weight_cube[:, None, :, :], 0.0), axis=(2, 3))
+    picker = picker.reshape(expert_count, per_device, MOST, tok_rows).transpose(1, 0, 2, 3)
+    slot_weight = slot_weight.reshape(expert_count, per_device, MOST).transpose(1, 0, 2)
     row_block = jnp.einsum(
-        "sqt,std->sqd", picker, inputs_all, preferred_element_type=jnp.float32
+        "esmt,std->esmd", picker, inputs_all, preferred_element_type=jnp.float32
     ).astype(jnp.bfloat16)
-    row_block = row_block.reshape(expert_count, per_device, MOST, model_width)
-    gate_proj = jnp.einsum("nemd,edf->nemf", row_block, w_gate, preferred_element_type=jnp.float32)
-    up_proj = jnp.einsum("nemd,edf->nemf", row_block, w_up, preferred_element_type=jnp.float32)
+    gate_proj = jnp.einsum("esmd,edf->esmf", row_block, w_gate, preferred_element_type=jnp.float32)
+    up_proj = jnp.einsum("esmd,edf->esmf", row_block, w_up, preferred_element_type=jnp.float32)
     hidden = (jax.nn.silu(gate_proj) * up_proj).astype(jnp.bfloat16)
-    down_out = jnp.einsum("nemf,efd->nemd", hidden, w_down, preferred_element_type=jnp.float32)
+    down_out = jnp.einsum("esmf,efd->esmd", hidden, w_down, preferred_element_type=jnp.float32)
     result = (slot_weight[..., None] * down_out).astype(jnp.bfloat16)
     partial_value = jnp.einsum(
-        "sqt,sqd->std",
-        picker,
-        result.reshape(expert_count, local_count, model_width),
-        preferred_element_type=jnp.float32,
+        "esmt,esmd->std", picker, result, preferred_element_type=jnp.float32
     )
     partial_value = partial_value.reshape(c_count, z_count, tok_rows, model_width)
     mixed, pair_tile = scatter_sums(

time: 97.4 us -> 95.1 us (0.976)
  matrix products: 16.9 us -> 14.4 us
    unnamed x9 -> x13, local copies, waits for them, and re-layouts: 4.42 us -> 6.94 us
    dot_general x4, matrix products: 16.6 us -> 14.2 us  [the longest x1 7.02 us: body(): jnp.einsum('esmt,esmd->std', picker, result, preferred_element_type=jnp.f...]
    convert_element_type x1 -> x0, local copies, waits for them, and re-layouts: 2.27 us -> none  [body(): result = (slot_weight[..., None] * down_out).astype(jnp.bfloat16)]
where the time goes in v11:
time: 95.1 us; the launch traced here: 94.7 us
  Pallas kernels  63.5 us (67%)
  matrix products  14.4 us (15%)
  local copies, waits for them, and re-layouts  9.28 us (10%)
  other arithmetic  6.69 us (7%)
    pallas_call x1, Pallas kernels, scatter_sums(): pl.pallas_call(functools.partial(combine_kernel, z_count, dp_count, seq_l...  32.3 us
    pallas_call x1, Pallas kernels, gather_blocks(): pl.pallas_call(functools.partial(dispatch_kernel, z_count, chunks), out_s...  31.3 us
    dot_general x1, matrix products, body(): jnp.einsum('esmt,esmd->std', picker, result, preferred_element_type=jnp.f...  7.02 us
    unnamed x13, local copies, waits for them, and re-layouts  6.94 us
    dot_general x1, matrix products, body(): jnp.einsum('esmt,std->esmd', picker, inputs_all, preferred_element_type=j...  3.3 us
    dot_general x1, matrix products, body(): jnp.einsum('esmd,edf->esmf', row_block, w_up, preferred_element_type=jnp....  1.99 us

profile of v11, /device:TPU:2, one launch (start us, length us, event | category | flops | bytes accessed | tf_op | source)
XLA Modules:
  0.0 94.7 jit_solution(16197050028327561825)
XLA Ops:
  0.6 0.7 broadcast_compare_fusion
  1.5 0.7 convert.13
  2.2 0.8 slice_reduce_fusion.1
  3.1 0.8 copy.36
  3.9 0.8 copy.35
  4.8 0.3 fusion.24
  5.2 1.1 %add_convert_fusion = bf16[64,2048]{1,0:T(8,128)(2,1)S(1)} fusion(bf16[64,2048]{1,0:T(8,128)(2,1)} %param.9, pred[64]{0:T(512)(128)(4,1)S(1)} %eq.47, bf16[2048]{0:T(1024)(128)(2,1)S(1)} %get-tuple-element.7, bf16[2048]{0:T(1024)(128)(2,1)S(1)} %get-tuple-element.6), kind=kLoop, calls=%fused_computation.29 | loop fusion | flops 655360 | bytes 532544 | tf_op jit(solution)/shard_map/convert_element_type | solution.py:301
  6.4 31.3 %shard_map.104 = bf16[16,64,2176]{2,1,0:T(8,128)(2,1)S(1)} custom-call(bf16[64,2176]{1,0:T(8,128)(2,1)S(1)} %pad_maximum_fusion.blk_ref), custom_call_target="tpu_custom_call" | custom-call | tf_op jit(solution)/shard_map/pallas_call | solution.py:116
  37.7 2.0 %copy-done.1 = bf16[16,64,2176]{2,1,0:T(8,128)(2,1)} copy-done((bf16[16,64,2176]{2,1,0:T(8,128)(2,1)}, bf16[16,64,2176]{2,1,0:T(8,128)(2,1)S(1)}, u32[]{:S(2)}) %copy-start.1) | copy-done | bytes 4456472
  39.8 0.5 fusion.28
  40.3 0.5 broadcast_divide_fusion
  40.8 0.2 copy.43
  40.9 0.2 fusion.27
  41.3 1.7 %select_reduce_fusion = f32[16,48]{1,0:T(8,128)S(1)} fusion(f32[16,64,8]{1,2,0:T(8,128)S(1)} %copy.43, s32[16,64,8]{1,2,0:T(8,128)S(1)} %copy.41), kind=kLoop, calls=%fused_computation.12 | loop fusion | flops 1178880 | bytes 68608 | tf_op jit(solution)/shard_map/reduce_sum | solution.py:326
  43.1 1.2 %fusion.14 = pred[16,48,64]{2,1,0:T(8,128)(4,1)S(1)} fusion(s32[16,64,8]{1,2,0:T(8,128)S(1)} %copy.41), kind=kLoop, calls=%fused_computation.14 | loop fusion | flops 737280 | bytes 81920 | tf_op jit(solution)/shard_map/reduce_or | solution.py:325
  44.3 3.3 %fusion.15 = bf16[2,16,24,2048]{3,2,0,1:T(8,128)(2,1)S(1)} fusion(pred[2,16,24,64]{3,2,0,1:T(8,128)(4,1)S(1)} %bitcast.43, bf16[16,64,2176]{2,1,0:T(8,128)(2,1)} %copy-done.1), kind=kOutput, calls=%fused_computation.15 | convolution fusion | flops 202899456 | bytes 7389184 | tf_op jit(solution)/shard_map/esmt,std->esmd/dot_general | solution.py:329
  47.7 1.8 %fusion.2 = f32[2,16,24,512]{3,2,1,0:T(8,128)S(1)} fusion(bf16[2,2048,512]{2,1,0:T(8,128)(2,1)S(1)} %copy-done.3, bf16[2,16,24,2048]{3,2,0,1:T(8,128)(2,1)S(1)} %fusion.15), kind=kOutput, calls=%fused_computation.4 | convolution fusion | flops 1610612736 | bytes 8912896 | tf_op jit(solution)/shard_map/esmd,edf->esmf/dot_general | solution.py:332
  49.6 0.3 copy-done.4
  49.9 2.0 %multiply_convert_fusion.1 = bf16[2,16,24,512]{3,2,1,0:T(8,128)(2,1)S(1)} fusion(f32[2,16,24,512]{3,2,1,0:T(8,128)S(1)} %fusion.2, bf16[2,2048,512]{2,1,0:T(8,128)(2,1)S(1)} %copy-done.4, bf16[2,16,24,2048]{3,2,0,1:T(8,128)(2,1)S(1)} %fusion.15), kind=kOutput, calls=%fused_computation.18 | convolution fusion | flops 1612972032 | bytes 9699328 | tf_op jit(solution)/shard_map/esmd,edf->esmf/dot_general | solution.py:333
  51.9 7.0 %bitcast_convert_fusion = bf16[16,64,2048]{2,1,0:T(8,128)(2,1)} fusion(pred[2,16,24,64]{3,2,0,1:T(8,128)(4,1)S(1)} %bitcast.44, bf16[2,512,2048]{2,1,0:T(8,128)(2,1)} %param.16, f32[2,16,24]{2,0,1:T(2,128)S(1)} %bitcast.45, bf16[2,16,24,512]{3,2,1,0:T(8,128)(2,1)S(1)} %multiply_convert_fusion.1), kind=kOutput, calls=%fused_computation | convolution fusion | flops 1817182208 | bytes 9227264 | tf_op jit(solution)/shard_map/esmt,esmd->std/dot_general | solution.py:337
  58.9 2.2 %copy-done = bf16[16,64,2048]{2,1,0:T(8,128)(2,1)S(1)} copy-done((bf16[16,64,2048]{2,1,0:T(8,128)(2,1)S(1)}, bf16[16,64,2048]{2,1,0:T(8,128)(2,1)}, u32[]{:S(2)}) %copy-start) | copy-done | bytes 4194328
  61.1 32.3 %shard_map.105 = (bf16[64,2048]{1,0:T(8,128)(2,1)S(1)}, f32[8,128]{1,0:T(8,128)S(1)}) custom-call(bf16[2,8,64,2048]{3,2,1,0:T(8,128)(2,1)S(1)} %bitcast.41, f32[1,2048]{1,0:T(1,128)S(1)} %bitcast.42), custom_call_target="tpu_custom_call" | custom-call | tf_op jit(solution)/shard_map/pallas_call | solution.py:262
  93.4 0.6 slice_reduce_fusion.2
  94.0 0.7 copy.62
  (19 shorter events, 1.1 us)
Async XLA Ops:
  37.7 2.0 %copy-start.1 = (bf16[16,64,2176]{2,1,0:T(8,128)(2,1)}, bf16[16,64,2176]{2,1,0:T(8,128)(2,1)S(1)}, u32[]{:S(2)}) copy-start(bf16[16,64,2176]{2,1,0:T(8,128)(2,1)S(1)} %shard_map.104) | copy-start | bytes 13369348
  44.3 3.5 %copy-start.3 = (bf16[2,2048,512]{2,1,0:T(8,128)(2,1)S(1)}, bf16[2,2048,512]{2,1,0:T(8,128)(2,1)}, u32[]{:S(2)}) copy-start(bf16[2,2048,512]{2,1,0:T(8,128)(2,1)} %param.14) | copy-start | bytes 12582916
  47.7 2.2 %copy-start.4 = (bf16[2,2048,512]{2,1,0:T(8,128)(2,1)S(1)}, bf16[2,2048,512]{2,1,0:T(8,128)(2,1)}, u32[]{:S(2)}) copy-start(bf16[2,2048,512]{2,1,0:T(8,128)(2,1)} %param.15) | copy-start | bytes 12582916
  51.9 7.0 %copy-start.2 = (f32[2048]{0:T(1024)S(1)}, f32[2048]{0:T(1024)}, u32[]{:S(2)}) copy-start(f32[2048]{0:T(1024)} %param.17) | copy-start | bytes 24580
  58.9 2.2 %copy-start = (bf16[16,64,2048]{2,1,0:T(8,128)(2,1)S(1)}, bf16[16,64,2048]{2,1,0:T(8,128)(2,1)}, u32[]{:S(2)}) copy-start(bf16[16,64,2048]{2,1,0:T(8,128)(2,1)} %bitcast_convert_fusion) | copy-start | bytes 12582916

commit v12 on v11

--- a/solution.py
+++ b/solution.py
@@ -116,22 +116,21 @@
     return pl.pallas_call(
         functools.partial(dispatch_kernel, z_count, chunks),
         out_shape=jax.ShapeDtypeStruct((count,) + block.shape, block.dtype),
-        in_specs=[pl.BlockSpec(memory_space=pltpu.VMEM)],
-        out_specs=pl.BlockSpec(memory_space=pltpu.VMEM),
+        in_specs=[pl.BlockSpec(memory_space=pl.ANY)],
+        out_specs=pl.BlockSpec(memory_space=pl.ANY),
         scratch_shapes=[
             pltpu.SemaphoreType.DMA((2 * count * chunks,)),
             pltpu.SemaphoreType.DMA((count * chunks,)),
             pltpu.SemaphoreType.DMA((1,)),
         ],
-        compiler_params=pltpu.CompilerParams(
-            collective_id=0, has_side_effects=True, vmem_limit_bytes=32 * 1024 * 1024
-        ),
+        compiler_params=pltpu.CompilerParams(collective_id=0, has_side_effects=True),
     )(block)
 
 
 def combine_kernel(
     z_count, dp_count, seq_len, chunks, part_ref, head_ref, out_ref, pair_out, pair_buf,
-    fwd_buf, bwd_buf, fwd_out, bwd_out, seq_out, seq_in, send_sem, recv_sem, seq_sem,
+    own_buf, fwd_buf, bwd_buf, fwd_out, bwd_out, seq_out, seq_in, send_sem, recv_sem, seq_sem,
+    own_sem,
 ):
     z = lax.axis_index("z")
     c = lax.axis_index("c")
@@ -185,13 +184,18 @@
 
     for n, dest in enumerate(order(-step)):
         send(part_ref.at[other, dest], pair_buf.at[n], n, pair_id)
+    loads = []
+    for n, dest in enumerate(order(step)):
+        load = pltpu.make_async_copy(part_ref.at[c, dest], own_buf.at[n], own_sem.at[n])
+        load.start()
+        loads.append(load)
+
     def own(dest, n, k):
         if k == 0:
+            loads[n].wait()
             arrive(pair_buf.at[n], n)
         rows = pl.ds(k * piece, piece)
-        return part_ref[c, dest, rows].astype(jnp.float32) + pair_buf[n, rows].astype(
-            jnp.float32
-        )
+        return own_buf[n, rows].astype(jnp.float32) + pair_buf[n, rows].astype(jnp.float32)
 
     fwd_sem = z_count
     bwd_sem = z_count + fwd_hops * chunks
@@ -265,9 +269,10 @@
             jax.ShapeDtypeStruct(block, partial.dtype),
             jax.ShapeDtypeStruct(tile, jnp.float32),
         ),
-        in_specs=[vmem, vmem],
+        in_specs=[pl.BlockSpec(memory_space=pl.ANY), vmem],
         out_specs=(vmem, vmem),
         scratch_shapes=[
+            pltpu.VMEM((z_count,) + block, partial.dtype),
             pltpu.VMEM((z_count,) + block, partial.dtype),
             pltpu.VMEM((fwd_hops,) + block, partial.dtype),
             pltpu.VMEM((bwd_hops,) + block, partial.dtype),
@@ -278,6 +283,7 @@
             pltpu.SemaphoreType.DMA((sems,)),
             pltpu.SemaphoreType.DMA((sems,)),
             pltpu.SemaphoreType.DMA((2,)),
+            pltpu.SemaphoreType.DMA((z_count,)),
         ],
         compiler_params=pltpu.CompilerParams(
             collective_id=1, has_side_effects=True, vmem_limit_bytes=48 * 1024 * 1024

time: 95.1 us -> 95.6 us (level)
  local copies, waits for them, and re-layouts: 9.28 us -> 7.25 us
  other arithmetic: 6.69 us -> 8.35 us
    unnamed x13 -> x11, local copies, waits for them, and re-layouts: 6.94 us -> 4.92 us
where the time goes in v12:
time: 95.6 us; the launch traced here: 95.2 us
  Pallas kernels  64.4 us (67%)
  matrix products  14.4 us (15%)
  other arithmetic  8.35 us (9%)
  local copies, waits for them, and re-layouts  7.25 us (8%)
    pallas_call x1, Pallas kernels, scatter_sums(): pl.pallas_call(functools.partial(combine_kernel, z_count, dp_count, seq_l...  32.3 us
    pallas_call x1, Pallas kernels, gather_blocks(): pl.pallas_call(functools.partial(dispatch_kernel, z_count, chunks), out_s...  32.1 us
    dot_general x1, matrix products, body(): jnp.einsum('esmt,esmd->std', picker, result, preferred_element_type=jnp.f...  7.03 us
    unnamed x11, local copies, waits for them, and re-layouts  4.92 us
    dot_general x1, matrix products, body(): jnp.einsum('esmt,std->esmd', picker, inputs_all, preferred_element_type=j...  3.3 us
    dot_general x1, matrix products, body(): jnp.einsum('esmd,edf->esmf', row_block, w_up, preferred_element_type=jnp....  1.99 us

profile of v12, /device:TPU:2, one launch (start us, length us, event | category | flops | bytes accessed | tf_op | source)
XLA Modules:
  0.0 95.2 jit_solution(7342112159819287358)
XLA Ops:
  0.6 0.7 broadcast_compare_fusion
  1.5 0.7 convert.13
  2.2 0.8 slice_reduce_fusion.1
  3.1 0.8 copy.36
  3.9 0.8 copy.35
  4.8 0.3 fusion.24
  5.2 1.1 %add_convert_fusion = bf16[64,2048]{1,0:T(8,128)(2,1)S(1)} fusion(bf16[64,2048]{1,0:T(8,128)(2,1)} %param.9, pred[64]{0:T(512)(128)(4,1)S(1)} %eq.47, bf16[2048]{0:T(1024)(128)(2,1)S(1)} %get-tuple-element.7, bf16[2048]{0:T(1024)(128)(2,1)S(1)} %get-tuple-element.6), kind=kLoop, calls=%fused_computation.29 | loop fusion | flops 655360 | bytes 532544 | tf_op jit(solution)/shard_map/convert_element_type | solution.py:307
  6.3 0.7 pad_maximum_fusion.blk_ref
  7.1 32.1 %shard_map.104 = bf16[16,64,2176]{2,1,0:T(8,128)(2,1)} custom-call(bf16[64,2176]{1,0:T(8,128)(2,1)} %pad_maximum_fusion.blk_ref), custom_call_target="tpu_custom_call" | custom-call | tf_op jit(solution)/shard_map/pallas_call | solution.py:116
  39.2 1.0 %slice_convert_fusion = s32[16,64,32]{2,1,0:T(8,128)S(1)} fusion(bf16[16,64,2176]{2,1,0:T(8,128)(2,1)} %shard_map.104), kind=kLoop, calls=%fused_computation.32 | loop fusion | flops 32768 | bytes 196608 | tf_op jit(solution)/shard_map/convert_element_type | solution.py:316
  40.2 0.5 fusion.28
  40.7 0.5 broadcast_divide_fusion
  41.3 0.2 fusion.27
  41.7 1.7 %select_reduce_fusion = f32[16,48]{1,0:T(8,128)S(1)} fusion(f32[16,64,8]{1,2,0:T(8,128)S(1)} %copy.43, s32[16,64,8]{1,2,0:T(8,128)S(1)} %copy.41), kind=kLoop, calls=%fused_computation.12 | loop fusion | flops 1178880 | bytes 68608 | tf_op jit(solution)/shard_map/reduce_sum | solution.py:332
  43.5 1.2 %fusion.14 = pred[16,48,64]{2,1,0:T(8,128)(4,1)S(1)} fusion(s32[16,64,8]{1,2,0:T(8,128)S(1)} %copy.41), kind=kLoop, calls=%fused_computation.14 | loop fusion | flops 737280 | bytes 81920 | tf_op jit(solution)/shard_map/reduce_or | solution.py:331
  44.7 3.3 %fusion.15 = bf16[2,16,24,2048]{3,2,0,1:T(8,128)(2,1)S(1)} fusion(pred[2,16,24,64]{3,2,0,1:T(8,128)(4,1)S(1)} %bitcast.43, bf16[16,64,2176]{2,1,0:T(8,128)(2,1)} %shard_map.104), kind=kOutput, calls=%fused_computation.15 | convolution fusion | flops 202899456 | bytes 7389184 | tf_op jit(solution)/shard_map/esmt,std->esmd/dot_general | solution.py:335
  48.1 1.8 %fusion.2 = f32[2,16,24,512]{3,2,1,0:T(8,128)S(1)} fusion(bf16[2,2048,512]{2,1,0:T(8,128)(2,1)S(1)} %copy-done.2, bf16[2,16,24,2048]{3,2,0,1:T(8,128)(2,1)S(1)} %fusion.15), kind=kOutput, calls=%fused_computation.4 | convolution fusion | flops 1610612736 | bytes 8912896 | tf_op jit(solution)/shard_map/esmd,edf->esmf/dot_general | solution.py:338
  50.0 0.3 copy-done.3
  50.3 2.0 %multiply_convert_fusion.1 = bf16[2,16,24,512]{3,2,1,0:T(8,128)(2,1)S(1)} fusion(f32[2,16,24,512]{3,2,1,0:T(8,128)S(1)} %fusion.2, bf16[2,2048,512]{2,1,0:T(8,128)(2,1)S(1)} %copy-done.3, bf16[2,16,24,2048]{3,2,0,1:T(8,128)(2,1)S(1)} %fusion.15), kind=kOutput, calls=%fused_computation.18 | convolution fusion | flops 1612972032 | bytes 9699328 | tf_op jit(solution)/shard_map/esmd,edf->esmf/dot_general | solution.py:339
  52.3 7.0 %bitcast_convert_fusion = bf16[16,64,2048]{2,1,0:T(8,128)(2,1)} fusion(pred[2,16,24,64]{3,2,0,1:T(8,128)(4,1)S(1)} %bitcast.44, bf16[2,512,2048]{2,1,0:T(8,128)(2,1)} %param.16, f32[2,16,24]{2,0,1:T(2,128)S(1)} %bitcast.45, bf16[2,16,24,512]{3,2,1,0:T(8,128)(2,1)S(1)} %multiply_convert_fusion.1), kind=kOutput, calls=%fused_computation | convolution fusion | flops 1817182208 | bytes 9227264 | tf_op jit(solution)/shard_map/esmt,esmd->std/dot_general | solution.py:343
  59.4 2.2 %copy-done = bf16[16,64,2048]{2,1,0:T(8,128)(2,1)S(1)} copy-done((bf16[16,64,2048]{2,1,0:T(8,128)(2,1)S(1)}, bf16[16,64,2048]{2,1,0:T(8,128)(2,1)}, u32[]{:S(2)}) %copy-start) | copy-done | bytes 4194328
  61.6 32.3 %shard_map.105 = (bf16[64,2048]{1,0:T(8,128)(2,1)S(1)}, f32[8,128]{1,0:T(8,128)S(1)}) custom-call(bf16[2,8,64,2048]{3,2,1,0:T(8,128)(2,1)S(1)} %bitcast.41, f32[1,2048]{1,0:T(1,128)S(1)} %bitcast.42), custom_call_target="tpu_custom_call" | custom-call | tf_op jit(solution)/shard_map/pallas_call | solution.py:266
  93.9 0.6 slice_reduce_fusion.2
  94.5 0.7 copy.62
  (17 shorter events, 1.2 us)
Async XLA Ops:
  44.7 3.5 %copy-start.2 = (bf16[2,2048,512]{2,1,0:T(8,128)(2,1)S(1)}, bf16[2,2048,512]{2,1,0:T(8,128)(2,1)}, u32[]{:S(2)}) copy-start(bf16[2,2048,512]{2,1,0:T(8,128)(2,1)} %param.14) | copy-start | bytes 12582916
  48.1 2.2 %copy-start.3 = (bf16[2,2048,512]{2,1,0:T(8,128)(2,1)S(1)}, bf16[2,2048,512]{2,1,0:T(8,128)(2,1)}, u32[]{:S(2)}) copy-start(bf16[2,2048,512]{2,1,0:T(8,128)(2,1)} %param.15) | copy-start | bytes 12582916
  52.3 7.0 %copy-start.1 = (f32[2048]{0:T(1024)S(1)}, f32[2048]{0:T(1024)}, u32[]{:S(2)}) copy-start(f32[2048]{0:T(1024)} %param.17) | copy-start | bytes 24580
  59.4 2.2 %copy-start = (bf16[16,64,2048]{2,1,0:T(8,128)(2,1)S(1)}, bf16[16,64,2048]{2,1,0:T(8,128)(2,1)}, u32[]{:S(2)}) copy-start(bf16[16,64,2048]{2,1,0:T(8,128)(2,1)} %bitcast_convert_fusion) | copy-start | bytes 12582916

commit v13 on v11

--- a/solution.py
+++ b/solution.py
@@ -334,6 +334,7 @@
     hidden = (jax.nn.silu(gate_proj) * up_proj).astype(jnp.bfloat16)
     down_out = jnp.einsum("esmf,efd->esmd", hidden, w_down, preferred_element_type=jnp.float32)
     result = (slot_weight[..., None] * down_out).astype(jnp.bfloat16)
+    result = lax.optimization_barrier(result)
     partial_value = jnp.einsum(
         "esmt,esmd->std", picker, result, preferred_element_type=jnp.float32
     )

time: 95.1 us -> 89.3 us (0.939)
  matrix products: 14.4 us -> 10.5 us
  local copies, waits for them, and re-layouts: 9.28 us -> 7.27 us
    dot_general x1, matrix products: 7.02 us -> 1.3 us  [body(): jnp.einsum('esmt,esmd->std', picker, result, preferred_element_type=jnp.f...]
    unnamed x13, local copies, waits for them, and re-layouts: 6.94 us -> 4.94 us
    dot_general x0 -> x1, matrix products: none -> 1.82 us  [body(): jnp.einsum('esmf,efd->esmd', hidden, w_down, preferred_element_type=jnp.f...]
where the time goes in v13:
time: 89.3 us; the launch traced here: 89 us
  Pallas kernels  63.7 us (71%)
  matrix products  10.5 us (12%)
  local copies, waits for them, and re-layouts  7.27 us (8%)
  other arithmetic  6.68 us (7%)
    pallas_call x1, Pallas kernels, scatter_sums(): pl.pallas_call(functools.partial(combine_kernel, z_count, dp_count, seq_l...  32.4 us
    pallas_call x1, Pallas kernels, gather_blocks(): pl.pallas_call(functools.partial(dispatch_kernel, z_count, chunks), out_s...  31.3 us
    unnamed x13, local copies, waits for them, and re-layouts  4.94 us
    dot_general x1, matrix products, body(): jnp.einsum('esmt,std->esmd', picker, inputs_all, preferred_element_type=j...  3.3 us
    dot_general x1, matrix products, body(): jnp.einsum('esmd,edf->esmf', row_block, w_up, preferred_element_type=jnp....  2 us
    dot_general x1, matrix products, body(): jnp.einsum('esmd,edf->esmf', row_block, w_gate, preferred_element_type=jn...  1.84 us
    dot_general x1, matrix products, body(): jnp.einsum('esmf,efd->esmd', hidden, w_down, preferred_element_type=jnp.f...  1.82 us

profile of v13, /device:TPU:2, one launch (start us, length us, event | category | flops | bytes accessed | tf_op | source)
XLA Modules:
  0.0 89.0 jit_solution(18367343753112755635)
XLA Ops:
  0.6 0.7 broadcast_compare_fusion
  1.5 0.7 convert.13
  2.2 0.8 slice_reduce_fusion.1
  3.1 0.8 copy.36
  3.9 0.8 copy.35
  4.8 0.3 fusion.24
  5.2 1.1 %add_convert_fusion = bf16[64,2048]{1,0:T(8,128)(2,1)S(1)} fusion(bf16[64,2048]{1,0:T(8,128)(2,1)} %param.9, pred[64]{0:T(512)(128)(4,1)S(1)} %eq.47, bf16[2048]{0:T(1024)(128)(2,1)S(1)} %get-tuple-element.7, bf16[2048]{0:T(1024)(128)(2,1)S(1)} %get-tuple-element.6), kind=kLoop, calls=%fused_computation.29 | loop fusion | flops 655360 | bytes 532544 | tf_op jit(solution)/shard_map/convert_element_type | solution.py:301
  6.4 31.3 %shard_map.104 = bf16[16,64,2176]{2,1,0:T(8,128)(2,1)S(1)} custom-call(bf16[64,2176]{1,0:T(8,128)(2,1)S(1)} %pad_maximum_fusion.blk_ref), custom_call_target="tpu_custom_call" | custom-call | tf_op jit(solution)/shard_map/pallas_call | solution.py:116
  37.7 2.0 %copy-done = bf16[16,64,2176]{2,1,0:T(8,128)(2,1)} copy-done((bf16[16,64,2176]{2,1,0:T(8,128)(2,1)}, bf16[16,64,2176]{2,1,0:T(8,128)(2,1)S(1)}, u32[]{:S(2)}) %copy-start) | copy-done | bytes 4456472
  39.8 0.5 fusion.28
  40.3 0.5 broadcast_divide_fusion
  40.9 0.2 fusion.27
  41.3 1.6 %select_reduce_fusion = f32[16,48]{1,0:T(8,128)S(1)} fusion(f32[16,64,8]{1,2,0:T(8,128)S(1)} %copy.43, s32[16,64,8]{1,2,0:T(8,128)S(1)} %copy.41), kind=kLoop, calls=%fused_computation.12 | loop fusion | flops 1178880 | bytes 68608 | tf_op jit(solution)/shard_map/reduce_sum | solution.py:326
  43.1 1.2 %fusion.14 = pred[16,48,64]{2,1,0:T(8,128)(4,1)S(1)} fusion(s32[16,64,8]{1,2,0:T(8,128)S(1)} %copy.41), kind=kLoop, calls=%fused_computation.14 | loop fusion | flops 737280 | bytes 81920 | tf_op jit(solution)/shard_map/reduce_or | solution.py:325
  44.3 3.3 %fusion.15 = bf16[2,16,24,2048]{3,2,0,1:T(8,128)(2,1)S(1)} fusion(pred[2,16,24,64]{3,2,0,1:T(8,128)(4,1)S(1)} %bitcast.42, bf16[16,64,2176]{2,1,0:T(8,128)(2,1)} %copy-done), kind=kOutput, calls=%fused_computation.15 | convolution fusion | flops 202899456 | bytes 7389184 | tf_op jit(solution)/shard_map/esmt,std->esmd/dot_general | solution.py:329
  47.7 1.8 %fusion.2 = f32[2,16,24,512]{3,2,1,0:T(8,128)S(1)} fusion(bf16[2,2048,512]{2,1,0:T(8,128)(2,1)S(1)} %copy-done.2, bf16[2,16,24,2048]{3,2,0,1:T(8,128)(2,1)S(1)} %fusion.15), kind=kOutput, calls=%fused_computation.4 | convolution fusion | flops 1610612736 | bytes 8912896 | tf_op jit(solution)/shard_map/esmd,edf->esmf/dot_general | solution.py:332
  49.5 0.3 copy-done.3
  49.9 2.0 %multiply_convert_fusion.1 = bf16[2,16,24,512]{3,2,1,0:T(8,128)(2,1)S(1)} fusion(f32[2,16,24,512]{3,2,1,0:T(8,128)S(1)} %fusion.2, bf16[2,2048,512]{2,1,0:T(8,128)(2,1)S(1)} %copy-done.3, bf16[2,16,24,2048]{3,2,0,1:T(8,128)(2,1)S(1)} %fusion.15), kind=kOutput, calls=%fused_computation.18 | convolution fusion | flops 1612972032 | bytes 9699328 | tf_op jit(solution)/shard_map/esmd,edf->esmf/dot_general | solution.py:333
  51.9 0.2 copy-done.4
  52.1 1.8 %multiply_convert_fusion = bf16[2,16,24,2048]{3,2,0,1:T(8,128)(2,1)S(1)} fusion(bf16[2,512,2048]{2,1,0:T(8,128)(2,1)S(1)} %copy-done.4, f32[2,16,24]{2,0,1:T(2,128)S(1)} %bitcast.44, bf16[2,16,24,512]{3,2,1,0:T(8,128)(2,1)S(1)} %multiply_convert_fusion.1), kind=kOutput, calls=%fused_computation.1 | convolution fusion | flops 1613758464 | bytes 8129536 | tf_op jit(solution)/shard_map/esmf,efd->esmd/dot_general | solution.py:335
  53.9 1.3 %bitcast_convert_fusion = bf16[16,64,2048]{2,1,0:T(8,128)(2,1)S(1)} fusion(pred[2,16,24,64]{3,2,0,1:T(8,128)(4,1)S(1)} %bitcast.43, bf16[2,16,24,2048]{3,2,0,1:T(8,128)(2,1)S(1)} %multiply_convert_fusion), kind=kOutput, calls=%fused_computation | convolution fusion | flops 203423744 | bytes 7389184 | tf_op jit(solution)/shard_map/esmt,esmd->std/dot_general | solution.py:338
  55.2 32.4 %shard_map.105 = (bf16[64,2048]{1,0:T(8,128)(2,1)S(1)}, f32[8,128]{1,0:T(8,128)S(1)}) custom-call(bf16[2,8,64,2048]{3,2,1,0:T(8,128)(2,1)S(1)} %bitcast.40, f32[1,2048]{1,0:T(1,128)S(1)} %bitcast.41), custom_call_target="tpu_custom_call" | custom-call | tf_op jit(solution)/shard_map/pallas_call | solution.py:262
  87.7 0.6 slice_reduce_fusion.2
  88.3 0.7 copy.60
  (20 shorter events, 1.2 us)
Async XLA Ops:
  37.7 2.0 %copy-start = (bf16[16,64,2176]{2,1,0:T(8,128)(2,1)}, bf16[16,64,2176]{2,1,0:T(8,128)(2,1)S(1)}, u32[]{:S(2)}) copy-start(bf16[16,64,2176]{2,1,0:T(8,128)(2,1)S(1)} %shard_map.104) | copy-start | bytes 13369348
  44.2 3.5 %copy-start.2 = (bf16[2,2048,512]{2,1,0:T(8,128)(2,1)S(1)}, bf16[2,2048,512]{2,1,0:T(8,128)(2,1)}, u32[]{:S(2)}) copy-start(bf16[2,2048,512]{2,1,0:T(8,128)(2,1)} %param.14) | copy-start | bytes 12582916
  47.7 2.2 %copy-start.3 = (bf16[2,2048,512]{2,1,0:T(8,128)(2,1)S(1)}, bf16[2,2048,512]{2,1,0:T(8,128)(2,1)}, u32[]{:S(2)}) copy-start(bf16[2,2048,512]{2,1,0:T(8,128)(2,1)} %param.15) | copy-start | bytes 12582916
  49.9 2.2 %copy-start.4 = (bf16[2,512,2048]{2,1,0:T(8,128)(2,1)S(1)}, bf16[2,512,2048]{2,1,0:T(8,128)(2,1)}, u32[]{:S(2)}) copy-start(bf16[2,512,2048]{2,1,0:T(8,128)(2,1)} %param.16) | copy-start | bytes 12582916
  53.9 1.3 %copy-start.1 = (f32[2048]{0:T(1024)S(1)}, f32[2048]{0:T(1024)}, u32[]{:S(2)}) copy-start(f32[2048]{0:T(1024)} %param.17) | copy-start | bytes 24580

commit v14 on v13

--- a/solution.py
+++ b/solution.py
@@ -116,16 +116,14 @@
     return pl.pallas_call(
         functools.partial(dispatch_kernel, z_count, chunks),
         out_shape=jax.ShapeDtypeStruct((count,) + block.shape, block.dtype),
-        in_specs=[pl.BlockSpec(memory_space=pltpu.VMEM)],
-        out_specs=pl.BlockSpec(memory_space=pltpu.VMEM),
+        in_specs=[pl.BlockSpec(memory_space=pl.ANY)],
+        out_specs=pl.BlockSpec(memory_space=pl.ANY),
         scratch_shapes=[
             pltpu.SemaphoreType.DMA((2 * count * chunks,)),
             pltpu.SemaphoreType.DMA((count * chunks,)),
             pltpu.SemaphoreType.DMA((1,)),
         ],
-        compiler_params=pltpu.CompilerParams(
-            collective_id=0, has_side_effects=True, vmem_limit_bytes=32 * 1024 * 1024
-        ),
+        compiler_params=pltpu.CompilerParams(collective_id=0, has_side_effects=True),
     )(block)
 
 

time: 89.3 us -> 89.8 us (level)
  local copies, waits for them, and re-layouts: 7.27 us -> 5.26 us
  other arithmetic: 6.68 us -> 8.33 us
    unnamed x13 -> x11, local copies, waits for them, and re-layouts: 4.94 us -> 2.92 us
    convert_element_type x1, other arithmetic: 0.05 us -> 1 us  [body(): gathered[:, :, model_width:model_width + 4 * top_count].astype(jnp.int32)]
where the time goes in v14:
time: 89.8 us; the launch traced here: 89.5 us
  Pallas kernels  64.5 us (72%)
  matrix products  10.6 us (12%)
  other arithmetic  8.33 us (9%)
  local copies, waits for them, and re-layouts  5.26 us (6%)
    pallas_call x1, Pallas kernels, scatter_sums(): pl.pallas_call(functools.partial(combine_kernel, z_count, dp_count, seq_l...  32.4 us
    pallas_call x1, Pallas kernels, gather_blocks(): pl.pallas_call(functools.partial(dispatch_kernel, z_count, chunks), out_s...  32.1 us
    dot_general x1, matrix products, body(): jnp.einsum('esmt,std->esmd', picker, inputs_all, preferred_element_type=j...  3.3 us
    unnamed x11, local copies, waits for them, and re-layouts  2.92 us
    dot_general x1, matrix products, body(): jnp.einsum('esmd,edf->esmf', row_block, w_up, preferred_element_type=jnp....  1.99 us
    dot_general x1, matrix products, body(): jnp.einsum('esmf,efd->esmd', hidden, w_down, preferred_element_type=jnp.f...  1.85 us
    dot_general x1, matrix products, body(): jnp.einsum('esmd,edf->esmf', row_block, w_gate, preferred_element_type=jn...  1.84 us

profile of v14, /device:TPU:2, one launch (start us, length us, event | category | flops | bytes accessed | tf_op | source)
XLA Modules:
  0.0 89.5 jit_solution(17702447239935902714)
XLA Ops:
  0.6 0.7 broadcast_compare_fusion
  1.5 0.7 convert.13
  2.2 0.8 slice_reduce_fusion.1
  3.1 0.8 copy.36
  3.9 0.8 copy.35
  4.8 0.3 fusion.24
  5.2 1.1 %add_convert_fusion = bf16[64,2048]{1,0:T(8,128)(2,1)S(1)} fusion(bf16[64,2048]{1,0:T(8,128)(2,1)} %param.9, pred[64]{0:T(512)(128)(4,1)S(1)} %eq.47, bf16[2048]{0:T(1024)(128)(2,1)S(1)} %get-tuple-element.7, bf16[2048]{0:T(1024)(128)(2,1)S(1)} %get-tuple-element.6), kind=kLoop, calls=%fused_computation.29 | loop fusion | flops 655360 | bytes 532544 | tf_op jit(solution)/shard_map/convert_element_type | solution.py:299
  6.3 0.7 pad_maximum_fusion.blk_ref
  7.1 32.1 %shard_map.104 = bf16[16,64,2176]{2,1,0:T(8,128)(2,1)} custom-call(bf16[64,2176]{1,0:T(8,128)(2,1)} %pad_maximum_fusion.blk_ref), custom_call_target="tpu_custom_call" | custom-call | tf_op jit(solution)/shard_map/pallas_call | solution.py:116
  39.2 1.0 %slice_convert_fusion = s32[16,64,32]{2,1,0:T(8,128)S(1)} fusion(bf16[16,64,2176]{2,1,0:T(8,128)(2,1)} %shard_map.104), kind=kLoop, calls=%fused_computation.32 | loop fusion | flops 32768 | bytes 196608 | tf_op jit(solution)/shard_map/convert_element_type | solution.py:308
  40.2 0.5 fusion.28
  40.7 0.5 broadcast_divide_fusion
  41.3 0.2 fusion.27
  41.7 1.6 %select_reduce_fusion = f32[16,48]{1,0:T(8,128)S(1)} fusion(f32[16,64,8]{1,2,0:T(8,128)S(1)} %copy.43, s32[16,64,8]{1,2,0:T(8,128)S(1)} %copy.41), kind=kLoop, calls=%fused_computation.12 | loop fusion | flops 1178880 | bytes 68608 | tf_op jit(solution)/shard_map/reduce_sum | solution.py:324
  43.5 1.2 %fusion.14 = pred[16,48,64]{2,1,0:T(8,128)(4,1)S(1)} fusion(s32[16,64,8]{1,2,0:T(8,128)S(1)} %copy.41), kind=kLoop, calls=%fused_computation.14 | loop fusion | flops 737280 | bytes 81920 | tf_op jit(solution)/shard_map/reduce_or | solution.py:323
  44.7 3.3 %fusion.15 = bf16[2,16,24,2048]{3,2,0,1:T(8,128)(2,1)S(1)} fusion(pred[2,16,24,64]{3,2,0,1:T(8,128)(4,1)S(1)} %bitcast.42, bf16[16,64,2176]{2,1,0:T(8,128)(2,1)} %shard_map.104), kind=kOutput, calls=%fused_computation.15 | convolution fusion | flops 202899456 | bytes 7389184 | tf_op jit(solution)/shard_map/esmt,std->esmd/dot_general | solution.py:327
  48.1 1.8 %fusion.2 = f32[2,16,24,512]{3,2,1,0:T(8,128)S(1)} fusion(bf16[2,2048,512]{2,1,0:T(8,128)(2,1)S(1)} %copy-done.1, bf16[2,16,24,2048]{3,2,0,1:T(8,128)(2,1)S(1)} %fusion.15), kind=kOutput, calls=%fused_computation.4 | convolution fusion | flops 1610612736 | bytes 8912896 | tf_op jit(solution)/shard_map/esmd,edf->esmf/dot_general | solution.py:330
  50.0 0.3 copy-done.2
  50.3 2.0 %multiply_convert_fusion.1 = bf16[2,16,24,512]{3,2,1,0:T(8,128)(2,1)S(1)} fusion(f32[2,16,24,512]{3,2,1,0:T(8,128)S(1)} %fusion.2, bf16[2,2048,512]{2,1,0:T(8,128)(2,1)S(1)} %copy-done.2, bf16[2,16,24,2048]{3,2,0,1:T(8,128)(2,1)S(1)} %fusion.15), kind=kOutput, calls=%fused_computation.18 | convolution fusion | flops 1612972032 | bytes 9699328 | tf_op jit(solution)/shard_map/esmd,edf->esmf/dot_general | solution.py:331
  52.5 1.8 %multiply_convert_fusion = bf16[2,16,24,2048]{3,2,0,1:T(8,128)(2,1)S(1)} fusion(bf16[2,512,2048]{2,1,0:T(8,128)(2,1)S(1)} %copy-done.3, f32[2,16,24]{2,0,1:T(2,128)S(1)} %bitcast.44, bf16[2,16,24,512]{3,2,1,0:T(8,128)(2,1)S(1)} %multiply_convert_fusion.1), kind=kOutput, calls=%fused_computation.1 | convolution fusion | flops 1613758464 | bytes 8129536 | tf_op jit(solution)/shard_map/esmf,efd->esmd/dot_general | solution.py:333
  54.4 1.3 %bitcast_convert_fusion = bf16[16,64,2048]{2,1,0:T(8,128)(2,1)S(1)} fusion(pred[2,16,24,64]{3,2,0,1:T(8,128)(4,1)S(1)} %bitcast.43, bf16[2,16,24,2048]{3,2,0,1:T(8,128)(2,1)S(1)} %multiply_convert_fusion), kind=kOutput, calls=%fused_computation | convolution fusion | flops 203423744 | bytes 7389184 | tf_op jit(solution)/shard_map/esmt,esmd->std/dot_general | solution.py:336
  55.7 32.4 %shard_map.105 = (bf16[64,2048]{1,0:T(8,128)(2,1)S(1)}, f32[8,128]{1,0:T(8,128)S(1)}) custom-call(bf16[2,8,64,2048]{3,2,1,0:T(8,128)(2,1)S(1)} %bitcast.40, f32[1,2048]{1,0:T(1,128)S(1)} %bitcast.41), custom_call_target="tpu_custom_call" | custom-call | tf_op jit(solution)/shard_map/pallas_call | solution.py:260
  88.1 0.6 slice_reduce_fusion.2
  88.7 0.7 copy.60
  (18 shorter events, 1.4 us)
Async XLA Ops:
  44.7 3.5 %copy-start.1 = (bf16[2,2048,512]{2,1,0:T(8,128)(2,1)S(1)}, bf16[2,2048,512]{2,1,0:T(8,128)(2,1)}, u32[]{:S(2)}) copy-start(bf16[2,2048,512]{2,1,0:T(8,128)(2,1)} %param.14) | copy-start | bytes 12582916
  48.1 2.2 %copy-start.2 = (bf16[2,2048,512]{2,1,0:T(8,128)(2,1)S(1)}, bf16[2,2048,512]{2,1,0:T(8,128)(2,1)}, u32[]{:S(2)}) copy-start(bf16[2,2048,512]{2,1,0:T(8,128)(2,1)} %param.15) | copy-start | bytes 12582916
  50.3 2.2 %copy-start.3 = (bf16[2,512,2048]{2,1,0:T(8,128)(2,1)S(1)}, bf16[2,512,2048]{2,1,0:T(8,128)(2,1)}, u32[]{:S(2)}) copy-start(bf16[2,512,2048]{2,1,0:T(8,128)(2,1)} %param.16) | copy-start | bytes 12582916
  54.4 1.3 %copy-start = (f32[2048]{0:T(1024)S(1)}, f32[2048]{0:T(1024)}, u32[]{:S(2)}) copy-start(f32[2048]{0:T(1024)} %param.17) | copy-start | bytes 24580

commit v15 on v13

--- a/solution.py
+++ b/solution.py
@@ -36,7 +36,9 @@
 MESH = pl.DeviceIdType.MESH
 
 
-def dispatch_kernel(z_count, chunks, blk_ref, out_ref, send_sem, recv_sem, local_sem):
+def dispatch_kernel(
+    z_count, chunks, blk_ref, rt_ref, out_ref, rt_out, send_sem, recv_sem, rt_sem, local_sem
+):
     z = lax.axis_index("z")
     c = lax.axis_index("c")
     row = lax.axis_index("dp")
@@ -55,39 +57,50 @@
     mine = c * z_count + z
     local = pltpu.make_async_copy(blk_ref, out_ref.at[mine], local_sem.at[0])
     local.start()
+    local_rt = pltpu.make_async_copy(rt_ref, rt_out.at[mine], local_sem.at[1])
+    local_rt.start()
     sends = []
 
     def part(ref, k):
         return ref.at[pl.ds(k * piece, piece)]
 
-    def send(src, slot, k, target):
+    def remote(src, dst, sem, target):
         copy = pltpu.make_async_remote_copy(
-            src_ref=part(src, k),
-            dst_ref=part(out_ref.at[slot], k),
+            src_ref=src,
+            dst_ref=dst,
             send_sem=send_sem.at[len(sends)],
-            recv_sem=recv_sem.at[slot * chunks + k],
+            recv_sem=sem,
             device_id=target,
             device_id_type=MESH,
         )
         copy.start()
         sends.append(copy)
 
-    def arrive(slot, k):
-        view = part(out_ref.at[slot], k)
+    def send(src, rt_src, slot, k, target):
+        remote(part(src, k), part(out_ref.at[slot], k), recv_sem.at[slot * chunks + k], target)
+        if k == 0:
+            remote(rt_src, rt_out.at[slot], rt_sem.at[slot], target)
+
+    def wait_for(view, sem):
         pltpu.make_async_remote_copy(
             src_ref=view,
             dst_ref=view,
             send_sem=send_sem.at[0],
-            recv_sem=recv_sem.at[slot * chunks + k],
+            recv_sem=sem,
             device_id=pair_id,
             device_id_type=MESH,
         ).wait_recv()
 
+    def arrive(slot, k):
+        wait_for(part(out_ref.at[slot], k), recv_sem.at[slot * chunks + k])
+        if k == 0:
+            wait_for(rt_out.at[slot], rt_sem.at[slot])
+
     for k in range(chunks):
-        send(blk_ref, mine, k, fwd_id)
-        send(blk_ref, mine, k, bwd_id)
+        send(blk_ref, rt_ref, mine, k, fwd_id)
+        send(blk_ref, rt_ref, mine, k, bwd_id)
     for k in range(chunks):
-        send(blk_ref, mine, k, pair_id)
+        send(blk_ref, rt_ref, mine, k, pair_id)
     fwd_hops = z_count // 2
     bwd_hops = z_count - 1 - fwd_hops
     for hop in range(1, fwd_hops + 1):
@@ -95,38 +108,44 @@
             slot = c * z_count + lax.rem(z - step * hop + 2 * z_count, z_count)
             arrive(slot, k)
             if hop < fwd_hops:
-                send(out_ref.at[slot], slot, k, fwd_id)
-            send(out_ref.at[slot], slot, k, pair_id)
+                send(out_ref.at[slot], rt_out.at[slot], slot, k, fwd_id)
+            send(out_ref.at[slot], rt_out.at[slot], slot, k, pair_id)
             if hop <= bwd_hops:
                 slot = c * z_count + lax.rem(z + step * hop + 2 * z_count, z_count)
                 arrive(slot, k)
                 if hop < bwd_hops:
-                    send(out_ref.at[slot], slot, k, bwd_id)
-                send(out_ref.at[slot], slot, k, pair_id)
+                    send(out_ref.at[slot], rt_out.at[slot], slot, k, bwd_id)
+                send(out_ref.at[slot], rt_out.at[slot], slot, k, pair_id)
     for zz in range(z_count):
         for k in range(chunks):
             arrive(other * z_count + zz, k)
     local.wait()
+    local_rt.wait()
     for copy in sends:
         copy.wait_send()
 
 
-def gather_blocks(block, z_count, chunks):
+def gather_blocks(block, route_tile, z_count, chunks):
     count = 2 * z_count
+    vmem = pl.BlockSpec(memory_space=pltpu.VMEM)
     return pl.pallas_call(
         functools.partial(dispatch_kernel, z_count, chunks),
-        out_shape=jax.ShapeDtypeStruct((count,) + block.shape, block.dtype),
-        in_specs=[pl.BlockSpec(memory_space=pltpu.VMEM)],
-        out_specs=pl.BlockSpec(memory_space=pltpu.VMEM),
+        out_shape=(
+            jax.ShapeDtypeStruct((count,) + block.shape, block.dtype),
+            jax.ShapeDtypeStruct((count,) + route_tile.shape, route_tile.dtype),
+        ),
+        in_specs=[vmem, vmem],
+        out_specs=(vmem, vmem),
         scratch_shapes=[
-            pltpu.SemaphoreType.DMA((2 * count * chunks,)),
+            pltpu.SemaphoreType.DMA((3 * count * chunks,)),
             pltpu.SemaphoreType.DMA((count * chunks,)),
-            pltpu.SemaphoreType.DMA((1,)),
+            pltpu.SemaphoreType.DMA((count,)),
+            pltpu.SemaphoreType.DMA((2,)),
         ],
         compiler_params=pltpu.CompilerParams(
             collective_id=0, has_side_effects=True, vmem_limit_bytes=32 * 1024 * 1024
         ),
-    )(block)
+    )(block, route_tile)
 
 
 def combine_kernel(
@@ -303,11 +322,9 @@
     routes = jnp.concatenate(
         [expert_ids, rank_in, gate_fixed // 256, gate_fixed % 256], axis=1
     ).astype(jnp.bfloat16)
-    routes = jnp.pad(routes, ((0, 0), (0, 128 - 4 * top_count)))
-    block = jnp.concatenate([inputs, routes], axis=1)
-    gathered = gather_blocks(block, z_count, 2)
-    inputs_all = gathered[:, :, :model_width]
-    routes_all = gathered[:, :, model_width : model_width + 4 * top_count].astype(jnp.int32)
+    route_tile = routes.reshape(-1, 128)
+    inputs_all, routes_all = gather_blocks(inputs, route_tile, z_count, 2)
+    routes_all = routes_all.reshape(expert_count, tok_rows, 4 * top_count).astype(jnp.int32)
     ids_cube = routes_all[..., :top_count]
     rank_cube = routes_all[..., top_count : 2 * top_count]
     fixed_val = (

time: 89.3 us -> 89.1 us (level)
    unnamed x13 -> x15, local copies, waits for them, and re-layouts: 4.94 us -> 5.2 us
where the time goes in v15:
time: 89.1 us; the launch traced here: 88.8 us
  Pallas kernels  63.3 us (71%)
  matrix products  10.5 us (12%)
  local copies, waits for them, and re-layouts  7.63 us (9%)
  other arithmetic  6.5 us (7%)
    pallas_call x1, Pallas kernels, scatter_sums(): pl.pallas_call(functools.partial(combine_kernel, z_count, dp_count, seq_l...  32.5 us
    pallas_call x1, Pallas kernels, gather_blocks(): pl.pallas_call(functools.partial(dispatch_kernel, z_count, chunks), out_s...  30.8 us
    unnamed x15, local copies, waits for them, and re-layouts  5.2 us
    dot_general x1, matrix products, body(): jnp.einsum('esmt,std->esmd', picker, inputs_all, preferred_element_type=j...  3.29 us
    dot_general x1, matrix products, body(): jnp.einsum('esmd,edf->esmf', row_block, w_up, preferred_element_type=jnp....  2 us
    dot_general x1, matrix products, body(): jnp.einsum('esmd,edf->esmf', row_block, w_gate, preferred_element_type=jn...  1.84 us
    dot_general x1, matrix products, body(): jnp.einsum('esmf,efd->esmd', hidden, w_down, preferred_element_type=jnp.f...  1.82 us

profile of v15, /device:TPU:2, one launch (start us, length us, event | category | flops | bytes accessed | tf_op | source)
XLA Modules:
  0.0 88.8 jit_solution(15549493307824615539)
XLA Ops:
  0.6 0.7 broadcast_compare_fusion
  1.5 0.7 convert.14
  2.2 0.8 slice_reduce_fusion.1
  3.1 0.8 copy.32
  3.9 0.8 copy.31
  4.8 0.3 fusion.23
  5.3 1.1 %add_convert_fusion.blk_ref = bf16[64,2048]{1,0:T(8,128)(2,1)S(1)} fusion(bf16[64,2048]{1,0:T(8,128)(2,1)} %param.9, pred[64]{0:T(512)(128)(4,1)S(1)} %eq.47, bf16[2048]{0:T(1024)(128)(2,1)S(1)} %get-tuple-element.11, bf16[2048]{0:T(1024)(128)(2,1)S(1)} %get-tuple-element.10), kind=kLoop, calls=%fused_computation.25 | loop fusion | flops 655360 | bytes 532544 | tf_op jit(solution)/shard_map/convert_element_type | solution.py:320
  6.4 30.8 %shard_map.104 = (bf16[16,64,2048]{2,1,0:T(8,128)(2,1)S(1)}, bf16[16,16,128]{2,1,0:T(8,128)(2,1)S(1)}) custom-call(bf16[64,2048]{1,0:T(8,128)(2,1)S(1)} %add_convert_fusion.blk_ref, bf16[16,128]{1,0:T(8,128)(2,1)S(1)} %convert_element_type.55.rt_ref), custom_call_target="tpu_custom_call" | custom-call | tf_op jit(solution)/shard_map/pallas_call | solution.py:131
  37.3 1.9 %copy-done = bf16[16,64,2048]{2,1,0:T(8,128)(2,1)} copy-done((bf16[16,64,2048]{2,1,0:T(8,128)(2,1)}, bf16[16,64,2048]{2,1,0:T(8,128)(2,1)S(1)}, u32[]{:S(2)}) %copy-start) | copy-done | bytes 4194328
  39.4 0.5 fusion.42
  40.0 0.2 copy.37
  40.2 0.2 copy.48
  40.4 0.6 convert_divide_fusion
  41.0 1.6 %select_reduce_fusion = f32[16,48]{1,0:T(8,128)S(1)} fusion(f32[16,64,8]{1,2,0:T(8,128)S(1)} %convert_divide_fusion, s32[16,64,8]{1,2,0:T(8,128)S(1)} %copy.37), kind=kLoop, calls=%fused_computation.11 | loop fusion | flops 1178880 | bytes 68608 | tf_op jit(solution)/shard_map/reduce_sum | solution.py:343
  42.8 1.2 %fusion.13 = pred[16,48,64]{2,1,0:T(8,128)(4,1)S(1)} fusion(s32[16,64,8]{1,2,0:T(8,128)S(1)} %copy.37), kind=kLoop, calls=%fused_computation.13 | loop fusion | flops 737280 | bytes 81920 | tf_op jit(solution)/shard_map/reduce_or | solution.py:342
  44.0 3.3 %fusion.14 = bf16[2,16,24,2048]{3,2,0,1:T(8,128)(2,1)S(1)} fusion(pred[2,16,24,64]{3,2,0,1:T(8,128)(4,1)S(1)} %bitcast.42, bf16[16,64,2048]{2,1,0:T(8,128)(2,1)} %copy-done), kind=kOutput, calls=%fused_computation.14 | convolution fusion | flops 202899456 | bytes 7389184 | tf_op jit(solution)/shard_map/esmt,std->esmd/dot_general | solution.py:346
  47.4 1.8 %fusion.2 = f32[2,16,24,512]{3,2,1,0:T(8,128)S(1)} fusion(bf16[2,2048,512]{2,1,0:T(8,128)(2,1)S(1)} %copy-done.2, bf16[2,16,24,2048]{3,2,0,1:T(8,128)(2,1)S(1)} %fusion.14), kind=kOutput, calls=%fused_computation.4 | convolution fusion | flops 1610612736 | bytes 8912896 | tf_op jit(solution)/shard_map/esmd,edf->esmf/dot_general | solution.py:349
  49.3 0.3 copy-done.3
  49.6 2.0 %multiply_convert_fusion.1 = bf16[2,16,24,512]{3,2,1,0:T(8,128)(2,1)S(1)} fusion(f32[2,16,24,512]{3,2,1,0:T(8,128)S(1)} %fusion.2, bf16[2,2048,512]{2,1,0:T(8,128)(2,1)S(1)} %copy-done.3, bf16[2,16,24,2048]{3,2,0,1:T(8,128)(2,1)S(1)} %fusion.14), kind=kOutput, calls=%fused_computation.17 | convolution fusion | flops 1612972032 | bytes 9699328 | tf_op jit(solution)/shard_map/esmd,edf->esmf/dot_general | solution.py:350
  51.8 1.8 %multiply_convert_fusion = bf16[2,16,24,2048]{3,2,0,1:T(8,128)(2,1)S(1)} fusion(bf16[2,512,2048]{2,1,0:T(8,128)(2,1)S(1)} %copy-done.4, f32[2,16,24]{2,0,1:T(2,128)S(1)} %bitcast.44, bf16[2,16,24,512]{3,2,1,0:T(8,128)(2,1)S(1)} %multiply_convert_fusion.1), kind=kOutput, calls=%fused_computation.1 | convolution fusion | flops 1613758464 | bytes 8129536 | tf_op jit(solution)/shard_map/esmf,efd->esmd/dot_general | solution.py:352
  53.6 1.3 %bitcast_convert_fusion = bf16[16,64,2048]{2,1,0:T(8,128)(2,1)S(1)} fusion(pred[2,16,24,64]{3,2,0,1:T(8,128)(4,1)S(1)} %bitcast.43, bf16[2,16,24,2048]{3,2,0,1:T(8,128)(2,1)S(1)} %multiply_convert_fusion), kind=kOutput, calls=%fused_computation | convolution fusion | flops 203423744 | bytes 7389184 | tf_op jit(solution)/shard_map/esmt,esmd->std/dot_general | solution.py:355
  54.9 32.5 %shard_map.105 = (bf16[64,2048]{1,0:T(8,128)(2,1)S(1)}, f32[8,128]{1,0:T(8,128)S(1)}) custom-call(bf16[2,8,64,2048]{3,2,1,0:T(8,128)(2,1)S(1)} %bitcast.40, f32[1,2048]{1,0:T(1,128)S(1)} %bitcast.41), custom_call_target="tpu_custom_call" | custom-call | tf_op jit(solution)/shard_map/pallas_call | solution.py:281
  87.4 0.6 slice_reduce_fusion.2
  88.1 0.7 copy.58
  (21 shorter events, 1.5 us)
Async XLA Ops:
  37.3 1.9 %copy-start = (bf16[16,64,2048]{2,1,0:T(8,128)(2,1)}, bf16[16,64,2048]{2,1,0:T(8,128)(2,1)S(1)}, u32[]{:S(2)}) copy-start(bf16[16,64,2048]{2,1,0:T(8,128)(2,1)S(1)} %get-tuple-element.7) | copy-start | bytes 12582916
  44.0 3.5 %copy-start.2 = (bf16[2,2048,512]{2,1,0:T(8,128)(2,1)S(1)}, bf16[2,2048,512]{2,1,0:T(8,128)(2,1)}, u32[]{:S(2)}) copy-start(bf16[2,2048,512]{2,1,0:T(8,128)(2,1)} %param.14) | copy-start | bytes 12582916
  47.4 2.2 %copy-start.3 = (bf16[2,2048,512]{2,1,0:T(8,128)(2,1)S(1)}, bf16[2,2048,512]{2,1,0:T(8,128)(2,1)}, u32[]{:S(2)}) copy-start(bf16[2,2048,512]{2,1,0:T(8,128)(2,1)} %param.15) | copy-start | bytes 12582916
  49.6 2.2 %copy-start.4 = (bf16[2,512,2048]{2,1,0:T(8,128)(2,1)S(1)}, bf16[2,512,2048]{2,1,0:T(8,128)(2,1)}, u32[]{:S(2)}) copy-start(bf16[2,512,2048]{2,1,0:T(8,128)(2,1)} %param.16) | copy-start | bytes 12582916
  53.6 1.3 %copy-start.1 = (f32[2048]{0:T(1024)S(1)}, f32[2048]{0:T(1024)}, u32[]{:S(2)}) copy-start(f32[2048]{0:T(1024)} %param.17) | copy-start | bytes 24580

commit v16 on v13

--- a/solution.py
+++ b/solution.py
@@ -183,10 +183,18 @@
                 dests.append(lax.rem(z - ring_step * (bwd_hops + 1 - hop) + 2 * z_count, z_count))
         return dests + [z]
 
-    for n, dest in enumerate(order(-step)):
-        send(part_ref.at[other, dest], pair_buf.at[n], n, pair_id)
+    partner_order = order(-step)
+
+    def send_pair(n):
+        if n < len(partner_order):
+            send(part_ref.at[other, partner_order[n]], pair_buf.at[n], n, pair_id)
+
+    send_pair(0)
+    send_pair(1)
+
     def own(dest, n, k):
         if k == 0:
+            send_pair(n + 2)
             arrive(pair_buf.at[n], n)
         rows = pl.ds(k * piece, piece)
         return part_ref[c, dest, rows].astype(jnp.float32) + pair_buf[n, rows].astype(

time: 89.3 us -> 89.3 us (level)
  no operation moved by 1% of the time
where the time goes in v16:
time: 89.3 us; the launch traced here: 89 us
  Pallas kernels  63.7 us (71%)
  matrix products  10.5 us (12%)
  local copies, waits for them, and re-layouts  7.27 us (8%)
  other arithmetic  6.68 us (7%)
    pallas_call x1, Pallas kernels, scatter_sums(): pl.pallas_call(functools.partial(combine_kernel, z_count, dp_count, seq_l...  32.4 us
    pallas_call x1, Pallas kernels, gather_blocks(): pl.pallas_call(functools.partial(dispatch_kernel, z_count, chunks), out_s...  31.3 us
    unnamed x13, local copies, waits for them, and re-layouts  4.94 us
    dot_general x1, matrix products, body(): jnp.einsum('esmt,std->esmd', picker, inputs_all, preferred_element_type=j...  3.3 us
    dot_general x1, matrix products, body(): jnp.einsum('esmd,edf->esmf', row_block, w_up, preferred_element_type=jnp....  2 us
    dot_general x1, matrix products, body(): jnp.einsum('esmd,edf->esmf', row_block, w_gate, preferred_element_type=jn...  1.84 us
    dot_general x1, matrix products, body(): jnp.einsum('esmf,efd->esmd', hidden, w_down, preferred_element_type=jnp.f...  1.82 us

profile of v16, /device:TPU:2, one launch (start us, length us, event | category | flops | bytes accessed | tf_op | source)
XLA Modules:
  0.0 89.0 jit_solution(3916604960373500545)
XLA Ops:
  0.6 0.7 broadcast_compare_fusion
  1.5 0.7 convert.13
  2.2 0.8 slice_reduce_fusion.1
  3.1 0.8 copy.36
  3.9 0.8 copy.35
  4.8 0.3 fusion.24
  5.2 1.1 %add_convert_fusion = bf16[64,2048]{1,0:T(8,128)(2,1)S(1)} fusion(bf16[64,2048]{1,0:T(8,128)(2,1)} %param.9, pred[64]{0:T(512)(128)(4,1)S(1)} %eq.47, bf16[2048]{0:T(1024)(128)(2,1)S(1)} %get-tuple-element.7, bf16[2048]{0:T(1024)(128)(2,1)S(1)} %get-tuple-element.6), kind=kLoop, calls=%fused_computation.29 | loop fusion | flops 655360 | bytes 532544 | tf_op jit(solution)/shard_map/convert_element_type | solution.py:309
  6.4 31.3 %shard_map.104 = bf16[16,64,2176]{2,1,0:T(8,128)(2,1)S(1)} custom-call(bf16[64,2176]{1,0:T(8,128)(2,1)S(1)} %pad_maximum_fusion.blk_ref), custom_call_target="tpu_custom_call" | custom-call | tf_op jit(solution)/shard_map/pallas_call | solution.py:116
  37.7 2.0 %copy-done = bf16[16,64,2176]{2,1,0:T(8,128)(2,1)} copy-done((bf16[16,64,2176]{2,1,0:T(8,128)(2,1)}, bf16[16,64,2176]{2,1,0:T(8,128)(2,1)S(1)}, u32[]{:S(2)}) %copy-start) | copy-done | bytes 4456472
  39.8 0.5 fusion.28
  40.3 0.5 broadcast_divide_fusion
  40.9 0.2 fusion.27
  41.3 1.6 %select_reduce_fusion = f32[16,48]{1,0:T(8,128)S(1)} fusion(f32[16,64,8]{1,2,0:T(8,128)S(1)} %copy.43, s32[16,64,8]{1,2,0:T(8,128)S(1)} %copy.41), kind=kLoop, calls=%fused_computation.12 | loop fusion | flops 1178880 | bytes 68608 | tf_op jit(solution)/shard_map/reduce_sum | solution.py:334
  43.1 1.2 %fusion.14 = pred[16,48,64]{2,1,0:T(8,128)(4,1)S(1)} fusion(s32[16,64,8]{1,2,0:T(8,128)S(1)} %copy.41), kind=kLoop, calls=%fused_computation.14 | loop fusion | flops 737280 | bytes 81920 | tf_op jit(solution)/shard_map/reduce_or | solution.py:333
  44.3 3.3 %fusion.15 = bf16[2,16,24,2048]{3,2,0,1:T(8,128)(2,1)S(1)} fusion(pred[2,16,24,64]{3,2,0,1:T(8,128)(4,1)S(1)} %bitcast.42, bf16[16,64,2176]{2,1,0:T(8,128)(2,1)} %copy-done), kind=kOutput, calls=%fused_computation.15 | convolution fusion | flops 202899456 | bytes 7389184 | tf_op jit(solution)/shard_map/esmt,std->esmd/dot_general | solution.py:337
  47.7 1.8 %fusion.2 = f32[2,16,24,512]{3,2,1,0:T(8,128)S(1)} fusion(bf16[2,2048,512]{2,1,0:T(8,128)(2,1)S(1)} %copy-done.2, bf16[2,16,24,2048]{3,2,0,1:T(8,128)(2,1)S(1)} %fusion.15), kind=kOutput, calls=%fused_computation.4 | convolution fusion | flops 1610612736 | bytes 8912896 | tf_op jit(solution)/shard_map/esmd,edf->esmf/dot_general | solution.py:340
  49.5 0.3 copy-done.3
  49.9 2.0 %multiply_convert_fusion.1 = bf16[2,16,24,512]{3,2,1,0:T(8,128)(2,1)S(1)} fusion(f32[2,16,24,512]{3,2,1,0:T(8,128)S(1)} %fusion.2, bf16[2,2048,512]{2,1,0:T(8,128)(2,1)S(1)} %copy-done.3, bf16[2,16,24,2048]{3,2,0,1:T(8,128)(2,1)S(1)} %fusion.15), kind=kOutput, calls=%fused_computation.18 | convolution fusion | flops 1612972032 | bytes 9699328 | tf_op jit(solution)/shard_map/esmd,edf->esmf/dot_general | solution.py:341
  51.9 0.2 copy-done.4
  52.1 1.8 %multiply_convert_fusion = bf16[2,16,24,2048]{3,2,0,1:T(8,128)(2,1)S(1)} fusion(bf16[2,512,2048]{2,1,0:T(8,128)(2,1)S(1)} %copy-done.4, f32[2,16,24]{2,0,1:T(2,128)S(1)} %bitcast.44, bf16[2,16,24,512]{3,2,1,0:T(8,128)(2,1)S(1)} %multiply_convert_fusion.1), kind=kOutput, calls=%fused_computation.1 | convolution fusion | flops 1613758464 | bytes 8129536 | tf_op jit(solution)/shard_map/esmf,efd->esmd/dot_general | solution.py:343
  53.9 1.3 %bitcast_convert_fusion = bf16[16,64,2048]{2,1,0:T(8,128)(2,1)S(1)} fusion(pred[2,16,24,64]{3,2,0,1:T(8,128)(4,1)S(1)} %bitcast.43, bf16[2,16,24,2048]{3,2,0,1:T(8,128)(2,1)S(1)} %multiply_convert_fusion), kind=kOutput, calls=%fused_computation | convolution fusion | flops 203423744 | bytes 7389184 | tf_op jit(solution)/shard_map/esmt,esmd->std/dot_general | solution.py:346
  55.2 32.4 %shard_map.105 = (bf16[64,2048]{1,0:T(8,128)(2,1)S(1)}, f32[8,128]{1,0:T(8,128)S(1)}) custom-call(bf16[2,8,64,2048]{3,2,1,0:T(8,128)(2,1)S(1)} %bitcast.40, f32[1,2048]{1,0:T(1,128)S(1)} %bitcast.41), custom_call_target="tpu_custom_call" | custom-call | tf_op jit(solution)/shard_map/pallas_call | solution.py:270
  87.7 0.6 slice_reduce_fusion.2
  88.3 0.7 copy.60
  (20 shorter events, 1.2 us)
Async XLA Ops:
  37.7 2.0 %copy-start = (bf16[16,64,2176]{2,1,0:T(8,128)(2,1)}, bf16[16,64,2176]{2,1,0:T(8,128)(2,1)S(1)}, u32[]{:S(2)}) copy-start(bf16[16,64,2176]{2,1,0:T(8,128)(2,1)S(1)} %shard_map.104) | copy-start | bytes 13369348
  44.2 3.5 %copy-start.2 = (bf16[2,2048,512]{2,1,0:T(8,128)(2,1)S(1)}, bf16[2,2048,512]{2,1,0:T(8,128)(2,1)}, u32[]{:S(2)}) copy-start(bf16[2,2048,512]{2,1,0:T(8,128)(2,1)} %param.14) | copy-start | bytes 12582916
  47.7 2.2 %copy-start.3 = (bf16[2,2048,512]{2,1,0:T(8,128)(2,1)S(1)}, bf16[2,2048,512]{2,1,0:T(8,128)(2,1)}, u32[]{:S(2)}) copy-start(bf16[2,2048,512]{2,1,0:T(8,128)(2,1)} %param.15) | copy-start | bytes 12582916
  49.9 2.2 %copy-start.4 = (bf16[2,512,2048]{2,1,0:T(8,128)(2,1)S(1)}, bf16[2,512,2048]{2,1,0:T(8,128)(2,1)}, u32[]{:S(2)}) copy-start(bf16[2,512,2048]{2,1,0:T(8,128)(2,1)} %param.16) | copy-start | bytes 12582916
  53.9 1.3 %copy-start.1 = (f32[2048]{0:T(1024)S(1)}, f32[2048]{0:T(1024)}, u32[]{:S(2)}) copy-start(f32[2048]{0:T(1024)} %param.17) | copy-start | bytes 24580

commit v17 on v13

--- a/solution.py
+++ b/solution.py
@@ -23,14 +23,13 @@
 
 
 def route_ranks(expert_ids, expert_total):
-    flat_ids = expert_ids.reshape(-1)
-    entry_count = flat_ids.shape[0]
-    onehot = flat_ids[:, None] == jnp.arange(expert_total, dtype=jnp.int32)[None, :]
-    positions = jnp.arange(entry_count, dtype=jnp.int32)
+    tok_rows = expert_ids.shape[0]
+    onehot = expert_ids[:, :, None] == jnp.arange(expert_total, dtype=jnp.int32)[None, None, :]
+    per_token = jnp.any(onehot, axis=1).astype(jnp.bfloat16)
+    positions = jnp.arange(tok_rows, dtype=jnp.int32)
     earlier = (positions[:, None] > positions[None, :]).astype(jnp.bfloat16)
-    counts = jnp.dot(earlier, onehot.astype(jnp.bfloat16), preferred_element_type=jnp.float32)
-    rank_in = jnp.sum(jnp.where(onehot, counts, 0.0), axis=1).astype(jnp.int32)
-    return rank_in.reshape(expert_ids.shape)
+    counts = jnp.dot(earlier, per_token, preferred_element_type=jnp.float32)
+    return jnp.sum(jnp.where(onehot, counts[:, None, :], 0.0), axis=2).astype(jnp.int32)
 
 
 MESH = pl.DeviceIdType.MESH

time: 89.3 us -> 89.8 us (level)
  other arithmetic: 6.68 us -> 8.11 us
    unnamed x13 -> x12, local copies, waits for them, and re-layouts: 4.94 us -> 4.17 us
where the time goes in v17:
time: 89.8 us; the launch traced here: 89.4 us
  Pallas kernels  63.7 us (71%)
  matrix products  10.4 us (12%)
  other arithmetic  8.11 us (9%)
  local copies, waits for them, and re-layouts  6.42 us (7%)
    pallas_call x1, Pallas kernels, scatter_sums(): pl.pallas_call(functools.partial(combine_kernel, z_count, dp_count, seq_l...  32.4 us
    pallas_call x1, Pallas kernels, gather_blocks(): pl.pallas_call(functools.partial(dispatch_kernel, z_count, chunks), out_s...  31.3 us
    unnamed x12, local copies, waits for them, and re-layouts  4.17 us
    dot_general x1, matrix products, body(): jnp.einsum('esmt,std->esmd', picker, inputs_all, preferred_element_type=j...  3.29 us
    dot_general x1, matrix products, body(): jnp.einsum('esmd,edf->esmf', row_block, w_up, preferred_element_type=jnp....  2 us
    dot_general x1, matrix products, body(): jnp.einsum('esmd,edf->esmf', row_block, w_gate, preferred_element_type=jn...  1.84 us
    dot_general x1, matrix products, body(): jnp.einsum('esmf,efd->esmd', hidden, w_down, preferred_element_type=jnp.f...  1.82 us

profile of v17, /device:TPU:2, one launch (start us, length us, event | category | flops | bytes accessed | tf_op | source)
XLA Modules:
  0.0 89.4 jit_solution(15040417536095683640)
XLA Ops:
  0.6 0.7 broadcast_compare_fusion
  1.5 0.7 convert.12
  2.2 0.7 fusion.28
  2.9 0.8 slice_reduce_fusion.1
  3.8 0.7 select_reduce_fusion.1
  4.8 0.8 copy.38
  5.7 1.1 %add_convert_fusion = bf16[64,2048]{1,0:T(8,128)(2,1)S(1)} fusion(bf16[64,2048]{1,0:T(8,128)(2,1)} %param.9, pred[64]{0:T(512)(128)(4,1)S(1)} %eq.45, bf16[2048]{0:T(1024)(128)(2,1)S(1)} %get-tuple-element.7, bf16[2048]{0:T(1024)(128)(2,1)S(1)} %get-tuple-element.6), kind=kLoop, calls=%fused_computation.26 | loop fusion | flops 655360 | bytes 532544 | tf_op jit(solution)/shard_map/convert_element_type | solution.py:300
  6.8 31.3 %shard_map.104 = bf16[16,64,2176]{2,1,0:T(8,128)(2,1)S(1)} custom-call(bf16[64,2176]{1,0:T(8,128)(2,1)S(1)} %pad_maximum_fusion.blk_ref), custom_call_target="tpu_custom_call" | custom-call | tf_op jit(solution)/shard_map/pallas_call | solution.py:115
  38.1 2.0 %copy-done = bf16[16,64,2176]{2,1,0:T(8,128)(2,1)} copy-done((bf16[16,64,2176]{2,1,0:T(8,128)(2,1)}, bf16[16,64,2176]{2,1,0:T(8,128)(2,1)S(1)}, u32[]{:S(2)}) %copy-start) | copy-done | bytes 4456472
  40.2 0.5 fusion.27
  40.7 0.5 broadcast_divide_fusion
  41.4 0.2 fusion.26
  41.8 1.6 %select_reduce_fusion = f32[16,48]{1,0:T(8,128)S(1)} fusion(f32[16,64,8]{1,2,0:T(8,128)S(1)} %copy.46, s32[16,64,8]{1,2,0:T(8,128)S(1)} %copy.44), kind=kLoop, calls=%fused_computation.12 | loop fusion | flops 1178880 | bytes 68608 | tf_op jit(solution)/shard_map/reduce_sum | solution.py:325
  43.5 1.2 %fusion.14 = pred[16,48,64]{2,1,0:T(8,128)(4,1)S(1)} fusion(s32[16,64,8]{1,2,0:T(8,128)S(1)} %copy.44), kind=kLoop, calls=%fused_computation.14 | loop fusion | flops 737280 | bytes 81920 | tf_op jit(solution)/shard_map/reduce_or | solution.py:324
  44.7 3.3 %fusion.15 = bf16[2,16,24,2048]{3,2,0,1:T(8,128)(2,1)S(1)} fusion(pred[2,16,24,64]{3,2,0,1:T(8,128)(4,1)S(1)} %bitcast.43, bf16[16,64,2176]{2,1,0:T(8,128)(2,1)} %copy-done), kind=kOutput, calls=%fused_computation.15 | convolution fusion | flops 202899456 | bytes 7389184 | tf_op jit(solution)/shard_map/esmt,std->esmd/dot_general | solution.py:328
  48.1 1.8 %fusion.2 = f32[2,16,24,512]{3,2,1,0:T(8,128)S(1)} fusion(bf16[2,2048,512]{2,1,0:T(8,128)(2,1)S(1)} %copy-done.2, bf16[2,16,24,2048]{3,2,0,1:T(8,128)(2,1)S(1)} %fusion.15), kind=kOutput, calls=%fused_computation.4 | convolution fusion | flops 1610612736 | bytes 8912896 | tf_op jit(solution)/shard_map/esmd,edf->esmf/dot_general | solution.py:331
  50.0 0.3 copy-done.3
  50.3 2.0 %multiply_convert_fusion.1 = bf16[2,16,24,512]{3,2,1,0:T(8,128)(2,1)S(1)} fusion(f32[2,16,24,512]{3,2,1,0:T(8,128)S(1)} %fusion.2, bf16[2,2048,512]{2,1,0:T(8,128)(2,1)S(1)} %copy-done.3, bf16[2,16,24,2048]{3,2,0,1:T(8,128)(2,1)S(1)} %fusion.15), kind=kOutput, calls=%fused_computation.18 | convolution fusion | flops 1612972032 | bytes 9699328 | tf_op jit(solution)/shard_map/esmd,edf->esmf/dot_general | solution.py:332
  52.3 0.2 copy-done.4
  52.5 1.8 %multiply_convert_fusion = bf16[2,16,24,2048]{3,2,0,1:T(8,128)(2,1)S(1)} fusion(bf16[2,512,2048]{2,1,0:T(8,128)(2,1)S(1)} %copy-done.4, f32[2,16,24]{2,0,1:T(2,128)S(1)} %bitcast.45, bf16[2,16,24,512]{3,2,1,0:T(8,128)(2,1)S(1)} %multiply_convert_fusion.1), kind=kOutput, calls=%fused_computation.1 | convolution fusion | flops 1613758464 | bytes 8129536 | tf_op jit(solution)/shard_map/esmf,efd->esmd/dot_general | solution.py:334
  54.3 1.3 %bitcast_convert_fusion = bf16[16,64,2048]{2,1,0:T(8,128)(2,1)S(1)} fusion(pred[2,16,24,64]{3,2,0,1:T(8,128)(4,1)S(1)} %bitcast.44, bf16[2,16,24,2048]{3,2,0,1:T(8,128)(2,1)S(1)} %multiply_convert_fusion), kind=kOutput, calls=%fused_computation | convolution fusion | flops 203423744 | bytes 7389184 | tf_op jit(solution)/shard_map/esmt,esmd->std/dot_general | solution.py:337
  55.7 32.4 %shard_map.105 = (bf16[64,2048]{1,0:T(8,128)(2,1)S(1)}, f32[8,128]{1,0:T(8,128)S(1)}) custom-call(bf16[2,8,64,2048]{3,2,1,0:T(8,128)(2,1)S(1)} %bitcast.41, f32[1,2048]{1,0:T(1,128)S(1)} %bitcast.42), custom_call_target="tpu_custom_call" | custom-call | tf_op jit(solution)/shard_map/pallas_call | solution.py:261
  88.1 0.6 slice_reduce_fusion.2
  88.7 0.7 copy.63
  (20 shorter events, 1.3 us)
Async XLA Ops:
  38.1 2.0 %copy-start = (bf16[16,64,2176]{2,1,0:T(8,128)(2,1)}, bf16[16,64,2176]{2,1,0:T(8,128)(2,1)S(1)}, u32[]{:S(2)}) copy-start(bf16[16,64,2176]{2,1,0:T(8,128)(2,1)S(1)} %shard_map.104) | copy-start | bytes 13369348
  44.7 3.5 %copy-start.2 = (bf16[2,2048,512]{2,1,0:T(8,128)(2,1)S(1)}, bf16[2,2048,512]{2,1,0:T(8,128)(2,1)}, u32[]{:S(2)}) copy-start(bf16[2,2048,512]{2,1,0:T(8,128)(2,1)} %param.14) | copy-start | bytes 12582916
  48.1 2.2 %copy-start.3 = (bf16[2,2048,512]{2,1,0:T(8,128)(2,1)S(1)}, bf16[2,2048,512]{2,1,0:T(8,128)(2,1)}, u32[]{:S(2)}) copy-start(bf16[2,2048,512]{2,1,0:T(8,128)(2,1)} %param.15) | copy-start | bytes 12582916
  50.3 2.2 %copy-start.4 = (bf16[2,512,2048]{2,1,0:T(8,128)(2,1)S(1)}, bf16[2,512,2048]{2,1,0:T(8,128)(2,1)}, u32[]{:S(2)}) copy-start(bf16[2,512,2048]{2,1,0:T(8,128)(2,1)} %param.16) | copy-start | bytes 12582916
  54.3 1.3 %copy-start.1 = (f32[2048]{0:T(1024)S(1)}, f32[2048]{0:T(1024)}, u32[]{:S(2)}) copy-start(f32[2048]{0:T(1024)} %param.17) | copy-start | bytes 24580

commit v18 on v13

--- a/solution.py
+++ b/solution.py
@@ -326,9 +326,9 @@
     slot_weight = jnp.sum(jnp.where(match, weight_cube[:, None, :, :], 0.0), axis=(2, 3))
     picker = picker.reshape(expert_count, per_device, MOST, tok_rows).transpose(1, 0, 2, 3)
     slot_weight = slot_weight.reshape(expert_count, per_device, MOST).transpose(1, 0, 2)
-    row_block = jnp.einsum(
-        "esmt,std->esmd", picker, inputs_all, preferred_element_type=jnp.float32
-    ).astype(jnp.bfloat16)
+    token_of = jnp.argmax(picker, axis=3)
+    source_of = jnp.arange(expert_count, dtype=jnp.int32)[None, :, None]
+    row_block = inputs_all[source_of, token_of]
     gate_proj = jnp.einsum("esmd,edf->esmf", row_block, w_gate, preferred_element_type=jnp.float32)
     up_proj = jnp.einsum("esmd,edf->esmf", row_block, w_up, preferred_element_type=jnp.float32)
     hidden = (jax.nn.silu(gate_proj) * up_proj).astype(jnp.bfloat16)

time: 89.3 us -> 109 us (1.22)
  local copies, waits for them, and re-layouts: 7.27 us -> 25.6 us
  other arithmetic: 6.68 us -> 8.74 us
    gather x0 -> x1, local copies, waits for them, and re-layouts: none -> 13.9 us  [body(): row_block = inputs_all[source_of, token_of]]
    slice x0 -> x1, local copies, waits for them, and re-layouts: none -> 4.74 us  [body(): inputs_all = gathered[:, :, :model_width]]
    dot_general x1 -> x0, matrix products: 3.3 us -> none  [body(): jnp.einsum('esmt,std->esmd', picker, inputs_all, preferred_element_type=j...]
    dot_general x1, matrix products: 1.84 us -> 4.13 us  [body(): jnp.einsum('esmd,edf->esmf', row_block, w_gate, preferred_element_type=jn...]
    another operation x3 -> x4, other arithmetic: 0.74 us -> 2.78 us  [the longest x1 2.04 us: body(): token_of = jnp.argmax(picker, axis=3)]
    unnamed x13 -> x11, local copies, waits for them, and re-layouts: 4.94 us -> 4.57 us
where the time goes in v18:
time: 109 us; the launch traced here: 108 us
  Pallas kernels  63.3 us (58%)
  local copies, waits for them, and re-layouts  25.6 us (23%)
  matrix products  9.45 us (9%)
  other arithmetic  8.74 us (8%)
    pallas_call x1, Pallas kernels, scatter_sums(): pl.pallas_call(functools.partial(combine_kernel, z_count, dp_count, seq_l...  32 us
    pallas_call x1, Pallas kernels, gather_blocks(): pl.pallas_call(functools.partial(dispatch_kernel, z_count, chunks), out_s...  31.3 us
    gather x1, local copies, waits for them, and re-layouts, body(): row_block = inputs_all[source_of, token_of]  13.9 us
    slice x1, local copies, waits for them, and re-layouts, body(): inputs_all = gathered[:, :, :model_width]  4.74 us
    unnamed x11, local copies, waits for them, and re-layouts  4.57 us
    dot_general x1, matrix products, body(): jnp.einsum('esmd,edf->esmf', row_block, w_gate, preferred_element_type=jn...  4.13 us

profile of v18, /device:TPU:2, one launch (start us, length us, event | category | flops | bytes accessed | tf_op | source)
XLA Modules:
  0.0 107.9 jit_solution(16575590574072343178)
XLA Ops:
  0.6 0.8 copy.41
  1.4 0.8 copy.40
  2.3 0.3 fusion.11
  2.7 0.7 convert.14
  3.6 0.7 broadcast_compare_fusion
  4.4 0.8 slice_reduce_fusion.1
  5.2 1.1 %add_convert_fusion = bf16[64,2048]{1,0:T(8,128)(2,1)S(1)} fusion(bf16[64,2048]{1,0:T(8,128)(2,1)} %param.9, pred[64]{0:T(512)(128)(4,1)S(1)} %eq.49, bf16[2048]{0:T(1024)(128)(2,1)S(1)} %get-tuple-element.9, bf16[2048]{0:T(1024)(128)(2,1)S(1)} %get-tuple-element.8), kind=kLoop, calls=%fused_computation.23 | loop fusion | flops 655360 | bytes 532544 | tf_op jit(solution)/shard_map/convert_element_type | solution.py:301
  6.4 31.3 %shard_map.104 = bf16[16,64,2176]{2,1,0:T(8,128)(2,1)S(1)} custom-call(bf16[64,2176]{1,0:T(8,128)(2,1)S(1)} %pad_maximum_fusion.blk_ref), custom_call_target="tpu_custom_call" | custom-call | tf_op jit(solution)/shard_map/pallas_call | solution.py:116
  37.7 2.0 %copy-done = bf16[16,64,2176]{2,1,0:T(8,128)(2,1)} copy-done((bf16[16,64,2176]{2,1,0:T(8,128)(2,1)}, bf16[16,64,2176]{2,1,0:T(8,128)(2,1)S(1)}, u32[]{:S(2)}) %copy-start) | copy-done | bytes 4456472
  40.1 1.2 %fusion.8 = pred[16,48,64]{2,1,0:T(8,128)(4,1)S(1)} fusion(s32[16,64,8]{1,2,0:T(8,128)S(1)} %copy.46), kind=kLoop, calls=%fused_computation.11 | loop fusion | flops 737280 | bytes 81920 | tf_op jit(solution)/shard_map/reduce_or | solution.py:325
  41.3 0.5 fusion.15
  41.9 0.5 broadcast_divide_fusion
  42.5 1.6 %select_reduce_fusion = f32[16,48]{1,0:T(8,128)S(1)} fusion(f32[16,64,8]{1,2,0:T(8,128)S(1)} %copy.48, s32[16,64,8]{1,2,0:T(8,128)S(1)} %copy.46), kind=kLoop, calls=%fused_computation.9 | loop fusion | flops 1178880 | bytes 68608 | tf_op jit(solution)/shard_map/reduce_sum | solution.py:326
  44.2 4.7 %slice.34 = bf16[16,64,2048]{2,1,0:T(8,128)(2,1)} slice(bf16[16,64,2176]{2,1,0:T(8,128)(2,1)} %copy-done), slice={[0:16], [0:64], [0:2048]} | slice | bytes 8388608 | tf_op jit(solution)/shard_map/slice | solution.py:309
  49.0 2.0 %iota_reduce_fusion = (bf16[2,16,24]{2,0,1:T(2,128)(2,1)}, s32[2,16,24]{2,0,1:T(2,128)S(1)}) fusion(pred[2,16,24,64]{3,2,0,1:T(8,128)(4,1)S(1)} %bitcast.41), kind=kLoop, calls=%fused_computation.24 | loop fusion | flops 484608 | bytes 53760 | tf_op jit(solution)/shard_map/body/reduce | solution.py:329
  51.2 13.9 %gather_fusion = bf16[768,2048]{1,0:T(8,128)(2,1)S(1)} fusion(bf16[16,64,2048]{2,1,0:T(8,128)(2,1)} %slice.34, s32[768]{0:T(1024)S(1)} %reshape.40), kind=kCustom, calls=%fused_computation | custom fusion | bytes 6297600 | tf_op jit(solution)/shard_map/gather | solution.py:331
  65.0 4.1 %fusion.2 = f32[2,16,24,512]{3,2,1,0:T(8,128)S(1)} fusion(bf16[2,16,24,2048]{3,2,1,0:T(8,128)(2,1)S(1)} %bitcast.39, bf16[2,2048,512]{2,1,0:T(8,128)(2,1)} %param.14), kind=kOutput, calls=%fused_computation.5 | convolution fusion | flops 1610612736 | bytes 8912896 | tf_op jit(solution)/shard_map/esmd,edf->esmf/dot_general | solution.py:332
  69.2 1.9 %multiply_convert_fusion.1 = bf16[2,16,24,512]{3,2,1,0:T(8,128)(2,1)S(1)} fusion(f32[2,16,24,512]{3,2,1,0:T(8,128)S(1)} %fusion.2, bf16[2,16,24,2048]{3,2,1,0:T(8,128)(2,1)S(1)} %bitcast.40, bf16[2,2048,512]{2,1,0:T(8,128)(2,1)S(1)} %copy-done.2), kind=kOutput, calls=%fused_computation.12 | convolution fusion | flops 1612972032 | bytes 9699328 | tf_op jit(solution)/shard_map/esmd,edf->esmf/dot_general | solution.py:333
  71.1 0.3 copy-done.3
  71.4 1.8 %multiply_convert_fusion = bf16[2,16,24,2048]{3,2,0,1:T(8,128)(2,1)S(1)} fusion(bf16[2,512,2048]{2,1,0:T(8,128)(2,1)S(1)} %copy-done.3, f32[2,16,24]{2,0,1:T(2,128)S(1)} %bitcast.43, bf16[2,16,24,512]{3,2,1,0:T(8,128)(2,1)S(1)} %multiply_convert_fusion.1), kind=kOutput, calls=%fused_computation.2 | convolution fusion | flops 1613758464 | bytes 8129536 | tf_op jit(solution)/shard_map/esmf,efd->esmd/dot_general | solution.py:335
  73.2 1.3 %bitcast_convert_fusion = bf16[16,64,2048]{2,1,0:T(8,128)(2,1)S(1)} fusion(pred[2,16,24,64]{3,2,0,1:T(8,128)(4,1)S(1)} %bitcast.42, bf16[2,16,24,2048]{3,2,0,1:T(8,128)(2,1)S(1)} %multiply_convert_fusion), kind=kOutput, calls=%fused_computation.1 | convolution fusion | flops 203423744 | bytes 7389184 | tf_op jit(solution)/shard_map/esmt,esmd->std/dot_general | solution.py:338
  74.6 32.0 %shard_map.105 = (bf16[64,2048]{1,0:T(8,128)(2,1)S(1)}, f32[8,128]{1,0:T(8,128)S(1)}) custom-call(bf16[2,8,64,2048]{3,2,1,0:T(8,128)(2,1)S(1)} %bitcast.37, f32[1,2048]{1,0:T(1,128)S(1)} %bitcast.38), custom_call_target="tpu_custom_call" | custom-call | tf_op jit(solution)/shard_map/pallas_call | solution.py:262
  106.6 0.6 slice_reduce_fusion.2
  107.2 0.7 copy.58
  (23 shorter events, 1.4 us)
Async XLA Ops:
  37.7 2.0 %copy-start = (bf16[16,64,2176]{2,1,0:T(8,128)(2,1)}, bf16[16,64,2176]{2,1,0:T(8,128)(2,1)S(1)}, u32[]{:S(2)}) copy-start(bf16[16,64,2176]{2,1,0:T(8,128)(2,1)S(1)} %shard_map.104) | copy-start | bytes 13369348
  65.0 4.2 %copy-start.2 = (bf16[2,2048,512]{2,1,0:T(8,128)(2,1)S(1)}, bf16[2,2048,512]{2,1,0:T(8,128)(2,1)}, u32[]{:S(2)}) copy-start(bf16[2,2048,512]{2,1,0:T(8,128)(2,1)} %param.15) | copy-start | bytes 12582916
  69.2 2.2 %copy-start.3 = (bf16[2,512,2048]{2,1,0:T(8,128)(2,1)S(1)}, bf16[2,512,2048]{2,1,0:T(8,128)(2,1)}, u32[]{:S(2)}) copy-start(bf16[2,512,2048]{2,1,0:T(8,128)(2,1)} %param.16) | copy-start | bytes 12582916
  73.2 1.3 %copy-start.1 = (f32[2048]{0:T(1024)S(1)}, f32[2048]{0:T(1024)}, u32[]{:S(2)}) copy-start(f32[2048]{0:T(1024)} %param.17) | copy-start | bytes 24580

commit v19 on v13

--- a/solution.py
+++ b/solution.py
@@ -130,8 +130,8 @@
 
 
 def combine_kernel(
-    z_count, dp_count, seq_len, chunks, part_ref, head_ref, out_ref, pair_out, pair_buf,
-    fwd_buf, bwd_buf, fwd_out, bwd_out, seq_out, seq_in, send_sem, recv_sem, seq_sem,
+    z_count, chunks, part_ref, out_ref, pair_buf, fwd_buf, bwd_buf, fwd_out, bwd_out,
+    send_sem, recv_sem,
 ):
     z = lax.axis_index("z")
     c = lax.axis_index("c")
@@ -141,15 +141,14 @@
     fwd = lax.rem(z + step + z_count, z_count)
     bwd = lax.rem(z - step + z_count, z_count)
     fwd_id, bwd_id, pair_id = (row, fwd, c), (row, bwd, c), (row, z, other)
-    mate_id = (lax.rem(row + dp_count // 2, dp_count), z, c)
     fwd_hops = z_count // 2
     bwd_hops = z_count - 1 - fwd_hops
     piece = part_ref.shape[2] // chunks
 
     barrier = pltpu.get_barrier_semaphore()
-    for target in (fwd_id, bwd_id, pair_id, mate_id):
+    for target in (fwd_id, bwd_id, pair_id):
         pl.semaphore_signal(barrier, 1, device_id=target, device_id_type=MESH)
-    pl.semaphore_wait(barrier, 4)
+    pl.semaphore_wait(barrier, 3)
 
     sends = []
 
@@ -227,9 +226,21 @@
             arrive(bwd_buf.at[bwd_hops - 1, rows], bwd_sem + (bwd_hops - 1) * chunks + k)
             total = total + bwd_buf[bwd_hops - 1, rows].astype(jnp.float32)
         out_ref[rows] = total.astype(out_ref.dtype)
-    tok_rows, width = out_ref.shape
+    for copy in sends:
+        copy.wait_send()
+
+
+def score_kernel(dp_count, seq_len, mixed_ref, head_ref, pair_out, seq_out, seq_in, seq_sem):
+    z = lax.axis_index("z")
+    c = lax.axis_index("c")
+    row = lax.axis_index("dp")
+    mate_id = (lax.rem(row + dp_count // 2, dp_count), z, c)
+    barrier = pltpu.get_barrier_semaphore()
+    pl.semaphore_signal(barrier, 1, device_id=mate_id, device_id_type=MESH)
+    pl.semaphore_wait(barrier, 1)
+    tok_rows, width = mixed_ref.shape
     seqs = tok_rows // seq_len
-    scored = out_ref[...].astype(jnp.float32) * head_ref[...]
+    scored = mixed_ref[...].astype(jnp.float32) * head_ref[...]
     per_seq = jnp.sum(scored.reshape(seqs, seq_len, width), axis=1)
     seq_score = jnp.sum(per_seq, axis=1, keepdims=True)
     seq_out[...] = jnp.zeros(seq_out.shape, jnp.float32)
@@ -247,8 +258,6 @@
     mine = seq_out[...]
     theirs = seq_in[...]
     pair_out[...] = jnp.abs(mine - theirs) + 0.5 * (mine + theirs)
-    for copy in sends:
-        copy.wait_send()
 
 
 def scatter_sums(partial, score_head, dp_count, seq_len, chunks):
@@ -259,30 +268,37 @@
     vmem = pl.BlockSpec(memory_space=pltpu.VMEM)
     sems = z_count + (fwd_hops + bwd_hops) * chunks
     tile = (8, 128)
-    return pl.pallas_call(
-        functools.partial(combine_kernel, z_count, dp_count, seq_len, chunks),
-        out_shape=(
-            jax.ShapeDtypeStruct(block, partial.dtype),
-            jax.ShapeDtypeStruct(tile, jnp.float32),
-        ),
-        in_specs=[vmem, vmem],
-        out_specs=(vmem, vmem),
+    mixed = pl.pallas_call(
+        functools.partial(combine_kernel, z_count, chunks),
+        out_shape=jax.ShapeDtypeStruct(block, partial.dtype),
+        in_specs=[vmem],
+        out_specs=vmem,
         scratch_shapes=[
             pltpu.VMEM((z_count,) + block, partial.dtype),
             pltpu.VMEM((fwd_hops,) + block, partial.dtype),
             pltpu.VMEM((bwd_hops,) + block, partial.dtype),
             pltpu.VMEM((fwd_hops,) + block, partial.dtype),
             pltpu.VMEM((bwd_hops,) + block, partial.dtype),
-            pltpu.VMEM(tile, jnp.float32),
-            pltpu.VMEM(tile, jnp.float32),
             pltpu.SemaphoreType.DMA((sems,)),
             pltpu.SemaphoreType.DMA((sems,)),
-            pltpu.SemaphoreType.DMA((2,)),
         ],
         compiler_params=pltpu.CompilerParams(
             collective_id=1, has_side_effects=True, vmem_limit_bytes=48 * 1024 * 1024
         ),
-    )(partial, score_head.reshape(1, -1))
+    )(partial)
+    pair_tile = pl.pallas_call(
+        functools.partial(score_kernel, dp_count, seq_len),
+        out_shape=jax.ShapeDtypeStruct(tile, jnp.float32),
+        in_specs=[vmem, vmem],
+        out_specs=vmem,
+        scratch_shapes=[
+            pltpu.VMEM(tile, jnp.float32),
+            pltpu.VMEM(tile, jnp.float32),
+            pltpu.SemaphoreType.DMA((2,)),
+        ],
+        compiler_params=pltpu.CompilerParams(collective_id=2, has_side_effects=True),
+    )(mixed, score_head.reshape(1, -1))
+    return mixed, pair_tile
 
 
 def body(

time: 89.3 us -> 93.6 us (1.048)
  local copies, waits for them, and re-layouts: 7.27 us -> 9.6 us
  Pallas kernels: 63.7 us -> 65.6 us
    pallas_call x1 -> x2, Pallas kernels: 32.4 us -> 34.3 us  [the longest x1 27.4 us: scatter_sums(): pl.pallas_call(functools.partial(combine_kernel, z_count, chunks), out_sh...]
    unnamed x13, local copies, waits for them, and re-layouts: 4.94 us -> 6.59 us
where the time goes in v19:
time: 93.6 us; the launch traced here: 93.2 us
  Pallas kernels  65.6 us (70%)
  matrix products  10.6 us (11%)
  local copies, waits for them, and re-layouts  9.6 us (10%)
  other arithmetic  6.68 us (7%)
    pallas_call x1, Pallas kernels, gather_blocks(): pl.pallas_call(functools.partial(dispatch_kernel, z_count, chunks), out_s...  31.3 us
    pallas_call x1, Pallas kernels, scatter_sums(): pl.pallas_call(functools.partial(combine_kernel, z_count, chunks), out_sh...  27.4 us
    pallas_call x1, Pallas kernels, scatter_sums(): pl.pallas_call(functools.partial(score_kernel, dp_count, seq_len), out_sh...  6.87 us
    unnamed x13, local copies, waits for them, and re-layouts  6.59 us
    dot_general x1, matrix products, body(): jnp.einsum('esmt,std->esmd', picker, inputs_all, preferred_element_type=j...  3.3 us
    dot_general x1, matrix products, body(): jnp.einsum('esmd,edf->esmf', row_block, w_up, preferred_element_type=jnp....  1.99 us

profile of v19, /device:TPU:2, one launch (start us, length us, event | category | flops | bytes accessed | tf_op | source)
XLA Modules:
  0.0 93.2 jit_solution(11902091938715101762)
XLA Ops:
  0.6 0.7 broadcast_compare_fusion
  1.5 0.7 convert.13
  2.2 0.8 slice_reduce_fusion.1
  3.1 0.8 copy.36
  3.9 0.8 copy.35
  4.8 0.3 fusion.24
  5.2 1.1 %add_convert_fusion = bf16[64,2048]{1,0:T(8,128)(2,1)S(1)} fusion(bf16[64,2048]{1,0:T(8,128)(2,1)} %param.9, pred[64]{0:T(512)(128)(4,1)S(1)} %eq.47, bf16[2048]{0:T(1024)(128)(2,1)S(1)} %get-tuple-element.3, bf16[2048]{0:T(1024)(128)(2,1)S(1)} %get-tuple-element.2), kind=kLoop, calls=%fused_computation.29 | loop fusion | flops 655360 | bytes 532544 | tf_op jit(solution)/shard_map/convert_element_type | solution.py:317
  6.4 31.3 %shard_map.104 = bf16[16,64,2176]{2,1,0:T(8,128)(2,1)S(1)} custom-call(bf16[64,2176]{1,0:T(8,128)(2,1)S(1)} %pad_maximum_fusion.blk_ref), custom_call_target="tpu_custom_call" | custom-call | tf_op jit(solution)/shard_map/pallas_call | solution.py:116
  37.7 2.0 %copy-done = bf16[16,64,2176]{2,1,0:T(8,128)(2,1)} copy-done((bf16[16,64,2176]{2,1,0:T(8,128)(2,1)}, bf16[16,64,2176]{2,1,0:T(8,128)(2,1)S(1)}, u32[]{:S(2)}) %copy-start) | copy-done | bytes 4456472
  39.8 0.5 fusion.28
  40.3 0.5 broadcast_divide_fusion
  41.3 1.6 %select_reduce_fusion = f32[16,48]{1,0:T(8,128)S(1)} fusion(f32[16,64,8]{1,2,0:T(8,128)S(1)} %copy.43, s32[16,64,8]{1,2,0:T(8,128)S(1)} %copy.41), kind=kLoop, calls=%fused_computation.12 | loop fusion | flops 1178880 | bytes 68608 | tf_op jit(solution)/shard_map/reduce_sum | solution.py:342
  43.1 1.2 %fusion.14 = pred[16,48,64]{2,1,0:T(8,128)(4,1)S(1)} fusion(s32[16,64,8]{1,2,0:T(8,128)S(1)} %copy.41), kind=kLoop, calls=%fused_computation.14 | loop fusion | flops 737280 | bytes 81920 | tf_op jit(solution)/shard_map/reduce_or | solution.py:341
  44.3 3.3 %fusion.15 = bf16[2,16,24,2048]{3,2,0,1:T(8,128)(2,1)S(1)} fusion(pred[2,16,24,64]{3,2,0,1:T(8,128)(4,1)S(1)} %bitcast.41, bf16[16,64,2176]{2,1,0:T(8,128)(2,1)} %copy-done), kind=kOutput, calls=%fused_computation.15 | convolution fusion | flops 202899456 | bytes 7389184 | tf_op jit(solution)/shard_map/esmt,std->esmd/dot_general | solution.py:345
  47.7 1.8 %fusion.2 = f32[2,16,24,512]{3,2,1,0:T(8,128)S(1)} fusion(bf16[2,2048,512]{2,1,0:T(8,128)(2,1)S(1)} %copy-done.2, bf16[2,16,24,2048]{3,2,0,1:T(8,128)(2,1)S(1)} %fusion.15), kind=kOutput, calls=%fused_computation.4 | convolution fusion | flops 1610612736 | bytes 8912896 | tf_op jit(solution)/shard_map/esmd,edf->esmf/dot_general | solution.py:348
  49.5 0.3 copy-done.3
  49.9 2.0 %multiply_convert_fusion.1 = bf16[2,16,24,512]{3,2,1,0:T(8,128)(2,1)S(1)} fusion(f32[2,16,24,512]{3,2,1,0:T(8,128)S(1)} %fusion.2, bf16[2,2048,512]{2,1,0:T(8,128)(2,1)S(1)} %copy-done.3, bf16[2,16,24,2048]{3,2,0,1:T(8,128)(2,1)S(1)} %fusion.15), kind=kOutput, calls=%fused_computation.18 | convolution fusion | flops 1612972032 | bytes 9699328 | tf_op jit(solution)/shard_map/esmd,edf->esmf/dot_general | solution.py:349
  52.1 1.8 %multiply_convert_fusion = bf16[2,16,24,2048]{3,2,0,1:T(8,128)(2,1)S(1)} fusion(bf16[2,512,2048]{2,1,0:T(8,128)(2,1)S(1)} %copy-done.4, f32[2,16,24]{2,0,1:T(2,128)S(1)} %bitcast.43, bf16[2,16,24,512]{3,2,1,0:T(8,128)(2,1)S(1)} %multiply_convert_fusion.1), kind=kOutput, calls=%fused_computation.1 | convolution fusion | flops 1613758464 | bytes 8129536 | tf_op jit(solution)/shard_map/esmf,efd->esmd/dot_general | solution.py:351
  53.9 1.3 %bitcast_convert_fusion = bf16[16,64,2048]{2,1,0:T(8,128)(2,1)S(1)} fusion(pred[2,16,24,64]{3,2,0,1:T(8,128)(4,1)S(1)} %bitcast.42, bf16[2,16,24,2048]{3,2,0,1:T(8,128)(2,1)S(1)} %multiply_convert_fusion), kind=kOutput, calls=%fused_computation | convolution fusion | flops 203423744 | bytes 7389184 | tf_op jit(solution)/shard_map/esmt,esmd->std/dot_general | solution.py:354
  55.2 27.4 %shard_map.105.mixed_ref = bf16[64,2048]{1,0:T(8,128)(2,1)S(1)} custom-call(bf16[2,8,64,2048]{3,2,1,0:T(8,128)(2,1)S(1)} %bitcast.40), custom_call_target="tpu_custom_call" | custom-call | tf_op jit(solution)/shard_map/pallas_call | solution.py:271
  82.7 0.7 copy-done.1
  83.4 6.9 %shard_map.106 = f32[8,128]{1,0:T(8,128)} custom-call(bf16[64,2048]{1,0:T(8,128)(2,1)} %copy-done.1, f32[1,2048]{1,0:T(1,128)} %bitcast.44), custom_call_target="tpu_custom_call" | custom-call | tf_op jit(solution)/shard_map/pallas_call | solution.py:289
  90.2 1.3 %slice_reduce_fusion.2 = f32[4]{0:T(128)} fusion(f32[8,128]{1,0:T(8,128)} %shard_map.106), kind=kLoop, calls=%fused_computation.56 | loop fusion | bytes 32 | tf_op jit(solution)/shard_map/slice | solution.py:361
  91.5 1.7 %copy.60 = bf16[64,2048]{1,0:T(8,128)(2,1)} copy(bf16[64,2048]{1,0:T(8,128)(2,1)} %copy-done.1) | data formatting | bytes 524288
  (21 shorter events, 1.6 us)
Async XLA Ops:
  37.7 2.0 %copy-start = (bf16[16,64,2176]{2,1,0:T(8,128)(2,1)}, bf16[16,64,2176]{2,1,0:T(8,128)(2,1)S(1)}, u32[]{:S(2)}) copy-start(bf16[16,64,2176]{2,1,0:T(8,128)(2,1)S(1)} %shard_map.104) | copy-start | bytes 13369348
  44.2 3.5 %copy-start.2 = (bf16[2,2048,512]{2,1,0:T(8,128)(2,1)S(1)}, bf16[2,2048,512]{2,1,0:T(8,128)(2,1)}, u32[]{:S(2)}) copy-start(bf16[2,2048,512]{2,1,0:T(8,128)(2,1)} %param.14) | copy-start | bytes 12582916
  47.7 2.2 %copy-start.3 = (bf16[2,2048,512]{2,1,0:T(8,128)(2,1)S(1)}, bf16[2,2048,512]{2,1,0:T(8,128)(2,1)}, u32[]{:S(2)}) copy-start(bf16[2,2048,512]{2,1,0:T(8,128)(2,1)} %param.15) | copy-start | bytes 12582916
  49.9 2.2 %copy-start.4 = (bf16[2,512,2048]{2,1,0:T(8,128)(2,1)S(1)}, bf16[2,512,2048]{2,1,0:T(8,128)(2,1)}, u32[]{:S(2)}) copy-start(bf16[2,512,2048]{2,1,0:T(8,128)(2,1)} %param.16) | copy-start | bytes 12582916
  82.7 0.7 copy-start.1

commit v20 on v13

--- a/solution.py
+++ b/solution.py
@@ -323,9 +323,11 @@
         local_key[:, None, :, :] == jnp.arange(local_count, dtype=jnp.int32)[None, :, None, None]
     )
     picker = jnp.any(match, axis=3).astype(jnp.bfloat16)
-    slot_weight = jnp.sum(jnp.where(match, weight_cube[:, None, :, :], 0.0), axis=(2, 3))
     picker = picker.reshape(expert_count, per_device, MOST, tok_rows).transpose(1, 0, 2, 3)
-    slot_weight = slot_weight.reshape(expert_count, per_device, MOST).transpose(1, 0, 2)
+    token_weight = jnp.stack(
+        [jnp.sum(jnp.where(local_slot == e, weight_cube, 0.0), axis=2) for e in range(per_device)]
+    )
+    slot_weight = jnp.sum(picker.astype(jnp.float32) * token_weight[:, :, None, :], axis=3)
     row_block = jnp.einsum(
         "esmt,std->esmd", picker, inputs_all, preferred_element_type=jnp.float32
     ).astype(jnp.bfloat16)

time: 89.3 us -> 92 us (1.030)
  other arithmetic: 6.68 us -> 9.73 us
    div x1, other arithmetic: 0.47 us -> 5.46 us  [body(): weight_cube = fixed_val / jnp.sum(fixed_val, axis=2, keepdims=True)]
    reduce_sum x2 -> x1, other arithmetic: 2.15 us -> 0.2 us  [body(): jnp.sum(picker.astype(jnp.float32) * token_weight[:, :, None, :], axis=3)]
where the time goes in v20:
time: 92 us; the launch traced here: 91.7 us
  Pallas kernels  63.7 us (69%)
  matrix products  10.5 us (11%)
  other arithmetic  9.73 us (11%)
  local copies, waits for them, and re-layouts  6.88 us (7%)
    pallas_call x1, Pallas kernels, scatter_sums(): pl.pallas_call(functools.partial(combine_kernel, z_count, dp_count, seq_l...  32.5 us
    pallas_call x1, Pallas kernels, gather_blocks(): pl.pallas_call(functools.partial(dispatch_kernel, z_count, chunks), out_s...  31.3 us
    div x1, other arithmetic, body(): weight_cube = fixed_val / jnp.sum(fixed_val, axis=2, keepdims=True)  5.46 us
    unnamed x13, local copies, waits for them, and re-layouts  4.81 us
    dot_general x1, matrix products, body(): jnp.einsum('esmt,std->esmd', picker, inputs_all, preferred_element_type=j...  3.29 us
    dot_general x1, matrix products, body(): jnp.einsum('esmd,edf->esmf', row_block, w_up, preferred_element_type=jnp....  1.99 us
    dot_general x1, matrix products, body(): jnp.einsum('esmf,efd->esmd', hidden, w_down, preferred_element_type=jnp.f...  1.84 us
    dot_general x1, matrix products, body(): jnp.einsum('esmd,edf->esmf', row_block, w_gate, preferred_element_type=jn...  1.84 us

profile of v20, /device:TPU:2, one launch (start us, length us, event | category | flops | bytes accessed | tf_op | source)
XLA Modules:
  0.0 91.7 jit_solution(10914180927326731980)
XLA Ops:
  0.6 0.7 broadcast_compare_fusion
  1.5 0.7 convert.15
  2.2 0.8 slice_reduce_fusion.1
  3.1 0.8 copy.25
  3.9 0.8 copy.24
  4.8 0.3 fusion.26
  5.2 1.1 %add_convert_fusion = bf16[64,2048]{1,0:T(8,128)(2,1)S(1)} fusion(bf16[64,2048]{1,0:T(8,128)(2,1)} %param.9, pred[64]{0:T(512)(128)(4,1)S(1)} %eq.56, bf16[2048]{0:T(1024)(128)(2,1)S(1)} %get-tuple-element.9, bf16[2048]{0:T(1024)(128)(2,1)S(1)} %get-tuple-element.8), kind=kLoop, calls=%fused_computation.32 | loop fusion | flops 655360 | bytes 532544 | tf_op jit(solution)/shard_map/convert_element_type | solution.py:301
  6.4 31.3 %shard_map.104 = bf16[16,64,2176]{2,1,0:T(8,128)(2,1)S(1)} custom-call(bf16[64,2176]{1,0:T(8,128)(2,1)S(1)} %pad_maximum_fusion.blk_ref), custom_call_target="tpu_custom_call" | custom-call | tf_op jit(solution)/shard_map/pallas_call | solution.py:116
  37.7 2.0 %copy-done = bf16[16,64,2176]{2,1,0:T(8,128)(2,1)} copy-done((bf16[16,64,2176]{2,1,0:T(8,128)(2,1)}, bf16[16,64,2176]{2,1,0:T(8,128)(2,1)S(1)}, u32[]{:S(2)}) %copy-start) | copy-done | bytes 4456472
  39.8 5.5 %select_reduce_fusion.1 = (f32[16,64]{1,0:T(8,128)S(1)}, f32[16,64]{1,0:T(8,128)S(1)}) fusion(s32[16,64,32]{2,1,0:T(8,128)S(1)} %slice_convert_fusion, s32[]{:T(128)S(6)} %mul.42), kind=kOutput, calls=%fused_computation.31 | output fusion | flops 89095 | bytes 1581060 | tf_op jit(solution)/shard_map/div | solution.py:316
  45.2 0.2 fusion.29
  45.4 0.2 copy.30
  45.6 1.2 %fusion.15 = pred[16,48,64]{2,1,0:T(8,128)(4,1)S(1)} fusion(s32[16,64,8]{1,2,0:T(8,128)S(1)} %copy.30), kind=kLoop, calls=%fused_computation.14 | loop fusion | flops 737280 | bytes 81920 | tf_op jit(solution)/shard_map/reduce_or | solution.py:325
  46.8 3.3 %fusion.16 = bf16[2,16,24,2048]{3,2,0,1:T(8,128)(2,1)S(1)} fusion(pred[2,16,24,64]{3,2,0,1:T(8,128)(4,1)S(1)} %bitcast.43, bf16[16,64,2176]{2,1,0:T(8,128)(2,1)} %copy-done), kind=kOutput, calls=%fused_computation.15 | convolution fusion | flops 202899456 | bytes 7389184 | tf_op jit(solution)/shard_map/esmt,std->esmd/dot_general | solution.py:331
  50.1 0.2 multiply_reduce_fusion
  50.4 1.8 %fusion.3 = f32[2,16,24,512]{3,2,1,0:T(8,128)S(1)} fusion(bf16[2,2048,512]{2,1,0:T(8,128)(2,1)S(1)} %copy-done.2, bf16[2,16,24,2048]{3,2,0,1:T(8,128)(2,1)S(1)} %fusion.16), kind=kOutput, calls=%fused_computation.5 | convolution fusion | flops 1610612736 | bytes 8912896 | tf_op jit(solution)/shard_map/esmd,edf->esmf/dot_general | solution.py:334
  52.2 0.3 copy-done.3
  52.6 2.0 %multiply_convert_fusion.1 = bf16[2,16,24,512]{3,2,1,0:T(8,128)(2,1)S(1)} fusion(f32[2,16,24,512]{3,2,1,0:T(8,128)S(1)} %fusion.3, bf16[2,2048,512]{2,1,0:T(8,128)(2,1)S(1)} %copy-done.3, bf16[2,16,24,2048]{3,2,0,1:T(8,128)(2,1)S(1)} %fusion.16), kind=kOutput, calls=%fused_computation.18 | convolution fusion | flops 1612972032 | bytes 9699328 | tf_op jit(solution)/shard_map/esmd,edf->esmf/dot_general | solution.py:335
  54.6 0.2 copy-done.4
  54.7 1.8 %multiply_convert_fusion = bf16[2,16,24,2048]{3,2,0,1:T(8,128)(2,1)S(1)} fusion(bf16[2,512,2048]{2,1,0:T(8,128)(2,1)S(1)} %copy-done.4, f32[2,16,24]{2,0,1:T(2,128)S(1)} %multiply_reduce_fusion, bf16[2,16,24,512]{3,2,1,0:T(8,128)(2,1)S(1)} %multiply_convert_fusion.1), kind=kOutput, calls=%fused_computation.2 | convolution fusion | flops 1613758464 | bytes 8129536 | tf_op jit(solution)/shard_map/esmf,efd->esmd/dot_general | solution.py:337
  56.6 1.3 %bitcast_convert_fusion = bf16[16,64,2048]{2,1,0:T(8,128)(2,1)S(1)} fusion(pred[2,16,24,64]{3,2,0,1:T(8,128)(4,1)S(1)} %bitcast.45, bf16[2,16,24,2048]{3,2,0,1:T(8,128)(2,1)S(1)} %multiply_convert_fusion), kind=kOutput, calls=%fused_computation.1 | convolution fusion | flops 203423744 | bytes 7389184 | tf_op jit(solution)/shard_map/esmt,esmd->std/dot_general | solution.py:340
  57.9 32.5 %shard_map.105 = (bf16[64,2048]{1,0:T(8,128)(2,1)S(1)}, f32[8,128]{1,0:T(8,128)S(1)}) custom-call(bf16[2,8,64,2048]{3,2,1,0:T(8,128)(2,1)S(1)} %bitcast.41, f32[1,2048]{1,0:T(1,128)S(1)} %bitcast.42), custom_call_target="tpu_custom_call" | custom-call | tf_op jit(solution)/shard_map/pallas_call | solution.py:262
  90.4 0.6 slice_reduce_fusion.2
  91.0 0.7 copy.47
  (18 shorter events, 0.7 us)
Async XLA Ops:
  37.7 2.0 %copy-start = (bf16[16,64,2176]{2,1,0:T(8,128)(2,1)}, bf16[16,64,2176]{2,1,0:T(8,128)(2,1)S(1)}, u32[]{:S(2)}) copy-start(bf16[16,64,2176]{2,1,0:T(8,128)(2,1)S(1)} %shard_map.104) | copy-start | bytes 13369348
  46.8 3.5 %copy-start.2 = (bf16[2,2048,512]{2,1,0:T(8,128)(2,1)S(1)}, bf16[2,2048,512]{2,1,0:T(8,128)(2,1)}, u32[]{:S(2)}) copy-start(bf16[2,2048,512]{2,1,0:T(8,128)(2,1)} %param.14) | copy-start | bytes 12582916
  50.4 2.2 %copy-start.3 = (bf16[2,2048,512]{2,1,0:T(8,128)(2,1)S(1)}, bf16[2,2048,512]{2,1,0:T(8,128)(2,1)}, u32[]{:S(2)}) copy-start(bf16[2,2048,512]{2,1,0:T(8,128)(2,1)} %param.15) | copy-start | bytes 12582916
  52.6 2.2 %copy-start.4 = (bf16[2,512,2048]{2,1,0:T(8,128)(2,1)S(1)}, bf16[2,512,2048]{2,1,0:T(8,128)(2,1)}, u32[]{:S(2)}) copy-start(bf16[2,512,2048]{2,1,0:T(8,128)(2,1)} %param.16) | copy-start | bytes 12582916
  56.6 1.3 %copy-start.1 = (f32[2048]{0:T(1024)S(1)}, f32[2048]{0:T(1024)}, u32[]{:S(2)}) copy-start(f32[2048]{0:T(1024)} %param.17) | copy-start | bytes 24580

commit v21 on v15

--- a/solution.py
+++ b/solution.py
@@ -357,7 +357,7 @@
     )
     partial_value = partial_value.reshape(c_count, z_count, tok_rows, model_width)
     mixed, pair_tile = scatter_sums(
-        partial_value.astype(jnp.bfloat16), score_head, lax.axis_size("dp"), SEQ_LEN, 2
+        partial_value.astype(jnp.bfloat16), score_head, lax.axis_size("dp"), SEQ_LEN, 1
     )
     pair_score = pair_tile[: tok_rows // SEQ_LEN, 0]
     return (mixed, pair_score)

time: 89.1 us -> 94 us (1.055)
  Pallas kernels: 63.3 us -> 68.2 us
    pallas_call x1, Pallas kernels: 32.5 us -> 37.4 us  [scatter_sums(): pl.pallas_call(functools.partial(combine_kernel, z_count, dp_count, seq_l...]
where the time goes in v21:
time: 94 us; the launch traced here: 93.7 us
  Pallas kernels  68.2 us (73%)
  matrix products  10.5 us (11%)
  local copies, waits for them, and re-layouts  7.63 us (8%)
  other arithmetic  6.5 us (7%)
    pallas_call x1, Pallas kernels, scatter_sums(): pl.pallas_call(functools.partial(combine_kernel, z_count, dp_count, seq_l...  37.4 us
    pallas_call x1, Pallas kernels, gather_blocks(): pl.pallas_call(functools.partial(dispatch_kernel, z_count, chunks), out_s...  30.8 us
    unnamed x15, local copies, waits for them, and re-layouts  5.2 us
    dot_general x1, matrix products, body(): jnp.einsum('esmt,std->esmd', picker, inputs_all, preferred_element_type=j...  3.29 us
    dot_general x1, matrix products, body(): jnp.einsum('esmd,edf->esmf', row_block, w_up, preferred_element_type=jnp....  2 us

profile of v21, /device:TPU:2, one launch (start us, length us, event | category | flops | bytes accessed | tf_op | source)
XLA Modules:
  0.0 93.7 jit_solution(148047107627955322)
XLA Ops:
  0.6 0.7 broadcast_compare_fusion
  1.5 0.7 convert.14
  2.2 0.8 slice_reduce_fusion.1
  3.1 0.8 copy.32
  3.9 0.8 copy.31
  4.8 0.3 fusion.23
  5.3 1.1 %add_convert_fusion.blk_ref = bf16[64,2048]{1,0:T(8,128)(2,1)S(1)} fusion(bf16[64,2048]{1,0:T(8,128)(2,1)} %param.9, pred[64]{0:T(512)(128)(4,1)S(1)} %eq.47, bf16[2048]{0:T(1024)(128)(2,1)S(1)} %get-tuple-element.11, bf16[2048]{0:T(1024)(128)(2,1)S(1)} %get-tuple-element.10), kind=kLoop, calls=%fused_computation.25 | loop fusion | flops 655360 | bytes 532544 | tf_op jit(solution)/shard_map/convert_element_type | solution.py:320
  6.4 30.8 %shard_map.104 = (bf16[16,64,2048]{2,1,0:T(8,128)(2,1)S(1)}, bf16[16,16,128]{2,1,0:T(8,128)(2,1)S(1)}) custom-call(bf16[64,2048]{1,0:T(8,128)(2,1)S(1)} %add_convert_fusion.blk_ref, bf16[16,128]{1,0:T(8,128)(2,1)S(1)} %convert_element_type.55.rt_ref), custom_call_target="tpu_custom_call" | custom-call | tf_op jit(solution)/shard_map/pallas_call | solution.py:131
  37.3 1.9 %copy-done = bf16[16,64,2048]{2,1,0:T(8,128)(2,1)} copy-done((bf16[16,64,2048]{2,1,0:T(8,128)(2,1)}, bf16[16,64,2048]{2,1,0:T(8,128)(2,1)S(1)}, u32[]{:S(2)}) %copy-start) | copy-done | bytes 4194328
  39.4 0.5 fusion.42
  40.0 0.2 copy.37
  40.2 0.2 copy.48
  40.4 0.6 convert_divide_fusion
  41.0 1.6 %select_reduce_fusion = f32[16,48]{1,0:T(8,128)S(1)} fusion(f32[16,64,8]{1,2,0:T(8,128)S(1)} %convert_divide_fusion, s32[16,64,8]{1,2,0:T(8,128)S(1)} %copy.37), kind=kLoop, calls=%fused_computation.11 | loop fusion | flops 1178880 | bytes 68608 | tf_op jit(solution)/shard_map/reduce_sum | solution.py:343
  42.8 1.2 %fusion.13 = pred[16,48,64]{2,1,0:T(8,128)(4,1)S(1)} fusion(s32[16,64,8]{1,2,0:T(8,128)S(1)} %copy.37), kind=kLoop, calls=%fused_computation.13 | loop fusion | flops 737280 | bytes 81920 | tf_op jit(solution)/shard_map/reduce_or | solution.py:342
  44.0 3.3 %fusion.14 = bf16[2,16,24,2048]{3,2,0,1:T(8,128)(2,1)S(1)} fusion(pred[2,16,24,64]{3,2,0,1:T(8,128)(4,1)S(1)} %bitcast.42, bf16[16,64,2048]{2,1,0:T(8,128)(2,1)} %copy-done), kind=kOutput, calls=%fused_computation.14 | convolution fusion | flops 202899456 | bytes 7389184 | tf_op jit(solution)/shard_map/esmt,std->esmd/dot_general | solution.py:346
  47.4 1.8 %fusion.2 = f32[2,16,24,512]{3,2,1,0:T(8,128)S(1)} fusion(bf16[2,2048,512]{2,1,0:T(8,128)(2,1)S(1)} %copy-done.2, bf16[2,16,24,2048]{3,2,0,1:T(8,128)(2,1)S(1)} %fusion.14), kind=kOutput, calls=%fused_computation.4 | convolution fusion | flops 1610612736 | bytes 8912896 | tf_op jit(solution)/shard_map/esmd,edf->esmf/dot_general | solution.py:349
  49.3 0.3 copy-done.3
  49.6 2.0 %multiply_convert_fusion.1 = bf16[2,16,24,512]{3,2,1,0:T(8,128)(2,1)S(1)} fusion(f32[2,16,24,512]{3,2,1,0:T(8,128)S(1)} %fusion.2, bf16[2,2048,512]{2,1,0:T(8,128)(2,1)S(1)} %copy-done.3, bf16[2,16,24,2048]{3,2,0,1:T(8,128)(2,1)S(1)} %fusion.14), kind=kOutput, calls=%fused_computation.17 | convolution fusion | flops 1612972032 | bytes 9699328 | tf_op jit(solution)/shard_map/esmd,edf->esmf/dot_general | solution.py:350
  51.8 1.8 %multiply_convert_fusion = bf16[2,16,24,2048]{3,2,0,1:T(8,128)(2,1)S(1)} fusion(bf16[2,512,2048]{2,1,0:T(8,128)(2,1)S(1)} %copy-done.4, f32[2,16,24]{2,0,1:T(2,128)S(1)} %bitcast.44, bf16[2,16,24,512]{3,2,1,0:T(8,128)(2,1)S(1)} %multiply_convert_fusion.1), kind=kOutput, calls=%fused_computation.1 | convolution fusion | flops 1613758464 | bytes 8129536 | tf_op jit(solution)/shard_map/esmf,efd->esmd/dot_general | solution.py:352
  53.6 1.3 %bitcast_convert_fusion = bf16[16,64,2048]{2,1,0:T(8,128)(2,1)S(1)} fusion(pred[2,16,24,64]{3,2,0,1:T(8,128)(4,1)S(1)} %bitcast.43, bf16[2,16,24,2048]{3,2,0,1:T(8,128)(2,1)S(1)} %multiply_convert_fusion), kind=kOutput, calls=%fused_computation | convolution fusion | flops 203423744 | bytes 7389184 | tf_op jit(solution)/shard_map/esmt,esmd->std/dot_general | solution.py:355
  54.9 37.4 %shard_map.105 = (bf16[64,2048]{1,0:T(8,128)(2,1)S(1)}, f32[8,128]{1,0:T(8,128)S(1)}) custom-call(bf16[2,8,64,2048]{3,2,1,0:T(8,128)(2,1)S(1)} %bitcast.40, f32[1,2048]{1,0:T(1,128)S(1)} %bitcast.41), custom_call_target="tpu_custom_call" | custom-call | tf_op jit(solution)/shard_map/pallas_call | solution.py:281
  92.3 0.6 slice_reduce_fusion.2
  93.0 0.7 copy.58
  (21 shorter events, 1.5 us)
Async XLA Ops:
  37.3 1.9 %copy-start = (bf16[16,64,2048]{2,1,0:T(8,128)(2,1)}, bf16[16,64,2048]{2,1,0:T(8,128)(2,1)S(1)}, u32[]{:S(2)}) copy-start(bf16[16,64,2048]{2,1,0:T(8,128)(2,1)S(1)} %get-tuple-element.7) | copy-start | bytes 12582916
  44.0 3.5 %copy-start.2 = (bf16[2,2048,512]{2,1,0:T(8,128)(2,1)S(1)}, bf16[2,2048,512]{2,1,0:T(8,128)(2,1)}, u32[]{:S(2)}) copy-start(bf16[2,2048,512]{2,1,0:T(8,128)(2,1)} %param.14) | copy-start | bytes 12582916
  47.4 2.2 %copy-start.3 = (bf16[2,2048,512]{2,1,0:T(8,128)(2,1)S(1)}, bf16[2,2048,512]{2,1,0:T(8,128)(2,1)}, u32[]{:S(2)}) copy-start(bf16[2,2048,512]{2,1,0:T(8,128)(2,1)} %param.15) | copy-start | bytes 12582916
  49.6 2.2 %copy-start.4 = (bf16[2,512,2048]{2,1,0:T(8,128)(2,1)S(1)}, bf16[2,512,2048]{2,1,0:T(8,128)(2,1)}, u32[]{:S(2)}) copy-start(bf16[2,512,2048]{2,1,0:T(8,128)(2,1)} %param.16) | copy-start | bytes 12582916
  53.6 1.3 %copy-start.1 = (f32[2048]{0:T(1024)S(1)}, f32[2048]{0:T(1024)}, u32[]{:S(2)}) copy-start(f32[2048]{0:T(1024)} %param.17) | copy-start | bytes 24580

commit v22 on v21

--- a/solution.py
+++ b/solution.py
@@ -357,7 +357,7 @@
     )
     partial_value = partial_value.reshape(c_count, z_count, tok_rows, model_width)
     mixed, pair_tile = scatter_sums(
-        partial_value.astype(jnp.bfloat16), score_head, lax.axis_size("dp"), SEQ_LEN, 1
+        partial_value.astype(jnp.bfloat16), score_head, lax.axis_size("dp"), SEQ_LEN, 4
     )
     pair_score = pair_tile[: tok_rows // SEQ_LEN, 0]
     return (mixed, pair_score)

time: 94 us -> 88.6 us (0.943)
  Pallas kernels: 68.2 us -> 62.8 us
    pallas_call x1, Pallas kernels: 37.4 us -> 32 us  [scatter_sums(): pl.pallas_call(functools.partial(combine_kernel, z_count, dp_count, seq_l...]
where the time goes in v22:
time: 88.6 us; the launch traced here: 88.2 us
  Pallas kernels  62.8 us (71%)
  matrix products  10.5 us (12%)
  local copies, waits for them, and re-layouts  7.63 us (9%)
  other arithmetic  6.5 us (7%)
    pallas_call x1, Pallas kernels, scatter_sums(): pl.pallas_call(functools.partial(combine_kernel, z_count, dp_count, seq_l...  32 us
    pallas_call x1, Pallas kernels, gather_blocks(): pl.pallas_call(functools.partial(dispatch_kernel, z_count, chunks), out_s...  30.8 us
    unnamed x15, local copies, waits for them, and re-layouts  5.2 us
    dot_general x1, matrix products, body(): jnp.einsum('esmt,std->esmd', picker, inputs_all, preferred_element_type=j...  3.29 us
    dot_general x1, matrix products, body(): jnp.einsum('esmd,edf->esmf', row_block, w_up, preferred_element_type=jnp....  2 us
    dot_general x1, matrix products, body(): jnp.einsum('esmd,edf->esmf', row_block, w_gate, preferred_element_type=jn...  1.84 us
    dot_general x1, matrix products, body(): jnp.einsum('esmf,efd->esmd', hidden, w_down, preferred_element_type=jnp.f...  1.82 us

profile of v22, /device:TPU:2, one launch (start us, length us, event | category | flops | bytes accessed | tf_op | source)
XLA Modules:
  0.0 88.2 jit_solution(7249146528080605034)
XLA Ops:
  0.6 0.7 broadcast_compare_fusion
  1.5 0.7 convert.14
  2.2 0.8 slice_reduce_fusion.1
  3.1 0.8 copy.32
  3.9 0.8 copy.31
  4.8 0.3 fusion.23
  5.3 1.1 %add_convert_fusion.blk_ref = bf16[64,2048]{1,0:T(8,128)(2,1)S(1)} fusion(bf16[64,2048]{1,0:T(8,128)(2,1)} %param.9, pred[64]{0:T(512)(128)(4,1)S(1)} %eq.47, bf16[2048]{0:T(1024)(128)(2,1)S(1)} %get-tuple-element.11, bf16[2048]{0:T(1024)(128)(2,1)S(1)} %get-tuple-element.10), kind=kLoop, calls=%fused_computation.25 | loop fusion | flops 655360 | bytes 532544 | tf_op jit(solution)/shard_map/convert_element_type | solution.py:320
  6.4 30.8 %shard_map.104 = (bf16[16,64,2048]{2,1,0:T(8,128)(2,1)S(1)}, bf16[16,16,128]{2,1,0:T(8,128)(2,1)S(1)}) custom-call(bf16[64,2048]{1,0:T(8,128)(2,1)S(1)} %add_convert_fusion.blk_ref, bf16[16,128]{1,0:T(8,128)(2,1)S(1)} %convert_element_type.55.rt_ref), custom_call_target="tpu_custom_call" | custom-call | tf_op jit(solution)/shard_map/pallas_call | solution.py:131
  37.3 1.9 %copy-done = bf16[16,64,2048]{2,1,0:T(8,128)(2,1)} copy-done((bf16[16,64,2048]{2,1,0:T(8,128)(2,1)}, bf16[16,64,2048]{2,1,0:T(8,128)(2,1)S(1)}, u32[]{:S(2)}) %copy-start) | copy-done | bytes 4194328
  39.4 0.5 fusion.42
  40.0 0.2 copy.37
  40.2 0.2 copy.48
  40.4 0.6 convert_divide_fusion
  41.0 1.6 %select_reduce_fusion = f32[16,48]{1,0:T(8,128)S(1)} fusion(f32[16,64,8]{1,2,0:T(8,128)S(1)} %convert_divide_fusion, s32[16,64,8]{1,2,0:T(8,128)S(1)} %copy.37), kind=kLoop, calls=%fused_computation.11 | loop fusion | flops 1178880 | bytes 68608 | tf_op jit(solution)/shard_map/reduce_sum | solution.py:343
  42.8 1.2 %fusion.13 = pred[16,48,64]{2,1,0:T(8,128)(4,1)S(1)} fusion(s32[16,64,8]{1,2,0:T(8,128)S(1)} %copy.37), kind=kLoop, calls=%fused_computation.13 | loop fusion | flops 737280 | bytes 81920 | tf_op jit(solution)/shard_map/reduce_or | solution.py:342
  44.0 3.3 %fusion.14 = bf16[2,16,24,2048]{3,2,0,1:T(8,128)(2,1)S(1)} fusion(pred[2,16,24,64]{3,2,0,1:T(8,128)(4,1)S(1)} %bitcast.42, bf16[16,64,2048]{2,1,0:T(8,128)(2,1)} %copy-done), kind=kOutput, calls=%fused_computation.14 | convolution fusion | flops 202899456 | bytes 7389184 | tf_op jit(solution)/shard_map/esmt,std->esmd/dot_general | solution.py:346
  47.4 1.8 %fusion.2 = f32[2,16,24,512]{3,2,1,0:T(8,128)S(1)} fusion(bf16[2,2048,512]{2,1,0:T(8,128)(2,1)S(1)} %copy-done.2, bf16[2,16,24,2048]{3,2,0,1:T(8,128)(2,1)S(1)} %fusion.14), kind=kOutput, calls=%fused_computation.4 | convolution fusion | flops 1610612736 | bytes 8912896 | tf_op jit(solution)/shard_map/esmd,edf->esmf/dot_general | solution.py:349
  49.3 0.3 copy-done.3
  49.6 2.0 %multiply_convert_fusion.1 = bf16[2,16,24,512]{3,2,1,0:T(8,128)(2,1)S(1)} fusion(f32[2,16,24,512]{3,2,1,0:T(8,128)S(1)} %fusion.2, bf16[2,2048,512]{2,1,0:T(8,128)(2,1)S(1)} %copy-done.3, bf16[2,16,24,2048]{3,2,0,1:T(8,128)(2,1)S(1)} %fusion.14), kind=kOutput, calls=%fused_computation.17 | convolution fusion | flops 1612972032 | bytes 9699328 | tf_op jit(solution)/shard_map/esmd,edf->esmf/dot_general | solution.py:350
  51.8 1.8 %multiply_convert_fusion = bf16[2,16,24,2048]{3,2,0,1:T(8,128)(2,1)S(1)} fusion(bf16[2,512,2048]{2,1,0:T(8,128)(2,1)S(1)} %copy-done.4, f32[2,16,24]{2,0,1:T(2,128)S(1)} %bitcast.44, bf16[2,16,24,512]{3,2,1,0:T(8,128)(2,1)S(1)} %multiply_convert_fusion.1), kind=kOutput, calls=%fused_computation.1 | convolution fusion | flops 1613758464 | bytes 8129536 | tf_op jit(solution)/shard_map/esmf,efd->esmd/dot_general | solution.py:352
  53.6 1.3 %bitcast_convert_fusion = bf16[16,64,2048]{2,1,0:T(8,128)(2,1)S(1)} fusion(pred[2,16,24,64]{3,2,0,1:T(8,128)(4,1)S(1)} %bitcast.43, bf16[2,16,24,2048]{3,2,0,1:T(8,128)(2,1)S(1)} %multiply_convert_fusion), kind=kOutput, calls=%fused_computation | convolution fusion | flops 203423744 | bytes 7389184 | tf_op jit(solution)/shard_map/esmt,esmd->std/dot_general | solution.py:355
  54.9 32.0 %shard_map.105 = (bf16[64,2048]{1,0:T(8,128)(2,1)S(1)}, f32[8,128]{1,0:T(8,128)S(1)}) custom-call(bf16[2,8,64,2048]{3,2,1,0:T(8,128)(2,1)S(1)} %bitcast.40, f32[1,2048]{1,0:T(1,128)S(1)} %bitcast.41), custom_call_target="tpu_custom_call" | custom-call | tf_op jit(solution)/shard_map/pallas_call | solution.py:281
  86.9 0.6 slice_reduce_fusion.2
  87.5 0.7 copy.58
  (21 shorter events, 1.5 us)
Async XLA Ops:
  37.3 1.9 %copy-start = (bf16[16,64,2048]{2,1,0:T(8,128)(2,1)}, bf16[16,64,2048]{2,1,0:T(8,128)(2,1)S(1)}, u32[]{:S(2)}) copy-start(bf16[16,64,2048]{2,1,0:T(8,128)(2,1)S(1)} %get-tuple-element.7) | copy-start | bytes 12582916
  44.0 3.5 %copy-start.2 = (bf16[2,2048,512]{2,1,0:T(8,128)(2,1)S(1)}, bf16[2,2048,512]{2,1,0:T(8,128)(2,1)}, u32[]{:S(2)}) copy-start(bf16[2,2048,512]{2,1,0:T(8,128)(2,1)} %param.14) | copy-start | bytes 12582916
  47.4 2.2 %copy-start.3 = (bf16[2,2048,512]{2,1,0:T(8,128)(2,1)S(1)}, bf16[2,2048,512]{2,1,0:T(8,128)(2,1)}, u32[]{:S(2)}) copy-start(bf16[2,2048,512]{2,1,0:T(8,128)(2,1)} %param.15) | copy-start | bytes 12582916
  49.6 2.2 %copy-start.4 = (bf16[2,512,2048]{2,1,0:T(8,128)(2,1)S(1)}, bf16[2,512,2048]{2,1,0:T(8,128)(2,1)}, u32[]{:S(2)}) copy-start(bf16[2,512,2048]{2,1,0:T(8,128)(2,1)} %param.16) | copy-start | bytes 12582916
  53.6 1.3 %copy-start.1 = (f32[2048]{0:T(1024)S(1)}, f32[2048]{0:T(1024)}, u32[]{:S(2)}) copy-start(f32[2048]{0:T(1024)} %param.17) | copy-start | bytes 24580

commit v23 on v22

--- a/solution.py
+++ b/solution.py
@@ -237,6 +237,9 @@
                 bwd_out[hop - 1, rows] = total.astype(bwd_out.dtype)
                 sem = bwd_sem + (hop - 1) * chunks + k
                 send(bwd_out.at[hop - 1, rows], bwd_buf.at[hop - 1, rows], sem, bwd_id)
+    width = out_ref.shape[1]
+    per_chunk = piece // seq_len
+    seq_out[...] = jnp.zeros(seq_out.shape, jnp.float32)
     for k in range(chunks):
         rows = pl.ds(k * piece, piece)
         total = own(z, fwd_hops + bwd_hops, k)
@@ -245,14 +248,14 @@
         if bwd_hops > 0:
             arrive(bwd_buf.at[bwd_hops - 1, rows], bwd_sem + (bwd_hops - 1) * chunks + k)
             total = total + bwd_buf[bwd_hops - 1, rows].astype(jnp.float32)
-        out_ref[rows] = total.astype(out_ref.dtype)
-    tok_rows, width = out_ref.shape
-    seqs = tok_rows // seq_len
-    scored = out_ref[...].astype(jnp.float32) * head_ref[...]
-    per_seq = jnp.sum(scored.reshape(seqs, seq_len, width), axis=1)
-    seq_score = jnp.sum(per_seq, axis=1, keepdims=True)
-    seq_out[...] = jnp.zeros(seq_out.shape, jnp.float32)
-    seq_out[pl.ds(0, seqs)] = jnp.broadcast_to(seq_score, (seqs, seq_out.shape[1]))
+        rounded = total.astype(out_ref.dtype)
+        out_ref[rows] = rounded
+        scored = rounded.astype(jnp.float32) * head_ref[...]
+        per_seq = jnp.sum(scored.reshape(per_chunk, seq_len, width), axis=1)
+        seq_score = jnp.sum(per_seq, axis=1, keepdims=True)
+        seq_out[pl.ds(k * per_chunk, per_chunk)] = jnp.broadcast_to(
+            seq_score, (per_chunk, seq_out.shape[1])
+        )
     mate = pltpu.make_async_remote_copy(
         src_ref=seq_out,
         dst_ref=seq_in,

time: 88.6 us -> 88.5 us (level)
  no operation moved by 1% of the time
where the time goes in v23:
time: 88.5 us; the launch traced here: 88.2 us
  Pallas kernels  62.7 us (71%)
  matrix products  10.5 us (12%)
  local copies, waits for them, and re-layouts  7.63 us (9%)
  other arithmetic  6.5 us (7%)
    pallas_call x1, Pallas kernels, scatter_sums(): pl.pallas_call(functools.partial(combine_kernel, z_count, dp_count, seq_l...  31.9 us
    pallas_call x1, Pallas kernels, gather_blocks(): pl.pallas_call(functools.partial(dispatch_kernel, z_count, chunks), out_s...  30.8 us
    unnamed x15, local copies, waits for them, and re-layouts  5.2 us
    dot_general x1, matrix products, body(): jnp.einsum('esmt,std->esmd', picker, inputs_all, preferred_element_type=j...  3.29 us
    dot_general x1, matrix products, body(): jnp.einsum('esmd,edf->esmf', row_block, w_up, preferred_element_type=jnp....  2 us
    dot_general x1, matrix products, body(): jnp.einsum('esmd,edf->esmf', row_block, w_gate, preferred_element_type=jn...  1.84 us
    dot_general x1, matrix products, body(): jnp.einsum('esmf,efd->esmd', hidden, w_down, preferred_element_type=jnp.f...  1.82 us

profile of v23, /device:TPU:2, one launch (start us, length us, event | category | flops | bytes accessed | tf_op | source)
XLA Modules:
  0.0 88.2 jit_solution(17916394959429799590)
XLA Ops:
  0.6 0.7 broadcast_compare_fusion
  1.5 0.7 convert.14
  2.2 0.8 slice_reduce_fusion.1
  3.1 0.8 copy.32
  3.9 0.8 copy.31
  4.8 0.3 fusion.23
  5.3 1.1 %add_convert_fusion.blk_ref = bf16[64,2048]{1,0:T(8,128)(2,1)S(1)} fusion(bf16[64,2048]{1,0:T(8,128)(2,1)} %param.9, pred[64]{0:T(512)(128)(4,1)S(1)} %eq.47, bf16[2048]{0:T(1024)(128)(2,1)S(1)} %get-tuple-element.11, bf16[2048]{0:T(1024)(128)(2,1)S(1)} %get-tuple-element.10), kind=kLoop, calls=%fused_computation.25 | loop fusion | flops 655360 | bytes 532544 | tf_op jit(solution)/shard_map/convert_element_type | solution.py:323
  6.4 30.8 %shard_map.104 = (bf16[16,64,2048]{2,1,0:T(8,128)(2,1)S(1)}, bf16[16,16,128]{2,1,0:T(8,128)(2,1)S(1)}) custom-call(bf16[64,2048]{1,0:T(8,128)(2,1)S(1)} %add_convert_fusion.blk_ref, bf16[16,128]{1,0:T(8,128)(2,1)S(1)} %convert_element_type.55.rt_ref), custom_call_target="tpu_custom_call" | custom-call | tf_op jit(solution)/shard_map/pallas_call | solution.py:131
  37.3 1.9 %copy-done = bf16[16,64,2048]{2,1,0:T(8,128)(2,1)} copy-done((bf16[16,64,2048]{2,1,0:T(8,128)(2,1)}, bf16[16,64,2048]{2,1,0:T(8,128)(2,1)S(1)}, u32[]{:S(2)}) %copy-start) | copy-done | bytes 4194328
  39.4 0.5 fusion.42
  40.0 0.2 copy.37
  40.2 0.2 copy.48
  40.4 0.6 convert_divide_fusion
  41.0 1.6 %select_reduce_fusion = f32[16,48]{1,0:T(8,128)S(1)} fusion(f32[16,64,8]{1,2,0:T(8,128)S(1)} %convert_divide_fusion, s32[16,64,8]{1,2,0:T(8,128)S(1)} %copy.37), kind=kLoop, calls=%fused_computation.11 | loop fusion | flops 1178880 | bytes 68608 | tf_op jit(solution)/shard_map/reduce_sum | solution.py:346
  42.8 1.2 %fusion.13 = pred[16,48,64]{2,1,0:T(8,128)(4,1)S(1)} fusion(s32[16,64,8]{1,2,0:T(8,128)S(1)} %copy.37), kind=kLoop, calls=%fused_computation.13 | loop fusion | flops 737280 | bytes 81920 | tf_op jit(solution)/shard_map/reduce_or | solution.py:345
  44.0 3.3 %fusion.14 = bf16[2,16,24,2048]{3,2,0,1:T(8,128)(2,1)S(1)} fusion(pred[2,16,24,64]{3,2,0,1:T(8,128)(4,1)S(1)} %bitcast.42, bf16[16,64,2048]{2,1,0:T(8,128)(2,1)} %copy-done), kind=kOutput, calls=%fused_computation.14 | convolution fusion | flops 202899456 | bytes 7389184 | tf_op jit(solution)/shard_map/esmt,std->esmd/dot_general | solution.py:349
  47.4 1.8 %fusion.2 = f32[2,16,24,512]{3,2,1,0:T(8,128)S(1)} fusion(bf16[2,2048,512]{2,1,0:T(8,128)(2,1)S(1)} %copy-done.2, bf16[2,16,24,2048]{3,2,0,1:T(8,128)(2,1)S(1)} %fusion.14), kind=kOutput, calls=%fused_computation.4 | convolution fusion | flops 1610612736 | bytes 8912896 | tf_op jit(solution)/shard_map/esmd,edf->esmf/dot_general | solution.py:352
  49.3 0.3 copy-done.3
  49.6 2.0 %multiply_convert_fusion.1 = bf16[2,16,24,512]{3,2,1,0:T(8,128)(2,1)S(1)} fusion(f32[2,16,24,512]{3,2,1,0:T(8,128)S(1)} %fusion.2, bf16[2,2048,512]{2,1,0:T(8,128)(2,1)S(1)} %copy-done.3, bf16[2,16,24,2048]{3,2,0,1:T(8,128)(2,1)S(1)} %fusion.14), kind=kOutput, calls=%fused_computation.17 | convolution fusion | flops 1612972032 | bytes 9699328 | tf_op jit(solution)/shard_map/esmd,edf->esmf/dot_general | solution.py:353
  51.8 1.8 %multiply_convert_fusion = bf16[2,16,24,2048]{3,2,0,1:T(8,128)(2,1)S(1)} fusion(bf16[2,512,2048]{2,1,0:T(8,128)(2,1)S(1)} %copy-done.4, f32[2,16,24]{2,0,1:T(2,128)S(1)} %bitcast.44, bf16[2,16,24,512]{3,2,1,0:T(8,128)(2,1)S(1)} %multiply_convert_fusion.1), kind=kOutput, calls=%fused_computation.1 | convolution fusion | flops 1613758464 | bytes 8129536 | tf_op jit(solution)/shard_map/esmf,efd->esmd/dot_general | solution.py:355
  53.6 1.3 %bitcast_convert_fusion = bf16[16,64,2048]{2,1,0:T(8,128)(2,1)S(1)} fusion(pred[2,16,24,64]{3,2,0,1:T(8,128)(4,1)S(1)} %bitcast.43, bf16[2,16,24,2048]{3,2,0,1:T(8,128)(2,1)S(1)} %multiply_convert_fusion), kind=kOutput, calls=%fused_computation | convolution fusion | flops 203423744 | bytes 7389184 | tf_op jit(solution)/shard_map/esmt,esmd->std/dot_general | solution.py:358
  54.9 31.9 %shard_map.105 = (bf16[64,2048]{1,0:T(8,128)(2,1)S(1)}, f32[8,128]{1,0:T(8,128)S(1)}) custom-call(bf16[2,8,64,2048]{3,2,1,0:T(8,128)(2,1)S(1)} %bitcast.40, f32[1,2048]{1,0:T(1,128)S(1)} %bitcast.41), custom_call_target="tpu_custom_call" | custom-call | tf_op jit(solution)/shard_map/pallas_call | solution.py:284
  86.8 0.6 slice_reduce_fusion.2
  87.5 0.7 copy.58
  (21 shorter events, 1.5 us)
Async XLA Ops:
  37.3 1.9 %copy-start = (bf16[16,64,2048]{2,1,0:T(8,128)(2,1)}, bf16[16,64,2048]{2,1,0:T(8,128)(2,1)S(1)}, u32[]{:S(2)}) copy-start(bf16[16,64,2048]{2,1,0:T(8,128)(2,1)S(1)} %get-tuple-element.7) | copy-start | bytes 12582916
  44.0 3.5 %copy-start.2 = (bf16[2,2048,512]{2,1,0:T(8,128)(2,1)S(1)}, bf16[2,2048,512]{2,1,0:T(8,128)(2,1)}, u32[]{:S(2)}) copy-start(bf16[2,2048,512]{2,1,0:T(8,128)(2,1)} %param.14) | copy-start | bytes 12582916
  47.4 2.2 %copy-start.3 = (bf16[2,2048,512]{2,1,0:T(8,128)(2,1)S(1)}, bf16[2,2048,512]{2,1,0:T(8,128)(2,1)}, u32[]{:S(2)}) copy-start(bf16[2,2048,512]{2,1,0:T(8,128)(2,1)} %param.15) | copy-start | bytes 12582916
  49.6 2.2 %copy-start.4 = (bf16[2,512,2048]{2,1,0:T(8,128)(2,1)S(1)}, bf16[2,512,2048]{2,1,0:T(8,128)(2,1)}, u32[]{:S(2)}) copy-start(bf16[2,512,2048]{2,1,0:T(8,128)(2,1)} %param.16) | copy-start | bytes 12582916
  53.6 1.3 %copy-start.1 = (f32[2048]{0:T(1024)S(1)}, f32[2048]{0:T(1024)}, u32[]{:S(2)}) copy-start(f32[2048]{0:T(1024)} %param.17) | copy-start | bytes 24580
